TPU v7x, 512 devices: a whole 4x4x16 slice. The times are simulated.
512 devices in a mesh: dom: 128 (over x, y_hi, z), rel: 4 (over y_lo, core).
Axes of the slice: x: 4, y: 4 (y_hi: 2, y_lo: 2; y = y_hi * 2 + y_lo), z: 16, core: 2. Of those that a mesh axis runs over, the one named last changes fastest.
Arguments:
- emb: float32 [32768, 400], P('dom'), may hold values from -1.2 to 1.2
- emb_state: float32 [32768], P('dom'), may hold values from 0.02 to 2
- rel_weight: float32 [32, 400], P('rel'), may hold values from 0.5 to 1.5
- rel_state: float32 [32], P('rel'), may hold values from 1 to 1000
- swap_mask: int32 [1], replicated, may hold values from 1 to 127
- src_rows: int32 [4, 65536], P('rel', 'dom'), may hold values from 0 to 255
- dst_rows: int32 [4, 65536], P('rel', 'dom'), may hold values from 0 to 255
- tile_rel: int32 [4, 512], P('rel', 'dom'), may hold values from 0 to 7
- live_tiles: int32 [4, 128], P('rel', 'dom'), may hold values from 1 to 4, as said below
- neg_tiles: int32 [4, 1024], P('rel', 'dom'), may hold values from 0 to 1
- bound_rows: int32 [32768], P('dom'), may hold values from 0 to 255
- band_src: int32 [4, 32768], P('rel', 'dom'), may hold values from 0 to 255
- band_dst: int32 [4, 32768], P('rel', 'dom'), may hold values from 0 to 255
- band_rel: int32 [4, 256], P('rel', 'dom'), may hold values from 0 to 7
Outputs:
- emb_new: float32 [32768, 400], P('dom')
- state_new: float32 [32768], P('dom')
- rel_new: float32 [32, 400], P('rel')
Inputs may be any that keep to these rules, and one draw needn't show every extreme that they name: `live_tiles`: each entry counts the leading edge tiles of one bucket that hold edges; some relation group and partition has all 4 tiles live in every draw. `swap_mask`: the same plan entry holds for every partition, so pairs are mutual.
All inputs are finite; a program needn't handle non-finite values.
Results may differ from a plain program's by a relative error of at most 0.0029.
Values may be sent and summed in bfloat16 or wider, within the bound.
No kernel may reach another device: no remote copies, remote signals or barrier semaphores. Data moves between devices by JAX's collectives and lax.ppermute only.
A program may use at most 64 MiB of HBM per device.

v0:
```python
import jax
import jax.numpy as jnp
from jax import lax
from jax.experimental import pallas as pl
from jax.experimental.pallas import tpu as pltpu
from jax.sharding import Mesh
from jax.sharding import PartitionSpec as P

step_rate = 0.25

D = 400
TILE = 128
ROWS = 256
BND = 128
E_ROWS = 512
B_ROWS = 256
A_ROWS = E_ROWS + B_ROWS
E_TILES = E_ROWS // TILE
B_TILES = B_ROWS // TILE
A_TILES = E_TILES + B_TILES
N_REL = 4
INFO = 8
SENT = ROWS + INFO
RELS = 8
NEG_TILES = 8
NEG = NEG_TILES * TILE
RIM = BND + B_ROWS + INFO

BF = jnp.bfloat16
F32 = jnp.float32
DOM = ("x", "yh", "z")
Z = 16
XY = 8


def vmem():
    return pl.BlockSpec(memory_space=pltpu.VMEM)


def smem():
    return pl.BlockSpec(memory_space=pltpu.SMEM)


def call(kernel, ins, outs, *args):
    return pl.pallas_call(
        kernel,
        in_specs=[smem() if kind == "s" else vmem() for kind in ins],
        out_specs=[vmem() for _ in outs],
        out_shape=[jax.ShapeDtypeStruct(shape, dtype) for shape, dtype in outs],
    )(*args)


def mm(a, b, dims):
    return lax.dot_general(a, b, (dims, ((), ())), preferred_element_type=F32)


NN = ((1,), (0,))
NT = ((1,), (1,))
TN = ((0,), (0,))


def two(values):
    high = values.astype(BF)
    return high, (values - high.astype(F32)).astype(BF)


def mm_two(a, b, dims):
    high, low = two(a)
    return mm(high, b, dims) + mm(low, b, dims)


def hits(rows, ids):
    return lax.broadcasted_iota(jnp.int32, (rows, ids.shape[1]), 0) == ids


def picks(rows, ids):
    return hits(rows, ids).astype(F32).astype(BF)


def row_of(lists):
    row = lax.broadcasted_iota(jnp.int32, (INFO, D), 0)
    block = jnp.zeros((INFO, D), F32)
    for k, values in enumerate(lists):
        if values.shape[1] < D:
            values = jnp.concatenate([values, jnp.zeros((1, D - values.shape[1]), F32)], axis=1)
        block = jnp.where(row == k, values, block)
    return block.astype(BF)


def start_kernel(
    tile_ref, band_ref, live_ref, neg_ref, embt_ref, relw_ref, src_ref, dst_ref, bsrc_ref,
    bdst_ref, bound_ref,
    emb_ref, part_ref, up_ref, down_ref, brows_ref,
):
    emb = embt_ref[...].T
    emb_ref[...] = emb
    emb_high, emb_low = two(emb)
    part_ref[:ROWS, :] = emb_high
    lane = lax.broadcasted_iota(jnp.int32, (1, D), 1)
    second = neg_ref[0, 0]
    for t in range(1, NEG_TILES):
        second = second + neg_ref[0, t]
    numbers = [tile_ref[0, t] for t in range(E_TILES)] + [band_ref[0, t] for t in range(B_TILES)]
    numbers += [live_ref[0, 0], second]
    scalars = jnp.zeros((1, D), F32)
    for k, number in enumerate(numbers):
        scalars = jnp.where(lane == k, number.astype(F32), scalars)
    part_ref[ROWS:, :] = row_of(
        [
            src_ref[:, :256].astype(F32),
            src_ref[:, 256:].astype(F32),
            dst_ref[:, :256].astype(F32),
            dst_ref[:, 256:].astype(F32),
            bsrc_ref[...].astype(F32),
            scalars,
        ]
    )
    rim = mm(picks(ROWS, bound_ref[...]), emb_high, TN).astype(BF)
    up_ref[:BND, :] = rim[BND:]
    down_ref[:BND, :] = rim[:BND]
    pick = picks(ROWS, bsrc_ref[...])
    rows = mm(pick, emb_high, TN) + mm(pick, emb_low, TN)
    brows_ref[...] = rows
    for t in range(B_TILES):
        q = (rows[t * TILE : (t + 1) * TILE] * relw_ref[pl.ds(band_ref[0, t], 1), :]).astype(BF)
        up_ref[BND + t * TILE : BND + (t + 1) * TILE, :] = q
        down_ref[BND + t * TILE : BND + (t + 1) * TILE, :] = q
    info = row_of([bdst_ref[...].astype(F32)])
    up_ref[BND + B_ROWS :, :] = info
    down_ref[BND + B_ROWS :, :] = info


def source_kernel(
    tile_ref, emb_ref, relw_ref, src_ref, bdst_ref, bound_ref, own_up_ref, own_down_ref,
    low_ref, high_ref,
    q_ref, rows_ref, dqb_ref, back_ref,
):
    emb_high, emb_low = two(emb_ref[...])
    pick = picks(ROWS, src_ref[...])
    rows = mm(pick, emb_high, TN) + mm(pick, emb_low, TN)
    rows_ref[...] = rows
    for t in range(E_TILES):
        at = slice(t * TILE, (t + 1) * TILE)
        q_ref[at, :] = (rows[at] * relw_ref[pl.ds(tile_ref[0, t], 1), :]).astype(BF)
    qb = own_up_ref[BND : BND + B_ROWS, :]
    q_ref[E_ROWS:, :] = qb
    near = jnp.concatenate([low_ref[:BND, :], high_ref[:BND, :]], axis=0)
    hit = hits(2 * BND, bdst_ref[...])
    pos = jnp.sum(jnp.where(hit, mm(near, qb, NT), 0.0), axis=0, keepdims=True)
    dqb_ref[...] = mm_two(jnp.where(hit, -jax.nn.sigmoid(-pos), 0.0), near, TN)
    grads = []
    for got_ref, mine_ref, shift in ((low_ref, own_down_ref, BND), (high_ref, own_up_ref, 0)):
        qn = got_ref[BND : BND + B_ROWS, :]
        ids = got_ref[BND + B_ROWS :, :].astype(F32)[:1, :B_ROWS].astype(jnp.int32) - shift
        hit = hits(BND, ids)
        pos = jnp.sum(jnp.where(hit, mm(mine_ref[:BND, :], qn, NT), 0.0), axis=0, keepdims=True)
        grads.append(mm_two(jnp.where(hit, -jax.nn.sigmoid(-pos), 0.0), qn, NN))
    high, low = two(jnp.concatenate(grads, axis=0))
    pick = picks(ROWS, bound_ref[...])
    back_ref[...] = mm(pick, high, NN) + mm(pick, low, NN)


def coefficients(scores, dst, live, second):
    edge = lax.broadcasted_iota(jnp.int32, (1, A_ROWS), 1)
    valid = jnp.where((edge < live * TILE) | (edge >= E_ROWS), 1.0, 0.0)
    hit = hits(ROWS, dst)
    pos = jnp.sum(jnp.where(hit, scores[:, :E_ROWS], 0.0), axis=0, keepdims=True)
    dpos = -jax.nn.sigmoid(-pos) * valid[:, :E_ROWS]
    counts = jnp.where(
        lax.broadcasted_iota(jnp.int32, (ROWS, 1), 0) < TILE, NEG_TILES - second, second
    )
    dneg = (jax.nn.sigmoid(scores) * (valid / NEG)).astype(BF).astype(F32) * counts
    return jnp.concatenate(
        [dneg[:, :E_ROWS] + jnp.where(hit, dpos, 0.0), dneg[:, E_ROWS:]], axis=1
    )


def relation_kernel(
    tile_ref, band_ref, live_ref, neg_ref, got_ref, q_ref, rows_ref, brows_ref, dqb_ref, relw_ref,
    dst_ref,
    gw_ref, step_ref,
):
    far = got_ref[:ROWS, :]
    second = neg_ref[0, 0]
    for t in range(1, NEG_TILES):
        second = second + neg_ref[0, t]
    scores = mm(far, q_ref[...], NT)
    coef = coefficients(scores, dst_ref[...], live_ref[0, 0], second.astype(F32))
    dq = mm_two(coef, far, TN)
    gw = jnp.zeros((RELS, D), F32)
    row8 = lax.broadcasted_iota(jnp.int32, (RELS, 1), 0)
    for t in range(A_TILES):
        piece = dq[t * TILE : (t + 1) * TILE]
        if t < E_TILES:
            ident = tile_ref[0, t]
            rows = rows_ref[t * TILE : (t + 1) * TILE, :]
        else:
            at = slice((t - E_TILES) * TILE, (t - E_TILES + 1) * TILE)
            ident = band_ref[0, t - E_TILES]
            rows = brows_ref[at, :]
            piece = piece + dqb_ref[at, :]
        gw = gw + jnp.where(row8 == ident, jnp.sum(piece * rows, axis=0, keepdims=True), 0.0)
        step_ref[t * TILE : (t + 1) * TILE, :] = piece * relw_ref[pl.ds(ident, 1), :]
    for k in range(Z):
        gw_ref[k, :, :] = gw.astype(BF)


def partner_kernel(
    got_ref, part_ref, relw_ref, step_ref, src_ref, bsrc_ref, back_ref,
    total_ref,
):
    far = got_ref[:ROWS, :]
    info = got_ref[ROWS:, :].astype(F32)
    src = jnp.concatenate([info[0:1, :256], info[1:2, :256], info[4:5, :256]], axis=1)
    dst = jnp.concatenate([info[2:3, :256], info[3:4, :256]], axis=1).astype(jnp.int32)
    rows = mm(picks(ROWS, src.astype(jnp.int32)), far, TN)
    row8 = lax.broadcasted_iota(jnp.int32, (RELS, 1), 0)
    parts = []
    for t in range(A_TILES):
        chosen = row8 == info[5:6, t : t + 1].astype(jnp.int32)
        w = jnp.sum(jnp.where(chosen, relw_ref[...], 0.0), axis=0, keepdims=True)
        parts.append((rows[t * TILE : (t + 1) * TILE] * w).astype(BF))
    q = jnp.concatenate(parts, axis=0)
    scores = mm(part_ref[:ROWS, :], q, NT)
    coef = coefficients(
        scores, dst, info[5:6, A_TILES : A_TILES + 1].astype(jnp.int32), info[5:6, A_TILES + 1 : A_TILES + 2]
    )
    high, low = two(step_ref[...])
    pick = jnp.concatenate([picks(ROWS, src_ref[...]), picks(ROWS, bsrc_ref[...])], axis=1)
    total_ref[...] = (
        back_ref[...] + mm(pick, high, NN) + mm(pick, low, NN) + mm_two(coef, q, NN)
    )


def final_kernel(mine_ref, other_ref, embt_ref, state_ref, new_ref, fresh_ref):
    grad = (mine_ref[...].astype(F32) + other_ref[...].astype(F32)).T
    fresh = state_ref[...] + jnp.sum(grad * grad, axis=0, keepdims=True) / D
    fresh_ref[...] = fresh
    new_ref[...] = embt_ref[...] - step_rate * grad / jnp.sqrt(fresh)


def swap(axes, size, number, block, work):
    def branch(k):
        def run(moved, *args):
            if k:
                moved = lax.ppermute(moved, axes, [(i, i ^ k) for i in range(size)])
            return (moved, *work(*args))

        return run

    return lambda *args: lax.switch(number, [branch(k) for k in range(size)], block, *args)


def trade(values, bit):
    return lax.ppermute(values, "rel", [(i, i ^ bit) for i in range(N_REL)])


def body(
    emb, emb_state, rel_weight, rel_state, swap_mask, src_rows, dst_rows, tile_rel, live_tiles,
    neg_tiles, bound_rows, band_src, band_dst, band_rel,
):
    mask = swap_mask[0]
    bound = bound_rows.reshape(1, 2 * BND)
    count = lax.axis_size(DOM)
    part_shape, rim_shape = (SENT, D), (RIM, D)
    emb_rows, part, to_up, to_down, band_rows = call(
        start_kernel,
        "ssssvvvvvvv",
        [((ROWS, D), F32), (part_shape, BF), (rim_shape, BF), (rim_shape, BF), ((B_ROWS, D), F32)],
        tile_rel, band_rel, live_tiles, neg_tiles, emb.T, rel_weight, src_rows, dst_rows, band_src,
        band_dst, bound,
    )
    from_low = lax.ppermute(to_up, DOM, [(i, i + 1) for i in range(count - 1)])
    from_high = lax.ppermute(to_down, DOM, [(i + 1, i) for i in range(count - 1)])
    (got,) = swap(("x", "yh"), XY, lax.shift_right_logical(mask, 4), part, lambda: ())()

    def sources(*args):
        return call(
            source_kernel,
            "svvvvvvvvv",
            [((A_ROWS, D), BF), ((E_ROWS, D), F32), ((B_ROWS, D), F32), ((ROWS, D), F32)],
            *args,
        )

    got, q, rows, dq_band, back = swap("z", Z, lax.bitwise_and(mask, 15), got, sources)(
        tile_rel, emb_rows, rel_weight, src_rows, band_dst, bound, to_up, to_down, from_low, from_high
    )
    gw, step = call(
        relation_kernel,
        "ssssvvvvvvv",
        [((Z, RELS, D), BF), ((A_ROWS, D), F32)],
        tile_rel, band_rel, live_tiles, neg_tiles, got, q, rows, band_rows, dq_band, rel_weight,
        dst_rows,
    )
    gw = lax.all_to_all(gw, "z", split_axis=0, concat_axis=0, tiled=True)
    (total,) = call(
        partner_kernel,
        "vvvvvvv",
        [((ROWS, D), F32)],
        got, part, rel_weight, step, src_rows, band_src, back,
    )
    pair = (total + trade(total, 1)).astype(BF)
    other = trade(pair, 2)
    new_t, fresh = call(
        final_kernel,
        "vvvv",
        [((D, ROWS), F32), ((1, ROWS), F32)],
        pair, other, emb.T, emb_state.reshape(1, ROWS),
    )
    gw = jnp.sum(gw.astype(F32), axis=0).astype(BF)
    gw = jnp.broadcast_to(gw[None], (XY, RELS, D))
    gw = lax.all_to_all(gw, ("x", "yh"), split_axis=0, concat_axis=0, tiled=True)
    gw = jnp.sum(gw.astype(F32), axis=0)
    rel_new = rel_weight - step_rate * gw / jnp.sqrt(rel_state + jnp.mean(gw * gw, axis=1))[:, None]
    return (new_t.T, fresh.reshape(ROWS), rel_new)


def solution(mesh):
    fine = Mesh(mesh.devices.reshape(4, 2, Z, N_REL), ("x", "yh", "z", "rel"))
    in_specs = (
        P(DOM, None),
        P(DOM),
        P("rel", None),
        P("rel"),
        P(),
        P("rel", DOM),
        P("rel", DOM),
        P("rel", DOM),
        P("rel", DOM),
        P("rel", DOM),
        P(DOM),
        P("rel", DOM),
        P("rel", DOM),
        P("rel", DOM),
    )
    out_specs = (P(DOM, None), P(DOM), P("rel", None))
    return jax.shard_map(
        body, mesh=fine, in_specs=in_specs, out_specs=out_specs, check_vma=False
    )
```

profile of v0, /device:TPU:34, one launch (start us, length us, event | category | flops | bytes accessed | tf_op | source)
XLA Modules:
  0.0 95.9 jit_solution(8543162349811462408)
XLA Ops:
  1.3 2.4 %shard_map.157 = (f32[256,400]{1,0:T(8,128)S(1)}, bf16[264,400]{1,0:T(8,128)(2,1)S(1)}, bf16[392,400]{1,0:T(8,128)(2,1)S(1)}, bf16[392,400]{1,0:T(8,128)(2,1)S(1)}, f32[256,400]{1,0:T(8,128)}) custom-call(s32[1,4]{1,0:T(1,128)} %tile_ref.3, s32[1,2]{1,0:T(1,128)} %band_ref.3, s32[1,1]{1,0:T(1,128)S(6)} %copy.106.live_ref, s32[1,8]{1,0:T(1,128)} %neg_ref.3, ...), custom_call_target="tpu_custom_call" | custom-call | tf_op jit(solution)/shard_map/pallas_call | solution.py:45
  3.7 3.8 %collective-permute-start.22 = (bf16[392,400]{1,0:T(8,128)(2,1)S(1)}, bf16[392,400]{1,0:T(8,128)(2,1)S(1)}, u32[]{:S(2)}, u32[]{:S(2)}) collective-permute-start(bf16[392,400]{1,0:T(8,128)(2,1)S(1)} %get-tuple-element.627), channel_id=1, source_target_pairs={{0,4},{4,8},{8,12},{12,16},{16,20},{20,24},{24,28},{28,32},{32,36}... | collective-permute-start | bytes 940808 | tf_op jit(solution)/shard_map/ppermute | solution.py:273
  7.5 2.0 %collective-permute-start.23 = (bf16[392,400]{1,0:T(8,128)(2,1)S(1)}, bf16[392,400]{1,0:T(8,128)(2,1)S(1)}, u32[]{:S(2)}, u32[]{:S(2)}) collective-permute-start(bf16[392,400]{1,0:T(8,128)(2,1)S(1)} %get-tuple-element.628), channel_id=1, source_target_pairs={{4,0},{8,4},{12,8},{16,12},{20,16},{24,20},{28,24},{32,28},{36,32}... | collective-permute-start | bytes 940808 | tf_op jit(solution)/shard_map/ppermute | solution.py:274
  10.2 0.7 conditional.2
  10.2 0.7 copy.17
  11.0 5.7 %collective-permute-done.22 = bf16[392,400]{1,0:T(8,128)(2,1)S(1)} collective-permute-done((bf16[392,400]{1,0:T(8,128)(2,1)S(1)}, bf16[392,400]{1,0:T(8,128)(2,1)S(1)}, u32[]{:S(2)}, u32[]{:S(2)}) %collective-permute-start.22) | collective-permute-done | bytes 313632 | tf_op jit(solution)/shard_map/ppermute | solution.py:273
  16.6 3.7 %collective-permute-done.23 = bf16[392,400]{1,0:T(8,128)(2,1)S(1)} collective-permute-done((bf16[392,400]{1,0:T(8,128)(2,1)S(1)}, bf16[392,400]{1,0:T(8,128)(2,1)S(1)}, u32[]{:S(2)}, u32[]{:S(2)}) %collective-permute-start.23) | collective-permute-done | bytes 313632 | tf_op jit(solution)/shard_map/ppermute | solution.py:274
  20.4 17.7 %conditional.3 = (bf16[264,400]{1,0:T(8,128)(2,1)}, bf16[768,400]{1,0:T(8,128)(2,1)}, f32[512,400]{1,0:T(8,128)S(1)}, f32[256,400]{1,0:T(8,128)}, f32[256,400]{1,0:T(8,128)}) conditional(s32[]{:T(128)} %bitcast, (s32[1,4]{1,0:T(1,128)}, f32[256,400]{1,0:T(8,128)S(1)}, f32[8,400]{1,0:T(8,128)}, s32[1,512]{1,0:T(1,128)}, ...), branch_computations={%region_8.0_spmd, %region_9.0_spmd, %region_10.0_spmd, %region_11.... | conditional | bytes 1267280 | solution.py:251
  20.4 5.0 %collective-permute-start.9 = (bf16[264,400]{1,0:T(8,128)(2,1)}, bf16[264,400]{1,0:T(8,128)(2,1)}, u32[]{:S(2)}, u32[]{:S(2)}) collective-permute-start(bf16[264,400]{1,0:T(8,128)(2,1)} %get-tuple-element.414), channel_id=1, source_target_pairs={{0,12},{4,8},{8,4},{12,0},{16,28},{20,24},{24,20},{28,16},{32,44},... | collective-permute-start | bytes 633608 | tf_op jit(solution)/shard_map/cond/branch_3_fun/ppermute | solution.py:246
  25.4 3.3 %branch_3_fun.1 = (bf16[768,400]{1,0:T(8,128)(2,1)}, f32[512,400]{1,0:T(8,128)S(1)}, f32[256,400]{1,0:T(8,128)}, f32[256,400]{1,0:T(8,128)}) custom-call(s32[1,4]{1,0:T(1,128)} %get-tuple-element.415.tile_ref, f32[256,400]{1,0:T(8,128)S(1)} %get-tuple-element.416.emb_ref, f32[8,400]{1,0:T(8,128)} %get-tuple-element.417.relw_ref, ...), custom_call_target="tpu_custom_call" | custom-call | tf_op jit(solution)/shard_map/cond/branch_3_fun/pallas_call | solution.py:45
  28.7 7.6 %collective-permute-done.9 = bf16[264,400]{1,0:T(8,128)(2,1)} collective-permute-done((bf16[264,400]{1,0:T(8,128)(2,1)}, bf16[264,400]{1,0:T(8,128)(2,1)}, u32[]{:S(2)}, u32[]{:S(2)}) %collective-permute-start.9) | collective-permute-done | bytes 211232 | tf_op jit(solution)/shard_map/cond/branch_3_fun/ppermute | solution.py:246
  36.4 1.7 %copy.40 = bf16[264,400]{1,0:T(8,128)(2,1)} copy(bf16[264,400]{1,0:T(8,128)(2,1)} %collective-permute-done.9) | data formatting | bytes 422400 | tf_op jit(solution)/shard_map/cond
  38.1 3.9 %shard_map.158 = (bf16[16,8,400]{2,1,0:T(8,128)(2,1)}, f32[768,400]{1,0:T(8,128)}) custom-call(s32[1,4]{1,0:T(1,128)} %tile_ref.3, s32[1,2]{1,0:T(1,128)} %band_ref.3, s32[1,1]{1,0:T(1,128)S(6)} %copy.106.live_ref, s32[1,8]{1,0:T(1,128)} %neg_ref.3, bf16[264,400]{1,0:T(8,128)(2,1)} %get-tuple-element.630.got_ref, bf16[768,400]{1,0:T(8,128)(2,1)} %get-tuple-element.631.q_ref, ...), custom_call_target="tpu_custom_call" | custom-call | tf_op jit(solution)/shard_map/pallas_call | solution.py:45
  42.0 0.0 copy-done
  42.0 0.0 copy-done.2
  42.0 0.0 copy-done.3
  42.0 0.0 copy-start.5
  42.0 4.0 %shard_map.159 = f32[256,400]{1,0:T(8,128)} custom-call(bf16[264,400]{1,0:T(8,128)(2,1)} %get-tuple-element.630.got_ref, bf16[264,400]{1,0:T(8,128)(2,1)S(1)} %get-tuple-element.629.part_ref, f32[8,400]{1,0:T(8,128)S(1)} %copy-done, f32[768,400]{1,0:T(8,128)} %get-tuple-element.635.step_ref, s32[1,512]{1,0:T(1,128)S(1)} %copy-done.2, s32[1,256]{1,0:T(1,128)} %bsrc_ref.3, ...), custom_call_target="tpu_custom_call" | custom-call | tf_op jit(solution)/shard_map/pallas_call | solution.py:45
  46.0 2.0 %collective-permute-start.24 = (f32[256,400]{1,0:T(8,128)}, f32[256,400]{1,0:T(8,128)S(1)}, u32[]{:S(2)}, u32[]{:S(2)}) collective-permute-start(f32[256,400]{1,0:T(8,128)} %shard_map.159), channel_id=1, source_target_pairs={{0,1},{1,0},{2,3},{3,2},{4,5},{5,4},{6,7},{7,6},{8,9},{9,8},{10,11... | collective-permute-start | bytes 1228808 | tf_op jit(solution)/shard_map/ppermute | solution.py:255
  48.1 27.0 %all_to_all.10 = bf16[16,8,400]{2,1,0:T(8,128)(2,1)S(1)} all-to-all(bf16[16,8,400]{2,1,0:T(8,128)(2,1)S(1)} %copy-done.5), channel_id=1, replica_groups=mesh['x'=4,'yh'=2,'z'=16,'rel'=4] {'z'}, dimensions={0} | all-to-all | bytes 204800 | tf_op jit(solution)/shard_map/all_to_all | solution.py:295
  75.1 0.6 broadcast_in_dim.2
  75.8 7.5 %all-to-all-start.1 = ((bf16[8,8,400]{2,1,0:T(8,128)(2,1)}), bf16[8,8,400]{2,1,0:T(8,128)(2,1)S(1)}, u32[]{:S(2)}, u32[]{:S(2)}) async-start(bf16[8,8,400]{2,1,0:T(8,128)(2,1)} %broadcast_in_dim.2), calls=%async_computation.1 | async-start | bytes 131072 | tf_op jit(solution)/shard_map/all_to_all | solution.py:312
  83.2 0.0 collective-permute-done.24
  83.2 1.1 %add_convert_fusion.mine_ref = bf16[256,400]{1,0:T(8,128)(2,1)S(1)} fusion(f32[256,400]{1,0:T(8,128)} %shard_map.159, f32[256,400]{1,0:T(8,128)S(1)} %collective-permute-done.24), kind=kLoop, calls=%fused_computation | loop fusion | flops 204800 | bytes 1024000 | tf_op jit(solution)/shard_map/convert_element_type | solution.py:302
  84.4 2.6 %collective-permute-start.25 = (bf16[256,400]{1,0:T(8,128)(2,1)S(1)}, bf16[256,400]{1,0:T(8,128)(2,1)S(1)}, u32[]{:S(2)}, u32[]{:S(2)}) collective-permute-start(bf16[256,400]{1,0:T(8,128)(2,1)S(1)} %add_convert_fusion.mine_ref), channel_id=1, source_target_pairs={{0,2},{1,3},{2,0},{3,1},{4,6},{5,7},{6,4},{7,5},{8,10},{9,11},{10,... | collective-permute-start | bytes 614408 | tf_op jit(solution)/shard_map/ppermute | solution.py:255
  87.0 2.6 %all-to-all-done.1 = bf16[8,8,400]{2,1,0:T(8,128)(2,1)S(1)} async-done(((bf16[8,8,400]{2,1,0:T(8,128)(2,1)}), bf16[8,8,400]{2,1,0:T(8,128)(2,1)S(1)}, u32[]{:S(2)}, u32[]{:S(2)}) %all-to-all-start.1) | async-done | bytes 51232 | tf_op jit(solution)/shard_map/all_to_all | solution.py:312
  89.5 0.1 multiply_reduce_fusion
  89.7 0.0 copy-done.6
  89.7 0.7 divide_subtract_fusion
  90.4 2.6 %collective-permute-done.25.other_ref = bf16[256,400]{1,0:T(8,128)(2,1)S(1)} collective-permute-done((bf16[256,400]{1,0:T(8,128)(2,1)S(1)}, bf16[256,400]{1,0:T(8,128)(2,1)S(1)}, u32[]{:S(2)}, u32[]{:S(2)}) %collective-permute-start.25) | collective-permute-done | bytes 204832 | tf_op jit(solution)/shard_map/ppermute | solution.py:255
  93.0 0.7 copy-done.4
  93.7 2.2 %shard_map.160 = (f32[400,256]{1,0:T(8,128)}, f32[1,256]{1,0:T(1,128)}) custom-call(bf16[256,400]{1,0:T(8,128)(2,1)} %copy-done.1, bf16[256,400]{1,0:T(8,128)(2,1)} %copy-done.4, f32[400,256]{1,0:T(8,128)} %bitcast.8, f32[1,256]{1,0:T(1,128)} %bitcast.26), custom_call_target="tpu_custom_call" | custom-call | tf_op jit(solution)/shard_map/pallas_call | solution.py:45
  (11 shorter events, 0.1 us)
Async XLA Ops:
  3.7 12.9 %collective-permute-start.22 = (bf16[392,400]{1,0:T(8,128)(2,1)S(1)}, bf16[392,400]{1,0:T(8,128)(2,1)S(1)}, u32[]{:S(2)}, u32[]{:S(2)}) collective-permute-start(bf16[392,400]{1,0:T(8,128)(2,1)S(1)} %get-tuple-element.627), channel_id=1, source_target_pairs={{0,4},{4,8},{8,12},{12,16},{16,20},{20,24},{24,28},{28,32},{32,36}... | collective-permute-start | bytes 940808 | tf_op jit(solution)/shard_map/ppermute | solution.py:273
  7.5 12.8 %collective-permute-start.23 = (bf16[392,400]{1,0:T(8,128)(2,1)S(1)}, bf16[392,400]{1,0:T(8,128)(2,1)S(1)}, u32[]{:S(2)}, u32[]{:S(2)}) collective-permute-start(bf16[392,400]{1,0:T(8,128)(2,1)S(1)} %get-tuple-element.628), channel_id=1, source_target_pairs={{4,0},{8,4},{12,8},{16,12},{20,16},{24,20},{28,24},{32,28},{36,32}... | collective-permute-start | bytes 940808 | tf_op jit(solution)/shard_map/ppermute | solution.py:274
  20.4 16.0 %collective-permute-start.9 = (bf16[264,400]{1,0:T(8,128)(2,1)}, bf16[264,400]{1,0:T(8,128)(2,1)}, u32[]{:S(2)}, u32[]{:S(2)}) collective-permute-start(bf16[264,400]{1,0:T(8,128)(2,1)} %get-tuple-element.414), channel_id=1, source_target_pairs={{0,12},{4,8},{8,4},{12,0},{16,28},{20,24},{24,20},{28,16},{32,44},... | collective-permute-start | bytes 633608 | tf_op jit(solution)/shard_map/cond/branch_3_fun/ppermute | solution.py:246
  38.1 3.9 %copy-start = (f32[8,400]{1,0:T(8,128)S(1)}, f32[8,400]{1,0:T(8,128)}, u32[]{:S(2)}) copy-start(f32[8,400]{1,0:T(8,128)} %relw_ref.5) | copy-start | bytes 38404
  38.1 3.9 %copy-start.2 = (s32[1,512]{1,0:T(1,128)S(1)}, s32[1,512]{1,0:T(1,128)}, u32[]{:S(2)}) copy-start(s32[1,512]{1,0:T(1,128)} %src_ref.3) | copy-start | bytes 6148
  38.1 3.9 %copy-start.3 = (f32[256,400]{1,0:T(8,128)S(1)}, f32[256,400]{1,0:T(8,128)}, u32[]{:S(2)}) copy-start(f32[256,400]{1,0:T(8,128)} %get-tuple-element.636.back_ref) | copy-start | bytes 1228804
  42.0 6.1 %copy-start.5 = (bf16[16,8,400]{2,1,0:T(8,128)(2,1)S(1)}, bf16[16,8,400]{2,1,0:T(8,128)(2,1)}, u32[]{:S(2)}) copy-start(bf16[16,8,400]{2,1,0:T(8,128)(2,1)} %get-tuple-element.639) | copy-start | bytes 307204
  46.0 43.7 %copy-start.6 = (f32[8]{0:T(128)S(1)}, f32[8]{0:T(128)}, u32[]{:S(2)}) copy-start(f32[8]{0:T(128)} %param.41) | copy-start | bytes 100
  46.0 37.2 %collective-permute-start.24 = (f32[256,400]{1,0:T(8,128)}, f32[256,400]{1,0:T(8,128)S(1)}, u32[]{:S(2)}, u32[]{:S(2)}) collective-permute-start(f32[256,400]{1,0:T(8,128)} %shard_map.159), channel_id=1, source_target_pairs={{0,1},{1,0},{2,3},{3,2},{4,5},{5,4},{6,7},{7,6},{8,9},{9,8},{10,11... | collective-permute-start | bytes 1228808 | tf_op jit(solution)/shard_map/ppermute | solution.py:255
  75.8 13.8 %all-to-all-start.1 = ((bf16[8,8,400]{2,1,0:T(8,128)(2,1)}), bf16[8,8,400]{2,1,0:T(8,128)(2,1)S(1)}, u32[]{:S(2)}, u32[]{:S(2)}) async-start(bf16[8,8,400]{2,1,0:T(8,128)(2,1)} %broadcast_in_dim.2), calls=%async_computation.1 | async-start | bytes 131072 | tf_op jit(solution)/shard_map/all_to_all | solution.py:312
  84.4 8.6 %copy-start.1 = (bf16[256,400]{1,0:T(8,128)(2,1)}, bf16[256,400]{1,0:T(8,128)(2,1)S(1)}, u32[]{:S(2)}) copy-start(bf16[256,400]{1,0:T(8,128)(2,1)S(1)} %add_convert_fusion.mine_ref) | copy-start | bytes 614404
  84.4 8.6 %collective-permute-start.25 = (bf16[256,400]{1,0:T(8,128)(2,1)S(1)}, bf16[256,400]{1,0:T(8,128)(2,1)S(1)}, u32[]{:S(2)}, u32[]{:S(2)}) collective-permute-start(bf16[256,400]{1,0:T(8,128)(2,1)S(1)} %add_convert_fusion.mine_ref), channel_id=1, source_target_pairs={{0,2},{1,3},{2,0},{3,1},{4,6},{5,7},{6,4},{7,5},{8,10},{9,11},{10,... | collective-permute-start | bytes 614408 | tf_op jit(solution)/shard_map/ppermute | solution.py:255
  93.0 0.7 copy-start.4
where the time goes:
time: 96.5 us; the launch traced here: 95.9 us
  blocking collectives  27 us (28%)
  starting transfers between devices  22.9 us (24%)
  waiting for transfers between devices  22.2 us (23%)
  Pallas kernels  15.8 us (16%)
  local copies, waits for them, and re-layouts  3.79 us (4%)
  between operations  2.02 us (2%)
  other arithmetic  2 us (2%)
    all_to_all x1, blocking collectives, body(): gw = lax.all_to_all(gw, 'z', split_axis=0, concat_axis=0, tiled=True)  27 us
    pallas_call x5, Pallas kernels, call(): pl.pallas_call(kernel, in_specs=[smem() if kind == 's' else vmem() for ki...  15.8 us
    ppermute x1, waiting for transfers between devices, run(): moved = lax.ppermute(moved, axes, [(i, i ^ k) for i in range(size)])  7.65 us
    all_to_all x1, starting transfers between devices, body(): lax.all_to_all(gw, ('x', 'yh'), split_axis=0, concat_axis=0, tiled=True)  7.46 us
    ppermute x1, waiting for transfers between devices, body(): from_low = lax.ppermute(to_up, DOM, [(i, i + 1) for i in range(count - 1)])  5.67 us
    ppermute x1, starting transfers between devices, run(): moved = lax.ppermute(moved, axes, [(i, i ^ k) for i in range(size)])  5.03 us
    ppermute x2, starting transfers between devices, trade(): return lax.ppermute(values, 'rel', [(i, i ^ bit) for i in range(N_REL)])  4.63 us
    ppermute x1, starting transfers between devices, body(): from_low = lax.ppermute(to_up, DOM, [(i, i + 1) for i in range(count - 1)])  3.81 us
  transfers between devices with their start and end apart: 6, of which 5 were waited for; matrix products, arithmetic and copies ran while one was open for 4% of the time, Pallas kernels for 3%

commit v1 on v0

v1 whole, which is shorter than its diff:
```python
import jax
import jax.numpy as jnp
from jax import lax
from jax.experimental import pallas as pl
from jax.experimental.pallas import tpu as pltpu
from jax.sharding import Mesh
from jax.sharding import PartitionSpec as P

step_rate = 0.25

D = 400
TILE = 128
ROWS = 256
HALF = ROWS // 2
BND = 128
E_ROWS = 512
B_ROWS = 256
A_ROWS = E_ROWS + B_ROWS
E_TILES = E_ROWS // TILE
B_TILES = B_ROWS // TILE
A_TILES = E_TILES + B_TILES
N_REL = 4
RELS = 8
NEG_TILES = 8
NEG = NEG_TILES * TILE
INFO = 16
SENT = D + INFO
RIM_INFO = 8
RIM = D + RIM_INFO
RIM_WIDTH = BND + B_ROWS

BF = jnp.bfloat16
F32 = jnp.float32
DOM = ("x", "yh", "z")
Z = 16
XY = 8


def vmem():
    return pl.BlockSpec(memory_space=pltpu.VMEM)


def smem():
    return pl.BlockSpec(memory_space=pltpu.SMEM)


def call(kernel, ins, outs, *args):
    return pl.pallas_call(
        kernel,
        in_specs=[smem() if kind == "s" else vmem() for kind in ins],
        out_specs=[vmem() for _ in outs],
        out_shape=[jax.ShapeDtypeStruct(shape, dtype) for shape, dtype in outs],
    )(*args)


def mm(a, b, dims):
    return lax.dot_general(a, b, (dims, ((), ())), preferred_element_type=F32)


NN = ((1,), (0,))
NT = ((1,), (1,))
TN = ((0,), (0,))


def two(values):
    high = values.astype(BF)
    return high, (values - high.astype(F32)).astype(BF)


def mm_two(a, b, dims):
    high, low = two(a)
    return mm(high, b, dims) + mm(low, b, dims)


def hits(count, ids):
    return lax.broadcasted_iota(jnp.int32, (count, ids.shape[1]), 0) == ids


def ones(mask):
    return mask.astype(F32).astype(BF)


def stacked(count, width, lists):
    row = lax.broadcasted_iota(jnp.int32, (count, width), 0)
    block = jnp.zeros((count, width), F32)
    for k, values in enumerate(lists):
        values = values.astype(F32)
        if values.shape[1] < width:
            values = jnp.concatenate(
                [values, jnp.zeros((1, width - values.shape[1]), F32)], axis=1
            )
        block = jnp.where(row == k, values, block)
    return block.astype(BF)


def relations(ids):
    spread = [jnp.broadcast_to(ident, (1, TILE)).astype(jnp.int32) for ident in ids]
    return ones(hits(RELS, jnp.concatenate(spread, axis=1)))


def weights(relw, chosen):
    high = relw.astype(BF)
    rest = relw - high.astype(F32)
    middle = rest.astype(BF)
    low = (rest - middle.astype(F32)).astype(BF)
    return (mm(high, chosen, TN) + mm(middle, chosen, TN)) + mm(low, chosen, TN)


def tile_ids(tile_ref, band_ref):
    return [tile_ref[0, t] for t in range(E_TILES)], [band_ref[0, t] for t in range(B_TILES)]


def second_count(neg_ref):
    second = neg_ref[0, 0]
    for t in range(1, NEG_TILES):
        second = second + neg_ref[0, t]
    return second


def start_kernel(
    core_ref, tile_ref, band_ref, live_ref, neg_ref, emb_ref, relw_ref, src_ref, dst_ref, bsrc_ref,
    bdst_ref, bound_ref,
    part_ref, up_ref, down_ref, brows_ref,
):
    high, low = two(emb_ref[...])
    part_ref[:D, :] = jnp.where(core_ref[0] == 0, high[:, :HALF], high[:, HALF:])
    edge_ids, band_ids = tile_ids(tile_ref, band_ref)
    lane = lax.broadcasted_iota(jnp.int32, (1, TILE), 1)
    scalars = jnp.zeros((1, TILE), F32)
    for k, number in enumerate([*edge_ids, *band_ids, live_ref[0, 0], second_count(neg_ref)]):
        scalars = jnp.where(lane == k, number.astype(F32), scalars)
    lists = []
    for ref in (src_ref, bsrc_ref, dst_ref):
        lists += [ref[:, k : k + TILE] for k in range(0, ref.shape[1], TILE)]
    part_ref[D:, :] = stacked(INFO, TILE, [*lists, scalars])
    rim = mm(high, ones(hits(ROWS, bound_ref[...])), NN).astype(BF)
    up_ref[:D, :BND] = rim[:, BND:]
    down_ref[:D, :BND] = rim[:, :BND]
    pick = ones(hits(ROWS, bsrc_ref[...]))
    rows = mm(high, pick, NN) + mm(low, pick, NN)
    brows_ref[...] = rows
    q = (rows * weights(relw_ref[...], relations(band_ids))).astype(BF)
    info = stacked(RIM_INFO, RIM_WIDTH, [bdst_ref[...]])
    for ref in (up_ref, down_ref):
        ref[:D, BND:] = q
        ref[D:, :] = info


def pull(scores, hit):
    pos = jnp.sum(jnp.where(hit, scores, 0.0), axis=0, keepdims=True)
    return jnp.where(hit, -jax.nn.sigmoid(-pos), 0.0)


def source_kernel(
    tile_ref, band_ref, emb_ref, relw_ref, src_ref, bdst_ref, bound_ref, own_up_ref, own_down_ref,
    low_ref, high_ref,
    q_ref, rows_ref, dqb_ref, back_ref,
):
    high, low = two(emb_ref[...])
    pick = ones(hits(ROWS, src_ref[...]))
    rows = mm(high, pick, NN) + mm(low, pick, NN)
    rows_ref[...] = rows
    edge_ids, _ = tile_ids(tile_ref, band_ref)
    q_ref[:, :E_ROWS] = (rows * weights(relw_ref[...], relations(edge_ids))).astype(BF)
    qb = own_up_ref[:D, BND:]
    q_ref[:, E_ROWS:] = qb
    near = jnp.concatenate([low_ref[:D, :BND], high_ref[:D, :BND]], axis=1)
    first, second = two(pull(mm(near, qb, TN), hits(2 * BND, bdst_ref[...])))
    dqb_ref[...] = mm(near, first, NN) + mm(near, second, NN)
    grads = []
    for got_ref, mine_ref, shift in ((low_ref, own_down_ref, BND), (high_ref, own_up_ref, 0)):
        qn = got_ref[:D, BND:]
        ids = got_ref[D:, :].astype(F32)[:1, :B_ROWS].astype(jnp.int32) - shift
        first, second = two(pull(mm(mine_ref[:D, :BND], qn, TN), hits(BND, ids)))
        grads.append(mm(qn, first, NT) + mm(qn, second, NT))
    back_ref[...] = mm_two(jnp.concatenate(grads, axis=1), ones(hits(ROWS, bound_ref[...])), NT)


def coefficients(scores, dst, live, second):
    edge = lax.broadcasted_iota(jnp.int32, (1, A_ROWS), 1)
    valid = jnp.where((edge < live * TILE) | (edge >= E_ROWS), 1.0, 0.0)
    counts = jnp.where(
        lax.broadcasted_iota(jnp.int32, (ROWS, 1), 0) < TILE, NEG_TILES - second, second
    )
    dneg = (jax.nn.sigmoid(scores) * (valid / NEG)).astype(BF).astype(F32) * counts
    positive = pull(scores[:, :E_ROWS], hits(ROWS, dst)) * valid[:, :E_ROWS]
    return two(jnp.concatenate([dneg[:, :E_ROWS] + positive, dneg[:, E_ROWS:]], axis=1))


def far_block(core_ref, got_ref, other_ref):
    got, other = got_ref[:D, :], other_ref[:D, :]
    first = core_ref[0] == 0
    return jnp.concatenate([jnp.where(first, got, other), jnp.where(first, other, got)], axis=1)


def relation_kernel(
    core_ref, tile_ref, band_ref, live_ref, neg_ref, got_ref, other_ref, q_ref, rows_ref, brows_ref,
    dqb_ref, relw_ref, dst_ref,
    gw_ref, step_ref,
):
    far = far_block(core_ref, got_ref, other_ref)
    scores = mm(far, q_ref[...], TN)
    high, low = coefficients(
        scores, dst_ref[...], live_ref[0, 0], second_count(neg_ref).astype(F32)
    )
    edge_ids, band_ids = tile_ids(tile_ref, band_ref)
    chosen = relations(edge_ids + band_ids)
    dq = mm(far, high, NN) + mm(far, low, NN)
    dq_band = dq[:, E_ROWS:] + dqb_ref[...]
    first, second = two(dq[:, :E_ROWS] * rows_ref[...])
    third, fourth = two(dq_band * brows_ref[...])
    gw = (mm(chosen[:, :E_ROWS], first, NT) + mm(chosen[:, :E_ROWS], second, NT)) + (
        mm(chosen[:, E_ROWS:], third, NT) + mm(chosen[:, E_ROWS:], fourth, NT)
    )
    gw = gw.astype(BF)
    for k in range(Z):
        gw_ref[k, :, :] = gw
    step_ref[:, :E_ROWS] = dq[:, :E_ROWS]
    step_ref[:, E_ROWS:] = dq_band


def partner_kernel(
    core_ref, tile_ref, band_ref, got_ref, other_ref, emb_ref, relw_ref, step_ref, src_ref, bsrc_ref,
    back_ref,
    total_ref,
):
    far = far_block(core_ref, got_ref, other_ref)
    info = got_ref[D:, :].astype(F32)
    ids = jnp.concatenate([info[k : k + 1, :] for k in range(10)], axis=1).astype(jnp.int32)
    scalars = info[10:11, :]
    relw = relw_ref[...]
    chosen = relations([scalars[:, t : t + 1] for t in range(A_TILES)])
    q = (mm(far, ones(hits(ROWS, ids[:, :A_ROWS])), NN) * weights(relw, chosen)).astype(BF)
    scores = mm(emb_ref[...].astype(BF), q, TN)
    high, low = coefficients(
        scores,
        ids[:, A_ROWS:],
        scalars[:, A_TILES : A_TILES + 1].astype(jnp.int32),
        scalars[:, A_TILES + 1 : A_TILES + 2],
    )
    edge_ids, band_ids = tile_ids(tile_ref, band_ref)
    steps = step_ref[...] * weights(relw, relations(edge_ids + band_ids))
    pick = jnp.concatenate([ones(hits(ROWS, src_ref[...])), ones(hits(ROWS, bsrc_ref[...]))], axis=1)
    total_ref[...] = (
        back_ref[...] + mm_two(steps, pick, NT) + mm(q, high, NT) + mm(q, low, NT)
    )


def final_kernel(mine_ref, other_ref, emb_ref, state_ref, new_ref, fresh_ref):
    grad = mine_ref[...].astype(F32) + other_ref[...].astype(F32)
    fresh = state_ref[...] + jnp.sum(grad * grad, axis=0, keepdims=True) / D
    fresh_ref[...] = fresh
    new_ref[...] = emb_ref[...] - step_rate * grad / jnp.sqrt(fresh)


def swap(axes, size, number, work):
    def branch(k):
        def run(moved, *args):
            if k:
                moved = lax.ppermute(moved, axes, [(i, i ^ k) for i in range(size)])
            return (moved, *work(*args))

        return run

    return lambda *args: lax.switch(number, [branch(k) for k in range(size)], *args)


def trade(values, bit):
    return lax.ppermute(values, "rel", [(i, i ^ bit) for i in range(N_REL)])


def body(
    emb, emb_state, rel_weight, rel_state, swap_mask, src_rows, dst_rows, tile_rel, live_tiles,
    neg_tiles, bound_rows, band_src, band_dst, band_rel,
):
    mask = swap_mask[0]
    bound = bound_rows.reshape(1, 2 * BND)
    core = lax.bitwise_and(lax.axis_index("rel").astype(jnp.int32), 1).reshape(1)
    count = lax.axis_size(DOM)
    emb_t = emb.T
    part, to_up, to_down, band_rows = call(
        start_kernel,
        "sssssvvvvvvv",
        [((SENT, HALF), BF), ((RIM, RIM_WIDTH), BF), ((RIM, RIM_WIDTH), BF), ((D, B_ROWS), F32)],
        core, tile_rel, band_rel, live_tiles, neg_tiles, emb_t, rel_weight, src_rows, dst_rows,
        band_src, band_dst, bound,
    )
    from_low = lax.ppermute(to_up, DOM, [(i, i + 1) for i in range(count - 1)])
    from_high = lax.ppermute(to_down, DOM, [(i + 1, i) for i in range(count - 1)])
    (got,) = swap(("x", "yh"), XY, lax.shift_right_logical(mask, 4), lambda: ())(part)

    def sources(*args):
        return call(
            source_kernel,
            "ssvvvvvvvvv",
            [((D, A_ROWS), BF), ((D, E_ROWS), F32), ((D, B_ROWS), F32), ((D, ROWS), F32)],
            *args,
        )

    got, q, rows, dq_band, back = swap("z", Z, lax.bitwise_and(mask, 15), sources)(
        got, tile_rel, band_rel, emb_t, rel_weight, src_rows, band_dst, bound, to_up, to_down,
        from_low, from_high,
    )
    other_half = trade(got, 1)
    gw, step = call(
        relation_kernel,
        "sssssvvvvvvvv",
        [((Z, RELS, D), BF), ((D, A_ROWS), F32)],
        core, tile_rel, band_rel, live_tiles, neg_tiles, got, other_half, q, rows, band_rows,
        dq_band, rel_weight, dst_rows,
    )
    gw = lax.all_to_all(gw, "z", split_axis=0, concat_axis=0, tiled=True)
    (total,) = call(
        partner_kernel,
        "sssvvvvvvvv",
        [((D, ROWS), F32)],
        core, tile_rel, band_rel, got, other_half, emb_t, rel_weight, step, src_rows,
        band_src, back,
    )
    pair = (total + trade(total, 1)).astype(BF)
    other = trade(pair, 2)
    new_t, fresh = call(
        final_kernel,
        "vvvv",
        [((D, ROWS), F32), ((1, ROWS), F32)],
        pair, other, emb_t, emb_state.reshape(1, ROWS),
    )
    gw = jnp.sum(gw.astype(F32), axis=0).astype(BF)
    gw = jnp.broadcast_to(gw[None], (XY, RELS, D))
    gw = lax.all_to_all(gw, ("x", "yh"), split_axis=0, concat_axis=0, tiled=True)
    gw = jnp.sum(gw.astype(F32), axis=0)
    rel_new = rel_weight - step_rate * gw / jnp.sqrt(rel_state + jnp.mean(gw * gw, axis=1))[:, None]
    return (new_t.T, fresh.reshape(ROWS), rel_new)


def solution(mesh):
    fine = Mesh(mesh.devices.reshape(4, 2, Z, N_REL), ("x", "yh", "z", "rel"))
    in_specs = (
        P(DOM, None),
        P(DOM),
        P("rel", None),
        P("rel"),
        P(),
        P("rel", DOM),
        P("rel", DOM),
        P("rel", DOM),
        P("rel", DOM),
        P("rel", DOM),
        P(DOM),
        P("rel", DOM),
        P("rel", DOM),
        P("rel", DOM),
    )
    out_specs = (P(DOM, None), P(DOM), P("rel", None))
    return jax.shard_map(
        body, mesh=fine, in_specs=in_specs, out_specs=out_specs, check_vma=False
    )
```

time: 96.5 us -> 91.4 us (0.947)
  waiting for transfers between devices: 22.2 us -> 13.7 us
  blocking collectives: 27 us -> 29.2 us
  starting transfers between devices: 22.9 us -> 25 us
  local copies, waits for them, and re-layouts: 3.79 us -> 2 us
    ppermute x1, waiting for transfers between devices: 7.65 us -> 0.01 us  [run(): moved = lax.ppermute(moved, axes, [(i, i ^ k) for i in range(size)])]
    cond x2 -> x1, local copies, waits for them, and re-layouts: 2.42 us -> 0.01 us
    all_to_all x1, blocking collectives: 27 us -> 29.2 us  [body(): gw = lax.all_to_all(gw, 'z', split_axis=0, concat_axis=0, tiled=True)]
    ppermute x2 -> x3, starting transfers between devices: 4.63 us -> 6.68 us  [trade(): return lax.ppermute(values, 'rel', [(i, i ^ bit) for i in range(N_REL)])]
    ppermute x1, waiting for transfers between devices: 5.67 us -> 4.49 us  [body(): from_low = lax.ppermute(to_up, DOM, [(i, i + 1) for i in range(count - 1)])]
    ppermute x2 -> x3, waiting for transfers between devices: 2.62 us -> 2.74 us  [trade(): return lax.ppermute(values, 'rel', [(i, i ^ bit) for i in range(N_REL)])]
  transfers between devices with their start and end apart: 6 -> 7, of which waited for: 5 -> 5; matrix products, arithmetic and copies ran while one was open for 4% -> 3% of each run, Pallas kernels for 3% -> 4%
where the time goes in v1:
time: 91.4 us; the launch traced here: 90.9 us
  blocking collectives  29.2 us (32%)
  starting transfers between devices  25 us (27%)
  Pallas kernels  16.4 us (18%)
  waiting for transfers between devices  13.7 us (15%)
  between operations  2.18 us (2%)
  local copies, waits for them, and re-layouts  2 us (2%)
  other arithmetic  1.9 us (2%)
    all_to_all x1, blocking collectives, body(): gw = lax.all_to_all(gw, 'z', split_axis=0, concat_axis=0, tiled=True)  29.2 us
    pallas_call x5, Pallas kernels, call(): pl.pallas_call(kernel, in_specs=[smem() if kind == 's' else vmem() for ki...  16.4 us
    all_to_all x1, starting transfers between devices, body(): lax.all_to_all(gw, ('x', 'yh'), split_axis=0, concat_axis=0, tiled=True)  7.46 us
    ppermute x3, starting transfers between devices, trade(): return lax.ppermute(values, 'rel', [(i, i ^ bit) for i in range(N_REL)])  6.68 us
    ppermute x1, starting transfers between devices, run(): moved = lax.ppermute(moved, axes, [(i, i ^ k) for i in range(size)])  5.04 us
    ppermute x1, waiting for transfers between devices, body(): from_low = lax.ppermute(to_up, DOM, [(i, i + 1) for i in range(count - 1)])  4.49 us
    ppermute x1, starting transfers between devices, body(): from_low = lax.ppermute(to_up, DOM, [(i, i + 1) for i in range(count - 1)])  3.81 us
    ppermute x1, waiting for transfers between devices, body(): lax.ppermute(to_down, DOM, [(i + 1, i) for i in range(count - 1)])  3.74 us
  transfers between devices with their start and end apart: 7, of which 5 were waited for; matrix products, arithmetic and copies ran while one was open for 3% of the time, Pallas kernels for 4%

profile of v1, /device:TPU:34, one launch (start us, length us, event | category | flops | bytes accessed | tf_op | source)
XLA Modules:
  0.0 90.9 jit_solution(979623546010886097)
XLA Ops:
  1.4 2.3 %shard_map.157 = (bf16[416,128]{1,0:T(8,128)(2,1)S(1)}, bf16[408,384]{1,0:T(8,128)(2,1)S(1)}, bf16[408,384]{1,0:T(8,128)(2,1)S(1)}, f32[400,256]{1,0:T(8,128)}) custom-call(s32[1]{0:T(128)} %bitcast.core_ref, s32[1,4]{1,0:T(1,128)} %tile_ref.5, s32[1,2]{1,0:T(1,128)} %band_ref.5, s32[1,1]{1,0:T(1,128)S(6)} %copy.106.live_ref, s32[1,8]{1,0:T(1,128)} %neg_ref.3, ...), custom_call_target="tpu_custom_call" | custom-call | tf_op jit(solution)/shard_map/pallas_call | solution.py:48
  3.7 3.8 %collective-permute-start.22 = (bf16[408,384]{1,0:T(8,128)(2,1)S(1)}, bf16[408,384]{1,0:T(8,128)(2,1)S(1)}, u32[]{:S(2)}, u32[]{:S(2)}) collective-permute-start(bf16[408,384]{1,0:T(8,128)(2,1)S(1)} %get-tuple-element.673), channel_id=1, source_target_pairs={{0,4},{4,8},{8,12},{12,16},{16,20},{20,24},{24,28},{28,32},{32,36}... | collective-permute-start | bytes 940040 | tf_op jit(solution)/shard_map/ppermute | solution.py:288
  7.5 2.0 %collective-permute-start.23 = (bf16[408,384]{1,0:T(8,128)(2,1)S(1)}, bf16[408,384]{1,0:T(8,128)(2,1)S(1)}, u32[]{:S(2)}, u32[]{:S(2)}) collective-permute-start(bf16[408,384]{1,0:T(8,128)(2,1)S(1)} %get-tuple-element.674), channel_id=1, source_target_pairs={{4,0},{8,4},{12,8},{16,12},{20,16},{24,20},{28,24},{32,28},{36,32}... | collective-permute-start | bytes 940040 | tf_op jit(solution)/shard_map/ppermute | solution.py:289
  10.3 4.5 %collective-permute-done.22 = bf16[408,384]{1,0:T(8,128)(2,1)S(1)} collective-permute-done((bf16[408,384]{1,0:T(8,128)(2,1)S(1)}, bf16[408,384]{1,0:T(8,128)(2,1)S(1)}, u32[]{:S(2)}, u32[]{:S(2)}) %collective-permute-start.22) | collective-permute-done | bytes 313376 | tf_op jit(solution)/shard_map/ppermute | solution.py:288
  14.7 3.7 %collective-permute-done.23 = bf16[408,384]{1,0:T(8,128)(2,1)S(1)} collective-permute-done((bf16[408,384]{1,0:T(8,128)(2,1)S(1)}, bf16[408,384]{1,0:T(8,128)(2,1)S(1)}, u32[]{:S(2)}, u32[]{:S(2)}) %collective-permute-start.23) | collective-permute-done | bytes 313376 | tf_op jit(solution)/shard_map/ppermute | solution.py:289
  18.5 0.0 copy-done.9
  18.5 0.0 copy-done.3
  18.5 0.0 copy-done.6
  18.5 0.0 copy-done.7
  18.5 0.0 copy-done
  18.5 8.7 %conditional.3 = (bf16[416,128]{1,0:T(8,128)(2,1)S(1)}, bf16[400,768]{1,0:T(8,128)(2,1)S(1)}, f32[400,512]{1,0:T(8,128)S(1)}, f32[400,256]{1,0:T(8,128)}, f32[400,256]{1,0:T(8,128)}) conditional(s32[]{:T(128)} %bitcast.1, (s32[1,4]{1,0:T(1,128)S(1)}, s32[1,2]{1,0:T(1,128)S(1)}, f32[400,256]{1,0:T(8,128)S(1)}, ...), branch_computations={%region_8.0_spmd, %region_9.0_spmd, %region_10.0_spmd, %region_11.... | conditional | bytes 639056 | solution.py:265
  18.6 5.0 %collective-permute-start.9 = (bf16[416,128]{1,0:T(8,128)(2,1)S(1)}, bf16[416,128]{1,0:T(8,128)(2,1)S(1)}, u32[]{:S(2)}, u32[]{:S(2)}) collective-permute-start(bf16[416,128]{1,0:T(8,128)(2,1)S(1)} %get-tuple-element.449), channel_id=1, source_target_pairs={{0,12},{4,8},{8,4},{12,0},{16,28},{20,24},{24,20},{28,16},{32,44},... | collective-permute-start | bytes 319496 | tf_op jit(solution)/shard_map/cond/branch_3_fun/ppermute | solution.py:260
  23.6 3.2 %branch_3_fun.1 = (bf16[400,768]{1,0:T(8,128)(2,1)S(1)}, f32[400,512]{1,0:T(8,128)S(1)}, f32[400,256]{1,0:T(8,128)}, f32[400,256]{1,0:T(8,128)}) custom-call(s32[1,4]{1,0:T(1,128)S(1)} %get-tuple-element.450.tile_ref, s32[1,2]{1,0:T(1,128)S(1)} %get-tuple-element.451.band_ref, f32[400,256]{1,0:T(8,128)S(1)} %get-tuple-element.452.emb_ref, ...), custom_call_target="tpu_custom_call" | custom-call | tf_op jit(solution)/shard_map/cond/branch_3_fun/pallas_call | solution.py:48
  26.8 0.0 collective-permute-done.9
  27.3 1.9 %collective-permute-start.24 = (bf16[416,128]{1,0:T(8,128)(2,1)S(1)}, bf16[416,128]{1,0:T(8,128)(2,1)S(1)}, u32[]{:S(2)}, u32[]{:S(2)}) collective-permute-start(bf16[416,128]{1,0:T(8,128)(2,1)S(1)} %get-tuple-element.676.got_ref), channel_id=1, source_target_pairs={{0,1},{1,0},{2,3},{3,2},{4,5},{5,4},{6,7},{7,6},{8,9},{9,8},{10,11... | collective-permute-start | bytes 319496 | tf_op jit(solution)/shard_map/ppermute | solution.py:269
  29.2 1.3 %collective-permute-done.24.other_ref = bf16[416,128]{1,0:T(8,128)(2,1)S(1)} collective-permute-done((bf16[416,128]{1,0:T(8,128)(2,1)S(1)}, bf16[416,128]{1,0:T(8,128)(2,1)S(1)}, u32[]{:S(2)}, u32[]{:S(2)}) %collective-permute-start.24) | collective-permute-done | bytes 106528 | tf_op jit(solution)/shard_map/ppermute | solution.py:269
  30.5 0.6 copy-done.4
  31.1 3.5 %shard_map.158 = (bf16[16,8,400]{2,1,0:T(8,128)(2,1)}, f32[400,768]{1,0:T(8,128)}) custom-call(s32[1]{0:T(128)} %bitcast.core_ref, s32[1,4]{1,0:T(1,128)S(1)} %copy-done.9, s32[1,2]{1,0:T(1,128)S(1)} %copy-done.10, s32[1,1]{1,0:T(1,128)S(6)} %copy.106.live_ref, s32[1,8]{1,0:T(1,128)} %neg_ref.3, bf16[416,128]{1,0:T(8,128)(2,1)S(1)} %get-tuple-element.676.got_ref, ...), custom_call_target="tpu_custom_call" | custom-call | tf_op jit(solution)/shard_map/pallas_call | solution.py:48
  34.6 5.4 %shard_map.159 = f32[400,256]{1,0:T(8,128)} custom-call(s32[1]{0:T(128)} %bitcast.core_ref, s32[1,4]{1,0:T(1,128)S(1)} %copy-done.9, s32[1,2]{1,0:T(1,128)S(1)} %copy-done.10, bf16[416,128]{1,0:T(8,128)(2,1)S(1)} %get-tuple-element.676.got_ref, bf16[416,128]{1,0:T(8,128)(2,1)} %copy-done.4, f32[400,256]{1,0:T(8,128)S(1)} %bitcast.25, ...), custom_call_target="tpu_custom_call" | custom-call | tf_op jit(solution)/shard_map/pallas_call | solution.py:48
  40.0 2.2 %collective-permute-start.25 = (f32[400,256]{1,0:T(8,128)}, f32[400,256]{1,0:T(8,128)S(1)}, u32[]{:S(2)}, u32[]{:S(2)}) collective-permute-start(f32[400,256]{1,0:T(8,128)} %shard_map.159), channel_id=1, source_target_pairs={{0,1},{1,0},{2,3},{3,2},{4,5},{5,4},{6,7},{7,6},{8,9},{9,8},{10,11... | collective-permute-start | bytes 1228808 | tf_op jit(solution)/shard_map/ppermute | solution.py:269
  42.2 29.2 %all_to_all.10 = bf16[16,8,400]{2,1,0:T(8,128)(2,1)S(1)} all-to-all(bf16[16,8,400]{2,1,0:T(8,128)(2,1)S(1)} %copy-done.11), channel_id=1, replica_groups=mesh['x'=4,'yh'=2,'z'=16,'rel'=4] {'z'}, dimensions={0} | all-to-all | bytes 204800 | tf_op jit(solution)/shard_map/all_to_all | solution.py:312
  71.5 0.6 broadcast_in_dim.2
  72.1 7.5 %all-to-all-start.1 = ((bf16[8,8,400]{2,1,0:T(8,128)(2,1)}), bf16[8,8,400]{2,1,0:T(8,128)(2,1)S(1)}, u32[]{:S(2)}, u32[]{:S(2)}) async-start(bf16[8,8,400]{2,1,0:T(8,128)(2,1)} %broadcast_in_dim.2), calls=%async_computation.1 | async-start | bytes 131072 | tf_op jit(solution)/shard_map/all_to_all | solution.py:330
  79.5 0.0 collective-permute-done.25
  79.5 1.0 %add_convert_fusion.mine_ref = bf16[400,256]{1,0:T(8,128)(2,1)S(1)} fusion(f32[400,256]{1,0:T(8,128)} %shard_map.159, f32[400,256]{1,0:T(8,128)S(1)} %collective-permute-done.25), kind=kLoop, calls=%fused_computation | loop fusion | flops 204800 | bytes 1024000 | tf_op jit(solution)/shard_map/convert_element_type | solution.py:320
  80.6 2.6 %collective-permute-start.26 = (bf16[400,256]{1,0:T(8,128)(2,1)S(1)}, bf16[400,256]{1,0:T(8,128)(2,1)S(1)}, u32[]{:S(2)}, u32[]{:S(2)}) collective-permute-start(bf16[400,256]{1,0:T(8,128)(2,1)S(1)} %add_convert_fusion.mine_ref), channel_id=1, source_target_pairs={{0,2},{1,3},{2,0},{3,1},{4,6},{5,7},{6,4},{7,5},{8,10},{9,11},{10,... | collective-permute-start | bytes 614408 | tf_op jit(solution)/shard_map/ppermute | solution.py:269
  83.2 2.8 %all-to-all-done.1 = bf16[8,8,400]{2,1,0:T(8,128)(2,1)S(1)} async-done(((bf16[8,8,400]{2,1,0:T(8,128)(2,1)}), bf16[8,8,400]{2,1,0:T(8,128)(2,1)S(1)}, u32[]{:S(2)}, u32[]{:S(2)}) %all-to-all-start.1) | async-done | bytes 51232 | tf_op jit(solution)/shard_map/all_to_all | solution.py:330
  86.0 0.1 multiply_reduce_fusion
  86.1 0.7 divide_subtract_fusion
  86.8 1.5 %collective-permute-done.26.other_ref = bf16[400,256]{1,0:T(8,128)(2,1)S(1)} collective-permute-done((bf16[400,256]{1,0:T(8,128)(2,1)S(1)}, bf16[400,256]{1,0:T(8,128)(2,1)S(1)}, u32[]{:S(2)}, u32[]{:S(2)}) %collective-permute-start.26) | collective-permute-done | bytes 204832 | tf_op jit(solution)/shard_map/ppermute | solution.py:269
  88.3 0.7 copy-done.8
  88.9 1.9 %shard_map.160 = (f32[400,256]{1,0:T(8,128)}, f32[1,256]{1,0:T(1,128)}) custom-call(bf16[400,256]{1,0:T(8,128)(2,1)} %copy-done.2, bf16[400,256]{1,0:T(8,128)(2,1)} %copy-done.8, f32[400,256]{1,0:T(8,128)S(1)} %bitcast.26, f32[1,256]{1,0:T(1,128)} %bitcast.44), custom_call_target="tpu_custom_call" | custom-call | tf_op jit(solution)/shard_map/pallas_call | solution.py:48
  (24 shorter events, 0.1 us)
Async XLA Ops:
  0.6 17.9 %copy-start.1 = (f32[8,400]{1,0:T(8,128)S(1)}, f32[8,400]{1,0:T(8,128)}, u32[]{:S(2)}) copy-start(f32[8,400]{1,0:T(8,128)} %relw_ref.5) | copy-start | bytes 38404
  0.6 17.8 %copy-start.10 = (s32[1,2]{1,0:T(1,128)S(1)}, s32[1,2]{1,0:T(1,128)}, u32[]{:S(2)}) copy-start(s32[1,2]{1,0:T(1,128)} %band_ref.5) | copy-start | bytes 28
  0.7 17.8 %copy-start.9 = (s32[1,4]{1,0:T(1,128)S(1)}, s32[1,4]{1,0:T(1,128)}, u32[]{:S(2)}) copy-start(s32[1,4]{1,0:T(1,128)} %tile_ref.5) | copy-start | bytes 52
  0.7 17.8 %copy-start.3 = (s32[1,512]{1,0:T(1,128)S(1)}, s32[1,512]{1,0:T(1,128)}, u32[]{:S(2)}) copy-start(s32[1,512]{1,0:T(1,128)} %src_ref.3) | copy-start | bytes 6148
  0.7 17.8 %copy-start.6 = (s32[1,256]{1,0:T(1,128)S(1)}, s32[1,256]{1,0:T(1,128)}, u32[]{:S(2)}) copy-start(s32[1,256]{1,0:T(1,128)} %bdst_ref.1) | copy-start | bytes 3076
  0.7 17.8 %copy-start.7 = (s32[256]{0:T(256)S(1)}, s32[256]{0:T(256)}, u32[]{:S(2)}) copy-start(s32[256]{0:T(256)} %param.48) | copy-start | bytes 3076
  0.7 17.8 %copy-start = (f32[256,400]{0,1:T(8,128)S(1)}, f32[256,400]{0,1:T(8,128)}, u32[]{:S(2)}) copy-start(f32[256,400]{0,1:T(8,128)} %param.38) | copy-start | bytes 1228804
  3.7 11.0 %collective-permute-start.22 = (bf16[408,384]{1,0:T(8,128)(2,1)S(1)}, bf16[408,384]{1,0:T(8,128)(2,1)S(1)}, u32[]{:S(2)}, u32[]{:S(2)}) collective-permute-start(bf16[408,384]{1,0:T(8,128)(2,1)S(1)} %get-tuple-element.673), channel_id=1, source_target_pairs={{0,4},{4,8},{8,12},{12,16},{16,20},{20,24},{24,28},{28,32},{32,36}... | collective-permute-start | bytes 940040 | tf_op jit(solution)/shard_map/ppermute | solution.py:288
  7.5 10.9 %collective-permute-start.23 = (bf16[408,384]{1,0:T(8,128)(2,1)S(1)}, bf16[408,384]{1,0:T(8,128)(2,1)S(1)}, u32[]{:S(2)}, u32[]{:S(2)}) collective-permute-start(bf16[408,384]{1,0:T(8,128)(2,1)S(1)} %get-tuple-element.674), channel_id=1, source_target_pairs={{4,0},{8,4},{12,8},{16,12},{20,16},{24,20},{28,24},{32,28},{36,32}... | collective-permute-start | bytes 940040 | tf_op jit(solution)/shard_map/ppermute | solution.py:289
  18.6 8.3 %collective-permute-start.9 = (bf16[416,128]{1,0:T(8,128)(2,1)S(1)}, bf16[416,128]{1,0:T(8,128)(2,1)S(1)}, u32[]{:S(2)}, u32[]{:S(2)}) collective-permute-start(bf16[416,128]{1,0:T(8,128)(2,1)S(1)} %get-tuple-element.449), channel_id=1, source_target_pairs={{0,12},{4,8},{8,4},{12,0},{16,28},{20,24},{24,20},{28,16},{32,44},... | collective-permute-start | bytes 319496 | tf_op jit(solution)/shard_map/cond/branch_3_fun/ppermute | solution.py:260
  27.3 3.2 %collective-permute-start.24 = (bf16[416,128]{1,0:T(8,128)(2,1)S(1)}, bf16[416,128]{1,0:T(8,128)(2,1)S(1)}, u32[]{:S(2)}, u32[]{:S(2)}) collective-permute-start(bf16[416,128]{1,0:T(8,128)(2,1)S(1)} %get-tuple-element.676.got_ref), channel_id=1, source_target_pairs={{0,1},{1,0},{2,3},{3,2},{4,5},{5,4},{6,7},{7,6},{8,9},{9,8},{10,11... | collective-permute-start | bytes 319496 | tf_op jit(solution)/shard_map/ppermute | solution.py:269
  30.5 0.6 copy-start.4
  31.1 3.5 %copy-start.5 = (f32[400,256]{1,0:T(8,128)S(1)}, f32[400,256]{1,0:T(8,128)}, u32[]{:S(2)}) copy-start(f32[400,256]{1,0:T(8,128)} %get-tuple-element.682.back_ref) | copy-start | bytes 1228804
  34.6 7.6 %copy-start.11 = (bf16[16,8,400]{2,1,0:T(8,128)(2,1)S(1)}, bf16[16,8,400]{2,1,0:T(8,128)(2,1)}, u32[]{:S(2)}) copy-start(bf16[16,8,400]{2,1,0:T(8,128)(2,1)} %get-tuple-element.685) | copy-start | bytes 307204
  40.0 46.1 %copy-start.12 = (f32[8]{0:T(128)S(1)}, f32[8]{0:T(128)}, u32[]{:S(2)}) copy-start(f32[8]{0:T(128)} %param.41) | copy-start | bytes 100
  40.0 39.5 %collective-permute-start.25 = (f32[400,256]{1,0:T(8,128)}, f32[400,256]{1,0:T(8,128)S(1)}, u32[]{:S(2)}, u32[]{:S(2)}) collective-permute-start(f32[400,256]{1,0:T(8,128)} %shard_map.159), channel_id=1, source_target_pairs={{0,1},{1,0},{2,3},{3,2},{4,5},{5,4},{6,7},{7,6},{8,9},{9,8},{10,11... | collective-permute-start | bytes 1228808 | tf_op jit(solution)/shard_map/ppermute | solution.py:269
  72.1 13.9 %all-to-all-start.1 = ((bf16[8,8,400]{2,1,0:T(8,128)(2,1)}), bf16[8,8,400]{2,1,0:T(8,128)(2,1)S(1)}, u32[]{:S(2)}, u32[]{:S(2)}) async-start(bf16[8,8,400]{2,1,0:T(8,128)(2,1)} %broadcast_in_dim.2), calls=%async_computation.1 | async-start | bytes 131072 | tf_op jit(solution)/shard_map/all_to_all | solution.py:330
  80.6 7.7 %copy-start.2 = (bf16[400,256]{1,0:T(8,128)(2,1)}, bf16[400,256]{1,0:T(8,128)(2,1)S(1)}, u32[]{:S(2)}) copy-start(bf16[400,256]{1,0:T(8,128)(2,1)S(1)} %add_convert_fusion.mine_ref) | copy-start | bytes 614404
  80.6 7.7 %collective-permute-start.26 = (bf16[400,256]{1,0:T(8,128)(2,1)S(1)}, bf16[400,256]{1,0:T(8,128)(2,1)S(1)}, u32[]{:S(2)}, u32[]{:S(2)}) collective-permute-start(bf16[400,256]{1,0:T(8,128)(2,1)S(1)} %add_convert_fusion.mine_ref), channel_id=1, source_target_pairs={{0,2},{1,3},{2,0},{3,1},{4,6},{5,7},{6,4},{7,5},{8,10},{9,11},{10,... | collective-permute-start | bytes 614408 | tf_op jit(solution)/shard_map/ppermute | solution.py:269
  88.3 0.7 copy-start.8

commit v2 on v1

--- a/solution.py
+++ b/solution.py
@@ -241,16 +241,28 @@
     edge_ids, band_ids = tile_ids(tile_ref, band_ref)
     steps = step_ref[...] * weights(relw, relations(edge_ids + band_ids))
     pick = jnp.concatenate([ones(hits(ROWS, src_ref[...])), ones(hits(ROWS, bsrc_ref[...]))], axis=1)
-    total_ref[...] = (
-        back_ref[...] + mm_two(steps, pick, NT) + mm(q, high, NT) + mm(q, low, NT)
-    )
-
-
-def final_kernel(mine_ref, other_ref, emb_ref, state_ref, new_ref, fresh_ref):
-    grad = mine_ref[...].astype(F32) + other_ref[...].astype(F32)
+    total = back_ref[...] + mm_two(steps, pick, NT) + mm(q, high, NT) + mm(q, low, NT)
+    total_ref[...] = total.astype(BF)
+
+
+def final_kernel(own_ref, core_ref, far_ref, cross_ref, emb_ref, state_ref, new_ref, fresh_ref):
+    near = own_ref[...].astype(F32) + core_ref[...].astype(F32)
+    grad = near + (far_ref[...].astype(F32) + cross_ref[...].astype(F32))
     fresh = state_ref[...] + jnp.sum(grad * grad, axis=0, keepdims=True) / D
     fresh_ref[...] = fresh
     new_ref[...] = emb_ref[...] - step_rate * grad / jnp.sqrt(fresh)
+
+
+def update_kernel(state_ref, gw_ref, relw_ref, new_ref):
+    gw = gw_ref[0, :, :].astype(F32)
+    for k in range(1, XY):
+        gw = gw + gw_ref[k, :, :].astype(F32)
+    row = lax.broadcasted_iota(jnp.int32, (RELS, 1), 0)
+    state = jnp.zeros((RELS, 1), F32)
+    for k in range(RELS):
+        state = jnp.where(row == k, state_ref[k], state)
+    fresh = state + jnp.sum(gw * gw, axis=1, keepdims=True) / D
+    new_ref[...] = relw_ref[...] - step_rate * gw / jnp.sqrt(fresh)
 
 
 def swap(axes, size, number, work):
@@ -287,7 +299,7 @@
     )
     from_low = lax.ppermute(to_up, DOM, [(i, i + 1) for i in range(count - 1)])
     from_high = lax.ppermute(to_down, DOM, [(i + 1, i) for i in range(count - 1)])
-    (got,) = swap(("x", "yh"), XY, lax.shift_right_logical(mask, 4), lambda: ())(part)
+    (got,) = swap("z", Z, lax.bitwise_and(mask, 15), lambda: ())(part)
 
     def sources(*args):
         return call(
@@ -297,7 +309,8 @@
             *args,
         )
 
-    got, q, rows, dq_band, back = swap("z", Z, lax.bitwise_and(mask, 15), sources)(
+    along_xy = swap(("x", "yh"), XY, lax.shift_right_logical(mask, 4), sources)
+    got, q, rows, dq_band, back = along_xy(
         got, tile_rel, band_rel, emb_t, rel_weight, src_rows, band_dst, bound, to_up, to_down,
         from_low, from_high,
     )
@@ -313,23 +326,23 @@
     (total,) = call(
         partner_kernel,
         "sssvvvvvvvv",
-        [((D, ROWS), F32)],
+        [((D, ROWS), BF)],
         core, tile_rel, band_rel, got, other_half, emb_t, rel_weight, step, src_rows,
         band_src, back,
     )
-    pair = (total + trade(total, 1)).astype(BF)
-    other = trade(pair, 2)
+    from_cross = trade(total, 3)
+    from_y = trade(total, 2)
+    from_core = trade(total, 1)
     new_t, fresh = call(
         final_kernel,
-        "vvvv",
+        "vvvvvv",
         [((D, ROWS), F32), ((1, ROWS), F32)],
-        pair, other, emb_t, emb_state.reshape(1, ROWS),
+        total, from_core, from_y, from_cross, emb_t, emb_state.reshape(1, ROWS),
     )
     gw = jnp.sum(gw.astype(F32), axis=0).astype(BF)
     gw = jnp.broadcast_to(gw[None], (XY, RELS, D))
     gw = lax.all_to_all(gw, ("x", "yh"), split_axis=0, concat_axis=0, tiled=True)
-    gw = jnp.sum(gw.astype(F32), axis=0)
-    rel_new = rel_weight - step_rate * gw / jnp.sqrt(rel_state + jnp.mean(gw * gw, axis=1))[:, None]
+    (rel_new,) = call(update_kernel, "svv", [((RELS, D), F32)], rel_state, gw, rel_weight)
     return (new_t.T, fresh.reshape(ROWS), rel_new)
 
 

time: 91.4 us -> 79.2 us (0.87)
  the two profiles are of different devices: /device:TPU:34 before, /device:TPU:32 now
where the time goes in v2:
time: 79.2 us; the launch traced here: 78.7 us
  starting transfers between devices  42.2 us (53%)
  Pallas kernels  18.1 us (23%)
  waiting for transfers between devices  13.4 us (17%)
  local copies, waits for them, and re-layouts  2.73 us (3%)
  between operations  2.17 us (3%)
    pallas_call x6, Pallas kernels, call(): pl.pallas_call(kernel, in_specs=[smem() if kind == 's' else vmem() for ki...  18.1 us
    all_to_all x1, starting transfers between devices, body(): gw = lax.all_to_all(gw, 'z', split_axis=0, concat_axis=0, tiled=True)  15.1 us
    ppermute x4, starting transfers between devices, trade(): return lax.ppermute(values, 'rel', [(i, i ^ bit) for i in range(N_REL)])  9.48 us
    all_to_all x1, starting transfers between devices, body(): lax.all_to_all(gw, ('x', 'yh'), split_axis=0, concat_axis=0, tiled=True)  6.86 us
    ppermute x1, waiting for transfers between devices, run(): moved = lax.ppermute(moved, axes, [(i, i ^ k) for i in range(size)])  6.37 us
    ppermute x1, starting transfers between devices, body(): lax.ppermute(to_down, DOM, [(i + 1, i) for i in range(count - 1)])  4.85 us
    all_to_all x1, waiting for transfers between devices, body(): lax.all_to_all(gw, ('x', 'yh'), split_axis=0, concat_axis=0, tiled=True)  4.71 us
    ppermute x1, starting transfers between devices, body(): from_low = lax.ppermute(to_up, DOM, [(i, i + 1) for i in range(count - 1)])  3.81 us
  transfers between devices with their start and end apart: 9, of which 4 were waited for; matrix products, arithmetic and copies ran while one was open for 1% of the time, Pallas kernels for 10%

profile of v2, /device:TPU:32, one launch (start us, length us, event | category | flops | bytes accessed | tf_op | source)
XLA Modules:
  0.0 78.7 jit_solution(9599997407034504180)
XLA Ops:
  1.3 2.3 %shard_map.157 = (bf16[416,128]{1,0:T(8,128)(2,1)S(1)}, bf16[408,384]{1,0:T(8,128)(2,1)S(1)}, bf16[408,384]{1,0:T(8,128)(2,1)S(1)}, f32[400,256]{1,0:T(8,128)}) custom-call(s32[1]{0:T(128)} %bitcast.core_ref, s32[1,4]{1,0:T(1,128)} %tile_ref.5, s32[1,2]{1,0:T(1,128)} %band_ref.5, s32[1,1]{1,0:T(1,128)S(6)} %copy.74.live_ref, s32[1,8]{1,0:T(1,128)} %neg_ref.3, ...), custom_call_target="tpu_custom_call" | custom-call | tf_op jit(solution)/shard_map/pallas_call | solution.py:48
  3.6 3.8 %collective-permute-start.22 = (bf16[408,384]{1,0:T(8,128)(2,1)S(1)}, bf16[408,384]{1,0:T(8,128)(2,1)S(1)}, u32[]{:S(2)}, u32[]{:S(2)}) collective-permute-start(bf16[408,384]{1,0:T(8,128)(2,1)S(1)} %get-tuple-element.369), channel_id=1, source_target_pairs={{0,4},{4,8},{8,12},{12,16},{16,20},{20,24},{24,28},{28,32},{32,36}... | collective-permute-start | bytes 940040 | tf_op jit(solution)/shard_map/ppermute | solution.py:300
  7.4 4.8 %collective-permute-start.23 = (bf16[408,384]{1,0:T(8,128)(2,1)S(1)}, bf16[408,384]{1,0:T(8,128)(2,1)S(1)}, u32[]{:S(2)}, u32[]{:S(2)}) collective-permute-start(bf16[408,384]{1,0:T(8,128)(2,1)S(1)} %get-tuple-element.370), channel_id=1, source_target_pairs={{4,0},{8,4},{12,8},{16,12},{20,16},{24,20},{28,24},{32,28},{36,32}... | collective-permute-start | bytes 940040 | tf_op jit(solution)/shard_map/ppermute | solution.py:301
  12.9 0.0 copy-start
  12.9 0.0 copy-start.1
  13.0 0.0 copy-start.8
  13.0 0.0 copy-start.10
  13.0 0.0 copy-start.11
  13.0 8.5 %conditional.2 = (bf16[416,128]{1,0:T(8,128)(2,1)S(1)}) conditional(s32[]{:T(128)} %bitcast.4, bf16[416,128]{1,0:T(8,128)(2,1)S(1)} %get-tuple-element.371, bf16[416,128]{1,0:T(8,128)(2,1)S(1)} %get-tuple-element.371, bf16[416,128]{1,0:T(8,128)(2,1)S(1)} %get-tuple-element.371, ...), branch_computations={%region_0.0_spmd, %region_1.0_spmd, %region_2.0_spmd, %region_3.0_... | conditional | bytes 639024 | solution.py:277
  13.1 2.1 %collective-permute-start.2 = (bf16[416,128]{1,0:T(8,128)(2,1)S(1)}, bf16[416,128]{1,0:T(8,128)(2,1)S(1)}, u32[]{:S(2)}, u32[]{:S(2)}) collective-permute-start(bf16[416,128]{1,0:T(8,128)(2,1)S(1)} %param.3), channel_id=1, source_target_pairs={{0,12},{4,8},{8,4},{12,0},{16,28},{20,24},{24,20},{28,16},{32,44},... | collective-permute-start | bytes 319496 | tf_op jit(solution)/shard_map/cond/branch_3_fun/ppermute | solution.py:272
  15.1 6.4 %collective-permute-done.2 = bf16[416,128]{1,0:T(8,128)(2,1)S(1)} collective-permute-done((bf16[416,128]{1,0:T(8,128)(2,1)S(1)}, bf16[416,128]{1,0:T(8,128)(2,1)S(1)}, u32[]{:S(2)}, u32[]{:S(2)}) %collective-permute-start.2) | collective-permute-done | bytes 106528 | tf_op jit(solution)/shard_map/cond/branch_3_fun/ppermute | solution.py:272
  21.6 3.2 %conditional.3 = (bf16[416,128]{1,0:T(8,128)(2,1)S(1)}, bf16[400,768]{1,0:T(8,128)(2,1)S(1)}, f32[400,512]{1,0:T(8,128)S(1)}, f32[400,256]{1,0:T(8,128)}, f32[400,256]{1,0:T(8,128)}) conditional(s32[]{:T(128)} %bitcast.1, (s32[1,4]{1,0:T(1,128)S(1)}, s32[1,2]{1,0:T(1,128)S(1)}, f32[400,256]{1,0:T(8,128)S(1)}, ...), branch_computations={%region_16.0_spmd, %region_17.0_spmd, %region_18.0_spmd, %region_1... | conditional | bytes 639056 | solution.py:277
  21.6 3.2 %branch_0_fun.1 = (bf16[400,768]{1,0:T(8,128)(2,1)S(1)}, f32[400,512]{1,0:T(8,128)S(1)}, f32[400,256]{1,0:T(8,128)}, f32[400,256]{1,0:T(8,128)}) custom-call(s32[1,4]{1,0:T(1,128)S(1)} %get-tuple-element.226.tile_ref, s32[1,2]{1,0:T(1,128)S(1)} %get-tuple-element.227.band_ref, f32[400,256]{1,0:T(8,128)S(1)} %get-tuple-element.228.emb_ref, ...), custom_call_target="tpu_custom_call" | custom-call | tf_op jit(solution)/shard_map/cond/branch_0_fun/pallas_call | solution.py:48
  24.8 1.9 %collective-permute-start.24 = (bf16[416,128]{1,0:T(8,128)(2,1)S(1)}, bf16[416,128]{1,0:T(8,128)(2,1)S(1)}, u32[]{:S(2)}, u32[]{:S(2)}) collective-permute-start(bf16[416,128]{1,0:T(8,128)(2,1)S(1)} %get-tuple-element.372.got_ref), channel_id=1, source_target_pairs={{0,1},{1,0},{2,3},{3,2},{4,5},{5,4},{6,7},{7,6},{8,9},{9,8},{10,11... | collective-permute-start | bytes 319496 | tf_op jit(solution)/shard_map/ppermute | solution.py:281
  26.7 1.3 %collective-permute-done.24.other_ref = bf16[416,128]{1,0:T(8,128)(2,1)S(1)} collective-permute-done((bf16[416,128]{1,0:T(8,128)(2,1)S(1)}, bf16[416,128]{1,0:T(8,128)(2,1)S(1)}, u32[]{:S(2)}, u32[]{:S(2)}) %collective-permute-start.24) | collective-permute-done | bytes 106528 | tf_op jit(solution)/shard_map/ppermute | solution.py:281
  28.0 0.6 copy-done.2
  28.7 3.5 %shard_map.158 = (bf16[16,8,400]{2,1,0:T(8,128)(2,1)}, f32[400,768]{1,0:T(8,128)}) custom-call(s32[1]{0:T(128)} %bitcast.core_ref, s32[1,4]{1,0:T(1,128)S(1)} %copy-done.11, s32[1,2]{1,0:T(1,128)S(1)} %copy-done.12, s32[1,1]{1,0:T(1,128)S(6)} %copy.74.live_ref, s32[1,8]{1,0:T(1,128)} %neg_ref.3, bf16[416,128]{1,0:T(8,128)(2,1)S(1)} %get-tuple-element.372.got_ref, ...), custom_call_target="tpu_custom_call" | custom-call | tf_op jit(solution)/shard_map/pallas_call | solution.py:48
  32.1 15.1 %all-to-all-start = ((bf16[16,8,400]{2,1,0:T(8,128)(2,1)}), bf16[16,8,400]{2,1,0:T(8,128)(2,1)S(1)}, u32[]{:S(2)}, u32[]{:S(2)}) async-start(bf16[16,8,400]{2,1,0:T(8,128)(2,1)} %get-tuple-element.381), calls=%async_computation | async-start | bytes 262144 | tf_op jit(solution)/shard_map/all_to_all | solution.py:325
  47.3 5.3 %shard_map.159.own_ref = bf16[400,256]{1,0:T(8,128)(2,1)} custom-call(s32[1]{0:T(128)} %bitcast.core_ref, s32[1,4]{1,0:T(1,128)S(1)} %copy-done.11, s32[1,2]{1,0:T(1,128)S(1)} %copy-done.12, bf16[416,128]{1,0:T(8,128)(2,1)S(1)} %get-tuple-element.372.got_ref, bf16[416,128]{1,0:T(8,128)(2,1)} %copy-done.2, f32[400,256]{1,0:T(8,128)S(1)} %bitcast.17, ...), custom_call_target="tpu_custom_call" | custom-call | tf_op jit(solution)/shard_map/pallas_call | solution.py:48
  52.6 2.7 %collective-permute-start.27 = (bf16[400,256]{1,0:T(8,128)(2,1)}, bf16[400,256]{1,0:T(8,128)(2,1)S(1)}, u32[]{:S(2)}, u32[]{:S(2)}) collective-permute-start(bf16[400,256]{1,0:T(8,128)(2,1)} %shard_map.159.own_ref), channel_id=1, source_target_pairs={{0,3},{1,2},{2,1},{3,0},{4,7},{5,6},{6,5},{7,4},{8,11},{9,10},{10,... | collective-permute-start | bytes 614408 | tf_op jit(solution)/shard_map/ppermute | solution.py:281
  55.3 2.7 %collective-permute-start.26 = (bf16[400,256]{1,0:T(8,128)(2,1)}, bf16[400,256]{1,0:T(8,128)(2,1)S(1)}, u32[]{:S(2)}, u32[]{:S(2)}) collective-permute-start(bf16[400,256]{1,0:T(8,128)(2,1)} %shard_map.159.own_ref), channel_id=1, source_target_pairs={{0,2},{1,3},{2,0},{3,1},{4,6},{5,7},{6,4},{7,5},{8,10},{9,11},{10,... | collective-permute-start | bytes 614408 | tf_op jit(solution)/shard_map/ppermute | solution.py:281
  58.0 2.2 %collective-permute-start.25 = (bf16[400,256]{1,0:T(8,128)(2,1)}, bf16[400,256]{1,0:T(8,128)(2,1)S(1)}, u32[]{:S(2)}, u32[]{:S(2)}) collective-permute-start(bf16[400,256]{1,0:T(8,128)(2,1)} %shard_map.159.own_ref), channel_id=1, source_target_pairs={{0,1},{1,0},{2,3},{3,2},{4,5},{5,4},{6,7},{7,6},{8,9},{9,8},{10,11... | collective-permute-start | bytes 614408 | tf_op jit(solution)/shard_map/ppermute | solution.py:281
  60.2 1.0 %all-to-all-done = bf16[16,8,400]{2,1,0:T(8,128)(2,1)S(1)} async-done(((bf16[16,8,400]{2,1,0:T(8,128)(2,1)}), bf16[16,8,400]{2,1,0:T(8,128)(2,1)S(1)}, u32[]{:S(2)}, u32[]{:S(2)}) %all-to-all-start) | async-done | bytes 102432 | tf_op jit(solution)/shard_map/all_to_all | solution.py:325
  61.2 0.6 broadcast_in_dim.2
  61.9 6.9 %all-to-all-start.1 = ((bf16[8,8,400]{2,1,0:T(8,128)(2,1)}), bf16[8,8,400]{2,1,0:T(8,128)(2,1)S(1)}, u32[]{:S(2)}, u32[]{:S(2)}) async-start(bf16[8,8,400]{2,1,0:T(8,128)(2,1)} %broadcast_in_dim.2), calls=%async_computation.1 | async-start | bytes 131072 | tf_op jit(solution)/shard_map/all_to_all | solution.py:344
  68.8 0.6 copy-done.5
  69.4 0.1 copy-done.6
  69.5 0.1 copy-done.7
  69.6 2.2 %shard_map.160 = (f32[400,256]{1,0:T(8,128)}, f32[1,256]{1,0:T(1,128)}) custom-call(bf16[400,256]{1,0:T(8,128)(2,1)} %shard_map.159.own_ref, bf16[400,256]{1,0:T(8,128)(2,1)} %copy-done.7, bf16[400,256]{1,0:T(8,128)(2,1)} %copy-done.6, bf16[400,256]{1,0:T(8,128)(2,1)} %copy-done.5, f32[400,256]{1,0:T(8,128)S(1)} %bitcast.18, f32[1,256]{1,0:T(1,128)} %bitcast.28), custom_call_target="tpu_custom_call" | custom-call | tf_op jit(solution)/shard_map/pallas_call | solution.py:48
  71.8 4.7 %all-to-all-done.1.gw_ref = bf16[8,8,400]{2,1,0:T(8,128)(2,1)S(1)} async-done(((bf16[8,8,400]{2,1,0:T(8,128)(2,1)}), bf16[8,8,400]{2,1,0:T(8,128)(2,1)S(1)}, u32[]{:S(2)}, u32[]{:S(2)}) %all-to-all-start.1) | async-done | bytes 51232 | tf_op jit(solution)/shard_map/all_to_all | solution.py:344
  76.5 0.6 copy-done.4
  77.1 1.6 %shard_map.161 = f32[8,400]{1,0:T(8,128)} custom-call(f32[8]{0:T(128)} %state_ref.1, bf16[8,8,400]{2,1,0:T(8,128)(2,1)} %copy-done.4, f32[8,400]{1,0:T(8,128)S(1)} %copy-done.1), custom_call_target="tpu_custom_call" | custom-call | tf_op jit(solution)/shard_map/pallas_call | solution.py:48
  (23 shorter events, 0.1 us)
Async XLA Ops:
  3.6 17.9 %collective-permute-start.22 = (bf16[408,384]{1,0:T(8,128)(2,1)S(1)}, bf16[408,384]{1,0:T(8,128)(2,1)S(1)}, u32[]{:S(2)}, u32[]{:S(2)}) collective-permute-start(bf16[408,384]{1,0:T(8,128)(2,1)S(1)} %get-tuple-element.369), channel_id=1, source_target_pairs={{0,4},{4,8},{8,12},{12,16},{16,20},{20,24},{24,28},{28,32},{32,36}... | collective-permute-start | bytes 940040 | tf_op jit(solution)/shard_map/ppermute | solution.py:300
  7.4 14.1 %collective-permute-start.23 = (bf16[408,384]{1,0:T(8,128)(2,1)S(1)}, bf16[408,384]{1,0:T(8,128)(2,1)S(1)}, u32[]{:S(2)}, u32[]{:S(2)}) collective-permute-start(bf16[408,384]{1,0:T(8,128)(2,1)S(1)} %get-tuple-element.370), channel_id=1, source_target_pairs={{4,0},{8,4},{12,8},{16,12},{20,16},{24,20},{28,24},{32,28},{36,32}... | collective-permute-start | bytes 940040 | tf_op jit(solution)/shard_map/ppermute | solution.py:301
  12.9 8.6 %copy-start = (f32[256,400]{0,1:T(8,128)S(1)}, f32[256,400]{0,1:T(8,128)}, u32[]{:S(2)}) copy-start(f32[256,400]{0,1:T(8,128)} %param.38) | copy-start | bytes 1228804
  12.9 8.6 %copy-start.1 = (f32[8,400]{1,0:T(8,128)S(1)}, f32[8,400]{1,0:T(8,128)}, u32[]{:S(2)}) copy-start(f32[8,400]{1,0:T(8,128)} %relw_ref.7) | copy-start | bytes 38404
  13.0 8.6 %copy-start.8 = (s32[1,512]{1,0:T(1,128)S(1)}, s32[1,512]{1,0:T(1,128)}, u32[]{:S(2)}) copy-start(s32[1,512]{1,0:T(1,128)} %src_ref.3) | copy-start | bytes 6148
  13.0 8.6 %copy-start.9 = (s32[1,256]{1,0:T(1,128)S(1)}, s32[1,256]{1,0:T(1,128)}, u32[]{:S(2)}) copy-start(s32[1,256]{1,0:T(1,128)} %bdst_ref.1) | copy-start | bytes 3076
  13.0 8.6 %copy-start.10 = (s32[256]{0:T(256)S(1)}, s32[256]{0:T(256)}, u32[]{:S(2)}) copy-start(s32[256]{0:T(256)} %param.48) | copy-start | bytes 3076
  13.0 8.6 %copy-start.11 = (s32[1,4]{1,0:T(1,128)S(1)}, s32[1,4]{1,0:T(1,128)}, u32[]{:S(2)}) copy-start(s32[1,4]{1,0:T(1,128)} %tile_ref.5) | copy-start | bytes 52
  13.0 8.6 %copy-start.12 = (s32[1,2]{1,0:T(1,128)S(1)}, s32[1,2]{1,0:T(1,128)}, u32[]{:S(2)}) copy-start(s32[1,2]{1,0:T(1,128)} %band_ref.5) | copy-start | bytes 28
  13.1 8.4 %collective-permute-start.2 = (bf16[416,128]{1,0:T(8,128)(2,1)S(1)}, bf16[416,128]{1,0:T(8,128)(2,1)S(1)}, u32[]{:S(2)}, u32[]{:S(2)}) collective-permute-start(bf16[416,128]{1,0:T(8,128)(2,1)S(1)} %param.3), channel_id=1, source_target_pairs={{0,12},{4,8},{8,4},{12,0},{16,28},{20,24},{24,20},{28,16},{32,44},... | collective-permute-start | bytes 319496 | tf_op jit(solution)/shard_map/cond/branch_3_fun/ppermute | solution.py:272
  24.8 3.2 %collective-permute-start.24 = (bf16[416,128]{1,0:T(8,128)(2,1)S(1)}, bf16[416,128]{1,0:T(8,128)(2,1)S(1)}, u32[]{:S(2)}, u32[]{:S(2)}) collective-permute-start(bf16[416,128]{1,0:T(8,128)(2,1)S(1)} %get-tuple-element.372.got_ref), channel_id=1, source_target_pairs={{0,1},{1,0},{2,3},{3,2},{4,5},{5,4},{6,7},{7,6},{8,9},{9,8},{10,11... | collective-permute-start | bytes 319496 | tf_op jit(solution)/shard_map/ppermute | solution.py:281
  28.0 0.6 copy-start.2
  28.7 18.6 %copy-start.3 = (f32[400,256]{1,0:T(8,128)S(1)}, f32[400,256]{1,0:T(8,128)}, u32[]{:S(2)}) copy-start(f32[400,256]{1,0:T(8,128)} %get-tuple-element.378.back_ref) | copy-start | bytes 1228804
  32.1 29.1 %all-to-all-start = ((bf16[16,8,400]{2,1,0:T(8,128)(2,1)}), bf16[16,8,400]{2,1,0:T(8,128)(2,1)S(1)}, u32[]{:S(2)}, u32[]{:S(2)}) async-start(bf16[16,8,400]{2,1,0:T(8,128)(2,1)} %get-tuple-element.381), calls=%async_computation | async-start | bytes 262144 | tf_op jit(solution)/shard_map/all_to_all | solution.py:325
  52.6 16.1 %collective-permute-start.27 = (bf16[400,256]{1,0:T(8,128)(2,1)}, bf16[400,256]{1,0:T(8,128)(2,1)S(1)}, u32[]{:S(2)}, u32[]{:S(2)}) collective-permute-start(bf16[400,256]{1,0:T(8,128)(2,1)} %shard_map.159.own_ref), channel_id=1, source_target_pairs={{0,3},{1,2},{2,1},{3,0},{4,7},{5,6},{6,5},{7,4},{8,11},{9,10},{10,... | collective-permute-start | bytes 614408 | tf_op jit(solution)/shard_map/ppermute | solution.py:281
  55.3 13.5 %collective-permute-start.26 = (bf16[400,256]{1,0:T(8,128)(2,1)}, bf16[400,256]{1,0:T(8,128)(2,1)S(1)}, u32[]{:S(2)}, u32[]{:S(2)}) collective-permute-start(bf16[400,256]{1,0:T(8,128)(2,1)} %shard_map.159.own_ref), channel_id=1, source_target_pairs={{0,2},{1,3},{2,0},{3,1},{4,6},{5,7},{6,4},{7,5},{8,10},{9,11},{10,... | collective-permute-start | bytes 614408 | tf_op jit(solution)/shard_map/ppermute | solution.py:281
  58.0 10.7 %collective-permute-start.25 = (bf16[400,256]{1,0:T(8,128)(2,1)}, bf16[400,256]{1,0:T(8,128)(2,1)S(1)}, u32[]{:S(2)}, u32[]{:S(2)}) collective-permute-start(bf16[400,256]{1,0:T(8,128)(2,1)} %shard_map.159.own_ref), channel_id=1, source_target_pairs={{0,1},{1,0},{2,3},{3,2},{4,5},{5,4},{6,7},{7,6},{8,9},{9,8},{10,11... | collective-permute-start | bytes 614408 | tf_op jit(solution)/shard_map/ppermute | solution.py:281
  61.9 14.6 %all-to-all-start.1 = ((bf16[8,8,400]{2,1,0:T(8,128)(2,1)}), bf16[8,8,400]{2,1,0:T(8,128)(2,1)S(1)}, u32[]{:S(2)}, u32[]{:S(2)}) async-start(bf16[8,8,400]{2,1,0:T(8,128)(2,1)} %broadcast_in_dim.2), calls=%async_computation.1 | async-start | bytes 131072 | tf_op jit(solution)/shard_map/all_to_all | solution.py:344
  68.7 0.7 copy-start.5
  68.7 0.7 copy-start.6
  68.8 0.8 %copy-start.7 = (bf16[400,256]{1,0:T(8,128)(2,1)}, bf16[400,256]{1,0:T(8,128)(2,1)S(1)}, u32[]{:S(2)}) copy-start(bf16[400,256]{1,0:T(8,128)(2,1)S(1)} %collective-permute-done.25.core_ref) | copy-start | bytes 614404
  76.5 0.6 copy-start.4

commit v3 on v2

--- a/solution.py
+++ b/solution.py
@@ -29,6 +29,8 @@
 RIM = D + RIM_INFO
 RIM_WIDTH = BND + B_ROWS
 
+LIMIT = 24 << 20
+
 BF = jnp.bfloat16
 F32 = jnp.float32
 DOM = ("x", "yh", "z")
@@ -50,6 +52,7 @@
         in_specs=[smem() if kind == "s" else vmem() for kind in ins],
         out_specs=[vmem() for _ in outs],
         out_shape=[jax.ShapeDtypeStruct(shape, dtype) for shape, dtype in outs],
+        compiler_params=pltpu.CompilerParams(vmem_limit_bytes=LIMIT),
     )(*args)
 
 
@@ -65,11 +68,6 @@
 def two(values):
     high = values.astype(BF)
     return high, (values - high.astype(F32)).astype(BF)
-
-
-def mm_two(a, b, dims):
-    high, low = two(a)
-    return mm(high, b, dims) + mm(low, b, dims)
 
 
 def hits(count, ids):
@@ -98,12 +96,28 @@
     return ones(hits(RELS, jnp.concatenate(spread, axis=1)))
 
 
-def weights(relw, chosen):
+def weights(relw, ids):
+    lane = lax.broadcasted_iota(jnp.int32, (RELS, TILE), 1)
+    row = lax.broadcasted_iota(jnp.int32, (RELS, TILE), 0)
+    chosen = jnp.zeros((RELS, TILE), F32)
+    for t, ident in enumerate(ids):
+        chosen = jnp.where((lane == t) & (row == ident), 1.0, chosen)
+    chosen = chosen.astype(BF)
     high = relw.astype(BF)
     rest = relw - high.astype(F32)
     middle = rest.astype(BF)
     low = (rest - middle.astype(F32)).astype(BF)
     return (mm(high, chosen, TN) + mm(middle, chosen, TN)) + mm(low, chosen, TN)
+
+
+def scaled(rows, columns):
+    return jnp.concatenate(
+        [
+            rows[:, t * TILE : (t + 1) * TILE] * columns[:, t : t + 1]
+            for t in range(rows.shape[1] // TILE)
+        ],
+        axis=1,
+    )
 
 
 def tile_ids(tile_ref, band_ref):
@@ -139,7 +153,7 @@
     pick = ones(hits(ROWS, bsrc_ref[...]))
     rows = mm(high, pick, NN) + mm(low, pick, NN)
     brows_ref[...] = rows
-    q = (rows * weights(relw_ref[...], relations(band_ids))).astype(BF)
+    q = scaled(rows, weights(relw_ref[...], band_ids)).astype(BF)
     info = stacked(RIM_INFO, RIM_WIDTH, [bdst_ref[...]])
     for ref in (up_ref, down_ref):
         ref[:D, BND:] = q
@@ -161,19 +175,18 @@
     rows = mm(high, pick, NN) + mm(low, pick, NN)
     rows_ref[...] = rows
     edge_ids, _ = tile_ids(tile_ref, band_ref)
-    q_ref[:, :E_ROWS] = (rows * weights(relw_ref[...], relations(edge_ids))).astype(BF)
+    q_ref[:, :E_ROWS] = scaled(rows, weights(relw_ref[...], edge_ids)).astype(BF)
     qb = own_up_ref[:D, BND:]
     q_ref[:, E_ROWS:] = qb
     near = jnp.concatenate([low_ref[:D, :BND], high_ref[:D, :BND]], axis=1)
-    first, second = two(pull(mm(near, qb, TN), hits(2 * BND, bdst_ref[...])))
-    dqb_ref[...] = mm(near, first, NN) + mm(near, second, NN)
+    dqb_ref[...] = mm(near, pull(mm(near, qb, TN), hits(2 * BND, bdst_ref[...])).astype(BF), NN)
     grads = []
     for got_ref, mine_ref, shift in ((low_ref, own_down_ref, BND), (high_ref, own_up_ref, 0)):
         qn = got_ref[:D, BND:]
         ids = got_ref[D:, :].astype(F32)[:1, :B_ROWS].astype(jnp.int32) - shift
-        first, second = two(pull(mm(mine_ref[:D, :BND], qn, TN), hits(BND, ids)))
-        grads.append(mm(qn, first, NT) + mm(qn, second, NT))
-    back_ref[...] = mm_two(jnp.concatenate(grads, axis=1), ones(hits(ROWS, bound_ref[...])), NT)
+        grads.append(mm(qn, pull(mm(mine_ref[:D, :BND], qn, TN), hits(BND, ids)).astype(BF), NT))
+    grads = jnp.concatenate(grads, axis=1).astype(BF)
+    back_ref[...] = mm(grads, ones(hits(ROWS, bound_ref[...])), NT)
 
 
 def coefficients(scores, dst, live, second):
@@ -184,7 +197,7 @@
     )
     dneg = (jax.nn.sigmoid(scores) * (valid / NEG)).astype(BF).astype(F32) * counts
     positive = pull(scores[:, :E_ROWS], hits(ROWS, dst)) * valid[:, :E_ROWS]
-    return two(jnp.concatenate([dneg[:, :E_ROWS] + positive, dneg[:, E_ROWS:]], axis=1))
+    return jnp.concatenate([dneg[:, :E_ROWS] + positive, dneg[:, E_ROWS:]], axis=1).astype(BF)
 
 
 def far_block(core_ref, got_ref, other_ref):
@@ -200,48 +213,43 @@
 ):
     far = far_block(core_ref, got_ref, other_ref)
     scores = mm(far, q_ref[...], TN)
-    high, low = coefficients(
+    coef = coefficients(
         scores, dst_ref[...], live_ref[0, 0], second_count(neg_ref).astype(F32)
     )
     edge_ids, band_ids = tile_ids(tile_ref, band_ref)
     chosen = relations(edge_ids + band_ids)
-    dq = mm(far, high, NN) + mm(far, low, NN)
+    dq = mm(far, coef, NN)
     dq_band = dq[:, E_ROWS:] + dqb_ref[...]
-    first, second = two(dq[:, :E_ROWS] * rows_ref[...])
-    third, fourth = two(dq_band * brows_ref[...])
-    gw = (mm(chosen[:, :E_ROWS], first, NT) + mm(chosen[:, :E_ROWS], second, NT)) + (
-        mm(chosen[:, E_ROWS:], third, NT) + mm(chosen[:, E_ROWS:], fourth, NT)
-    )
+    first = (dq[:, :E_ROWS] * rows_ref[...]).astype(BF)
+    second = (dq_band * brows_ref[...]).astype(BF)
+    gw = mm(chosen[:, :E_ROWS], first, NT) + mm(chosen[:, E_ROWS:], second, NT)
     gw = gw.astype(BF)
     for k in range(Z):
         gw_ref[k, :, :] = gw
-    step_ref[:, :E_ROWS] = dq[:, :E_ROWS]
-    step_ref[:, E_ROWS:] = dq_band
+    columns = weights(relw_ref[...], edge_ids + band_ids)
+    step_ref[:, :E_ROWS] = scaled(dq[:, :E_ROWS], columns).astype(BF)
+    step_ref[:, E_ROWS:] = scaled(dq_band, columns[:, E_TILES:A_TILES]).astype(BF)
 
 
 def partner_kernel(
-    core_ref, tile_ref, band_ref, got_ref, other_ref, emb_ref, relw_ref, step_ref, src_ref, bsrc_ref,
-    back_ref,
+    core_ref, got_ref, other_ref, emb_ref, relw_ref, step_ref, src_ref, bsrc_ref, back_ref,
     total_ref,
 ):
     far = far_block(core_ref, got_ref, other_ref)
     info = got_ref[D:, :].astype(F32)
     ids = jnp.concatenate([info[k : k + 1, :] for k in range(10)], axis=1).astype(jnp.int32)
     scalars = info[10:11, :]
-    relw = relw_ref[...]
-    chosen = relations([scalars[:, t : t + 1] for t in range(A_TILES)])
-    q = (mm(far, ones(hits(ROWS, ids[:, :A_ROWS])), NN) * weights(relw, chosen)).astype(BF)
+    columns = weights(relw_ref[...], [scalars[:, t : t + 1].astype(jnp.int32) for t in range(A_TILES)])
+    q = scaled(mm(far, ones(hits(ROWS, ids[:, :A_ROWS])), NN), columns).astype(BF)
     scores = mm(emb_ref[...].astype(BF), q, TN)
-    high, low = coefficients(
+    coef = coefficients(
         scores,
         ids[:, A_ROWS:],
         scalars[:, A_TILES : A_TILES + 1].astype(jnp.int32),
         scalars[:, A_TILES + 1 : A_TILES + 2],
     )
-    edge_ids, band_ids = tile_ids(tile_ref, band_ref)
-    steps = step_ref[...] * weights(relw, relations(edge_ids + band_ids))
     pick = jnp.concatenate([ones(hits(ROWS, src_ref[...])), ones(hits(ROWS, bsrc_ref[...]))], axis=1)
-    total = back_ref[...] + mm_two(steps, pick, NT) + mm(q, high, NT) + mm(q, low, NT)
+    total = back_ref[...] + mm(step_ref[...], pick, NT) + mm(q, coef, NT)
     total_ref[...] = total.astype(BF)
 
 
@@ -251,18 +259,6 @@
     fresh = state_ref[...] + jnp.sum(grad * grad, axis=0, keepdims=True) / D
     fresh_ref[...] = fresh
     new_ref[...] = emb_ref[...] - step_rate * grad / jnp.sqrt(fresh)
-
-
-def update_kernel(state_ref, gw_ref, relw_ref, new_ref):
-    gw = gw_ref[0, :, :].astype(F32)
-    for k in range(1, XY):
-        gw = gw + gw_ref[k, :, :].astype(F32)
-    row = lax.broadcasted_iota(jnp.int32, (RELS, 1), 0)
-    state = jnp.zeros((RELS, 1), F32)
-    for k in range(RELS):
-        state = jnp.where(row == k, state_ref[k], state)
-    fresh = state + jnp.sum(gw * gw, axis=1, keepdims=True) / D
-    new_ref[...] = relw_ref[...] - step_rate * gw / jnp.sqrt(fresh)
 
 
 def swap(axes, size, number, work):
@@ -318,16 +314,16 @@
     gw, step = call(
         relation_kernel,
         "sssssvvvvvvvv",
-        [((Z, RELS, D), BF), ((D, A_ROWS), F32)],
+        [((Z, RELS, D), BF), ((D, A_ROWS), BF)],
         core, tile_rel, band_rel, live_tiles, neg_tiles, got, other_half, q, rows, band_rows,
         dq_band, rel_weight, dst_rows,
     )
     gw = lax.all_to_all(gw, "z", split_axis=0, concat_axis=0, tiled=True)
     (total,) = call(
         partner_kernel,
-        "sssvvvvvvvv",
+        "svvvvvvvv",
         [((D, ROWS), BF)],
-        core, tile_rel, band_rel, got, other_half, emb_t, rel_weight, step, src_rows,
+        core, got, other_half, emb_t, rel_weight, step, src_rows,
         band_src, back,
     )
     from_cross = trade(total, 3)
@@ -342,7 +338,8 @@
     gw = jnp.sum(gw.astype(F32), axis=0).astype(BF)
     gw = jnp.broadcast_to(gw[None], (XY, RELS, D))
     gw = lax.all_to_all(gw, ("x", "yh"), split_axis=0, concat_axis=0, tiled=True)
-    (rel_new,) = call(update_kernel, "svv", [((RELS, D), F32)], rel_state, gw, rel_weight)
+    gw = jnp.sum(gw.astype(F32), axis=0)
+    rel_new = rel_weight - step_rate * gw / jnp.sqrt(rel_state + jnp.mean(gw * gw, axis=1))[:, None]
     return (new_t.T, fresh.reshape(ROWS), rel_new)
 
 

time: 79.2 us -> 79.2 us (level)
  Pallas kernels: 18.1 us -> 11.3 us
  waiting for transfers between devices: 13.4 us -> 17.3 us
  local copies, waits for them, and re-layouts: 2.73 us -> 4.46 us
  other arithmetic: 0.03 us -> 0.86 us
    pallas_call x6 -> x5, Pallas kernels: 18.1 us -> 11.3 us  [call(): pl.pallas_call(kernel, in_specs=[smem() if kind == 's' else vmem() for ki...]
    all_to_all x1, waiting for transfers between devices: 1.01 us -> 3.46 us  [body(): gw = lax.all_to_all(gw, 'z', split_axis=0, concat_axis=0, tiled=True)]
    all_to_all x1, waiting for transfers between devices: 4.71 us -> 6.1 us  [body(): lax.all_to_all(gw, ('x', 'yh'), split_axis=0, concat_axis=0, tiled=True)]
    unnamed x26 -> x32, local copies, waits for them, and re-layouts: 2.09 us -> 3.19 us
  transfers between devices with their start and end apart: 9 -> 9, of which waited for: 4 -> 4; matrix products, arithmetic and copies ran while one was open for 1% -> 2% of each run, Pallas kernels for 10% -> 5%
where the time goes in v3:
time: 79.2 us; the launch traced here: 78.6 us
  starting transfers between devices  42.4 us (54%)
  waiting for transfers between devices  17.3 us (22%)
  Pallas kernels  11.3 us (14%)
  local copies, waits for them, and re-layouts  4.46 us (6%)
  between operations  2.18 us (3%)
  other arithmetic  0.86 us (1%)
    all_to_all x1, starting transfers between devices, body(): gw = lax.all_to_all(gw, 'z', split_axis=0, concat_axis=0, tiled=True)  15.1 us
    pallas_call x5, Pallas kernels, call(): pl.pallas_call(kernel, in_specs=[smem() if kind == 's' else vmem() for ki...  11.3 us
    ppermute x4, starting transfers between devices, trade(): return lax.ppermute(values, 'rel', [(i, i ^ bit) for i in range(N_REL)])  9.67 us
    all_to_all x1, starting transfers between devices, body(): lax.all_to_all(gw, ('x', 'yh'), split_axis=0, concat_axis=0, tiled=True)  6.93 us
    ppermute x1, waiting for transfers between devices, run(): moved = lax.ppermute(moved, axes, [(i, i ^ k) for i in range(size)])  6.44 us
    all_to_all x1, waiting for transfers between devices, body(): lax.all_to_all(gw, ('x', 'yh'), split_axis=0, concat_axis=0, tiled=True)  6.1 us
    ppermute x1, starting transfers between devices, body(): lax.ppermute(to_down, DOM, [(i + 1, i) for i in range(count - 1)])  4.85 us
    ppermute x1, starting transfers between devices, body(): from_low = lax.ppermute(to_up, DOM, [(i, i + 1) for i in range(count - 1)])  3.82 us
  transfers between devices with their start and end apart: 9, of which 4 were waited for; matrix products, arithmetic and copies ran while one was open for 2% of the time, Pallas kernels for 5%

profile of v3, /device:TPU:32, one launch (start us, length us, event | category | flops | bytes accessed | tf_op | source)
XLA Modules:
  0.0 78.6 jit_solution(1540708449704100097)
XLA Ops:
  1.4 0.6 copy-done.7
  2.0 0.0 copy-done.8
  2.0 0.0 copy-done.6
  2.0 0.0 copy-done
  2.1 1.8 %shard_map.157 = (bf16[416,128]{1,0:T(8,128)(2,1)}, bf16[408,384]{1,0:T(8,128)(2,1)S(1)}, bf16[408,384]{1,0:T(8,128)(2,1)S(1)}, f32[400,256]{1,0:T(8,128)S(1)}) custom-call(s32[1]{0:T(128)} %bitcast.core_ref, s32[1,4]{1,0:T(1,128)S(1)} %copy-done.9, s32[1,2]{1,0:T(1,128)S(1)} %copy-done.12, s32[1,1]{1,0:T(1,128)S(6)} %copy.74.live_ref, ...), custom_call_target="tpu_custom_call" | custom-call | tf_op jit(solution)/shard_map/pallas_call | solution.py:50
  3.8 3.8 %collective-permute-start.22 = (bf16[408,384]{1,0:T(8,128)(2,1)S(1)}, bf16[408,384]{1,0:T(8,128)(2,1)S(1)}, u32[]{:S(2)}, u32[]{:S(2)}) collective-permute-start(bf16[408,384]{1,0:T(8,128)(2,1)S(1)} %get-tuple-element.369), channel_id=1, source_target_pairs={{0,4},{4,8},{8,12},{12,16},{16,20},{20,24},{24,28},{28,32},{32,36}... | collective-permute-start | bytes 940040 | tf_op jit(solution)/shard_map/ppermute | solution.py:296
  7.7 4.8 %collective-permute-start.23 = (bf16[408,384]{1,0:T(8,128)(2,1)S(1)}, bf16[408,384]{1,0:T(8,128)(2,1)S(1)}, u32[]{:S(2)}, u32[]{:S(2)}) collective-permute-start(bf16[408,384]{1,0:T(8,128)(2,1)S(1)} %get-tuple-element.370), channel_id=1, source_target_pairs={{4,0},{8,4},{12,8},{16,12},{20,16},{24,20},{28,24},{32,28},{36,32}... | collective-permute-start | bytes 940040 | tf_op jit(solution)/shard_map/ppermute | solution.py:297
  13.2 9.2 %conditional.2 = (bf16[416,128]{1,0:T(8,128)(2,1)}) conditional(s32[]{:T(128)} %bitcast.4, bf16[416,128]{1,0:T(8,128)(2,1)} %get-tuple-element.371, bf16[416,128]{1,0:T(8,128)(2,1)} %get-tuple-element.371, bf16[416,128]{1,0:T(8,128)(2,1)} %get-tuple-element.371, bf16[416,128]{1,0:T(8,128)(2,1)} %get-tuple-element.371, ...), branch_computations={%region_0.0_spmd, %region_1.0_spmd, %region_2.0_spmd, %region_3.0_... | conditional | bytes 639024 | solution.py:273
  13.2 2.1 %collective-permute-start.2 = (bf16[416,128]{1,0:T(8,128)(2,1)}, bf16[416,128]{1,0:T(8,128)(2,1)S(1)}, u32[]{:S(2)}, u32[]{:S(2)}) collective-permute-start(bf16[416,128]{1,0:T(8,128)(2,1)} %param.3), channel_id=1, source_target_pairs={{0,12},{4,8},{8,4},{12,0},{16,28},{20,24},{24,20},{28,16},{32,44},... | collective-permute-start | bytes 319496 | tf_op jit(solution)/shard_map/cond/branch_3_fun/ppermute | solution.py:268
  15.3 6.4 %collective-permute-done.2 = bf16[416,128]{1,0:T(8,128)(2,1)S(1)} collective-permute-done((bf16[416,128]{1,0:T(8,128)(2,1)}, bf16[416,128]{1,0:T(8,128)(2,1)S(1)}, u32[]{:S(2)}, u32[]{:S(2)}) %collective-permute-start.2) | collective-permute-done | bytes 106528 | tf_op jit(solution)/shard_map/cond/branch_3_fun/ppermute | solution.py:268
  21.7 0.6 copy.20
  22.4 0.6 copy-done.10
  23.0 2.6 %conditional.3 = (bf16[416,128]{1,0:T(8,128)(2,1)}, bf16[400,768]{1,0:T(8,128)(2,1)S(1)}, f32[400,512]{1,0:T(8,128)S(1)}, f32[400,256]{1,0:T(8,128)S(1)}, f32[400,256]{1,0:T(8,128)}) conditional(s32[]{:T(128)} %bitcast.1, (s32[1,4]{1,0:T(1,128)S(1)}, s32[1,2]{1,0:T(1,128)S(1)}, f32[400,256]{1,0:T(8,128)S(1)}, ...), branch_computations={%region_16.0_spmd, %region_17.0_spmd, %region_18.0_spmd, %region_1... | conditional | bytes 639056 | solution.py:273
  23.0 2.6 %branch_0_fun.1 = (bf16[400,768]{1,0:T(8,128)(2,1)S(1)}, f32[400,512]{1,0:T(8,128)S(1)}, f32[400,256]{1,0:T(8,128)S(1)}, f32[400,256]{1,0:T(8,128)}) custom-call(s32[1,4]{1,0:T(1,128)S(1)} %get-tuple-element.226.tile_ref, s32[1,2]{1,0:T(1,128)S(1)} %get-tuple-element.227.band_ref, f32[400,256]{1,0:T(8,128)S(1)} %get-tuple-element.228.emb_ref, ...), custom_call_target="tpu_custom_call" | custom-call | tf_op jit(solution)/shard_map/cond/branch_0_fun/pallas_call | solution.py:50
  25.6 2.1 %collective-permute-start.24 = (bf16[416,128]{1,0:T(8,128)(2,1)}, bf16[416,128]{1,0:T(8,128)(2,1)S(1)}, u32[]{:S(2)}, u32[]{:S(2)}) collective-permute-start(bf16[416,128]{1,0:T(8,128)(2,1)} %get-tuple-element.372.got_ref), channel_id=1, source_target_pairs={{0,1},{1,0},{2,3},{3,2},{4,5},{5,4},{6,7},{7,6},{8,9},{9,8},{10,11... | collective-permute-start | bytes 319496 | tf_op jit(solution)/shard_map/ppermute | solution.py:277
  27.7 1.3 %collective-permute-done.24.other_ref = bf16[416,128]{1,0:T(8,128)(2,1)S(1)} collective-permute-done((bf16[416,128]{1,0:T(8,128)(2,1)}, bf16[416,128]{1,0:T(8,128)(2,1)S(1)}, u32[]{:S(2)}, u32[]{:S(2)}) %collective-permute-start.24) | collective-permute-done | bytes 106528 | tf_op jit(solution)/shard_map/ppermute | solution.py:277
  29.0 0.7 copy-done.11
  29.7 3.2 %shard_map.158 = (bf16[16,8,400]{2,1,0:T(8,128)(2,1)}, bf16[400,768]{1,0:T(8,128)(2,1)S(1)}) custom-call(s32[1]{0:T(128)} %bitcast.core_ref, s32[1,4]{1,0:T(1,128)S(1)} %copy-done.11, s32[1,2]{1,0:T(1,128)S(1)} %copy-done.14, s32[1,1]{1,0:T(1,128)S(6)} %copy.74.live_ref, s32[1,8]{1,0:T(1,128)S(1)} %copy-done.2, bf16[416,128]{1,0:T(8,128)(2,1)} %get-tuple-element.372.got_ref, ...), custom_call_target="tpu_custom_call" | custom-call | tf_op jit(solution)/shard_map/pallas_call | solution.py:50
  32.9 15.1 %all-to-all-start = ((bf16[16,8,400]{2,1,0:T(8,128)(2,1)}), bf16[16,8,400]{2,1,0:T(8,128)(2,1)S(1)}, u32[]{:S(2)}, u32[]{:S(2)}) async-start(bf16[16,8,400]{2,1,0:T(8,128)(2,1)} %get-tuple-element.381), calls=%async_computation | async-start | bytes 262144 | tf_op jit(solution)/shard_map/all_to_all | solution.py:321
  48.0 2.8 %shard_map.159.own_ref = bf16[400,256]{1,0:T(8,128)(2,1)S(1)} custom-call(s32[1]{0:T(128)} %bitcast.core_ref, bf16[416,128]{1,0:T(8,128)(2,1)} %get-tuple-element.372.got_ref, bf16[416,128]{1,0:T(8,128)(2,1)S(1)} %collective-permute-done.24.other_ref, f32[400,256]{1,0:T(8,128)S(1)} %bitcast.18, f32[8,400]{1,0:T(8,128)S(1)} %copy-done.5, ...), custom_call_target="tpu_custom_call" | custom-call | tf_op jit(solution)/shard_map/pallas_call | solution.py:50
  50.8 2.7 %collective-permute-start.27 = (bf16[400,256]{1,0:T(8,128)(2,1)S(1)}, bf16[400,256]{1,0:T(8,128)(2,1)S(1)}, u32[]{:S(2)}, u32[]{:S(2)}) collective-permute-start(bf16[400,256]{1,0:T(8,128)(2,1)S(1)} %shard_map.159.own_ref), channel_id=1, source_target_pairs={{0,3},{1,2},{2,1},{3,0},{4,7},{5,6},{6,5},{7,4},{8,11},{9,10},{10,... | collective-permute-start | bytes 614408 | tf_op jit(solution)/shard_map/ppermute | solution.py:277
  53.5 2.7 %collective-permute-start.26 = (bf16[400,256]{1,0:T(8,128)(2,1)S(1)}, bf16[400,256]{1,0:T(8,128)(2,1)S(1)}, u32[]{:S(2)}, u32[]{:S(2)}) collective-permute-start(bf16[400,256]{1,0:T(8,128)(2,1)S(1)} %shard_map.159.own_ref), channel_id=1, source_target_pairs={{0,2},{1,3},{2,0},{3,1},{4,6},{5,7},{6,4},{7,5},{8,10},{9,11},{10,... | collective-permute-start | bytes 614408 | tf_op jit(solution)/shard_map/ppermute | solution.py:277
  56.2 2.2 %collective-permute-start.25 = (bf16[400,256]{1,0:T(8,128)(2,1)S(1)}, bf16[400,256]{1,0:T(8,128)(2,1)S(1)}, u32[]{:S(2)}, u32[]{:S(2)}) collective-permute-start(bf16[400,256]{1,0:T(8,128)(2,1)S(1)} %shard_map.159.own_ref), channel_id=1, source_target_pairs={{0,1},{1,0},{2,3},{3,2},{4,5},{5,4},{6,7},{7,6},{8,9},{9,8},{10,11... | collective-permute-start | bytes 614408 | tf_op jit(solution)/shard_map/ppermute | solution.py:277
  58.4 3.5 %all-to-all-done = bf16[16,8,400]{2,1,0:T(8,128)(2,1)S(1)} async-done(((bf16[16,8,400]{2,1,0:T(8,128)(2,1)}), bf16[16,8,400]{2,1,0:T(8,128)(2,1)S(1)}, u32[]{:S(2)}, u32[]{:S(2)}) %all-to-all-start) | async-done | bytes 102432 | tf_op jit(solution)/shard_map/all_to_all | solution.py:321
  61.9 0.6 broadcast_in_dim.2
  62.6 6.9 %all-to-all-start.1 = ((bf16[8,8,400]{2,1,0:T(8,128)(2,1)}), bf16[8,8,400]{2,1,0:T(8,128)(2,1)S(1)}, u32[]{:S(2)}, u32[]{:S(2)}) async-start(bf16[8,8,400]{2,1,0:T(8,128)(2,1)} %broadcast_in_dim.2), calls=%async_computation.1 | async-start | bytes 131072 | tf_op jit(solution)/shard_map/all_to_all | solution.py:340
  69.5 0.6 copy-done.3
  70.2 1.0 %shard_map.160 = (f32[400,256]{1,0:T(8,128)}, f32[1,256]{1,0:T(1,128)}) custom-call(bf16[400,256]{1,0:T(8,128)(2,1)S(1)} %shard_map.159.own_ref, bf16[400,256]{1,0:T(8,128)(2,1)S(1)} %collective-permute-done.25.core_ref, bf16[400,256]{1,0:T(8,128)(2,1)S(1)} %collective-permute-done.26.far_ref, bf16[400,256]{1,0:T(8,128)(2,1)S(1)} %collective-permute-done.27.cross_ref, ...), custom_call_target="tpu_custom_call" | custom-call | tf_op jit(solution)/shard_map/pallas_call | solution.py:50
  71.2 6.1 %all-to-all-done.1 = bf16[8,8,400]{2,1,0:T(8,128)(2,1)S(1)} async-done(((bf16[8,8,400]{2,1,0:T(8,128)(2,1)}), bf16[8,8,400]{2,1,0:T(8,128)(2,1)S(1)}, u32[]{:S(2)}, u32[]{:S(2)}) %all-to-all-start.1) | async-done | bytes 51232 | tf_op jit(solution)/shard_map/all_to_all | solution.py:340
  77.3 0.1 multiply_reduce_fusion
  77.4 0.5 copy-done.15
  77.9 0.7 divide_subtract_fusion
  (32 shorter events, 0.2 us)
Async XLA Ops:
  0.6 0.8 copy-start.9
  0.6 0.7 copy-start.12
  1.3 0.7 copy-start.7
  1.3 0.7 copy-start.8
  1.3 0.7 copy-start.6
  1.4 0.7 copy-start
  1.4 0.7 copy-start.1
  1.4 0.7 copy-start.2
  3.8 18.5 %collective-permute-start.22 = (bf16[408,384]{1,0:T(8,128)(2,1)S(1)}, bf16[408,384]{1,0:T(8,128)(2,1)S(1)}, u32[]{:S(2)}, u32[]{:S(2)}) collective-permute-start(bf16[408,384]{1,0:T(8,128)(2,1)S(1)} %get-tuple-element.369), channel_id=1, source_target_pairs={{0,4},{4,8},{8,12},{12,16},{16,20},{20,24},{24,28},{28,32},{32,36}... | collective-permute-start | bytes 940040 | tf_op jit(solution)/shard_map/ppermute | solution.py:296
  7.7 14.7 %collective-permute-start.23 = (bf16[408,384]{1,0:T(8,128)(2,1)S(1)}, bf16[408,384]{1,0:T(8,128)(2,1)S(1)}, u32[]{:S(2)}, u32[]{:S(2)}) collective-permute-start(bf16[408,384]{1,0:T(8,128)(2,1)S(1)} %get-tuple-element.370), channel_id=1, source_target_pairs={{4,0},{8,4},{12,8},{16,12},{20,16},{24,20},{28,24},{32,28},{36,32}... | collective-permute-start | bytes 940040 | tf_op jit(solution)/shard_map/ppermute | solution.py:297
  13.2 9.2 %copy-start.4 = (f32[256,400]{0,1:T(8,128)S(1)}, f32[256,400]{0,1:T(8,128)}, u32[]{:S(2)}) copy-start(f32[256,400]{0,1:T(8,128)} %param.38) | copy-start | bytes 1228804
  13.2 9.2 %copy-start.5 = (f32[8,400]{1,0:T(8,128)S(1)}, f32[8,400]{1,0:T(8,128)}, u32[]{:S(2)}) copy-start(f32[8,400]{1,0:T(8,128)} %relw_ref.5) | copy-start | bytes 38404
  13.2 8.5 %collective-permute-start.2 = (bf16[416,128]{1,0:T(8,128)(2,1)}, bf16[416,128]{1,0:T(8,128)(2,1)S(1)}, u32[]{:S(2)}, u32[]{:S(2)}) collective-permute-start(bf16[416,128]{1,0:T(8,128)(2,1)} %param.3), channel_id=1, source_target_pairs={{0,12},{4,8},{8,4},{12,0},{16,28},{20,24},{24,20},{28,16},{32,44},... | collective-permute-start | bytes 319496 | tf_op jit(solution)/shard_map/cond/branch_3_fun/ppermute | solution.py:268
  22.4 0.7 copy-start.10
  22.4 0.7 copy-start.13
  25.6 3.4 %collective-permute-start.24 = (bf16[416,128]{1,0:T(8,128)(2,1)}, bf16[416,128]{1,0:T(8,128)(2,1)S(1)}, u32[]{:S(2)}, u32[]{:S(2)}) collective-permute-start(bf16[416,128]{1,0:T(8,128)(2,1)} %get-tuple-element.372.got_ref), channel_id=1, source_target_pairs={{0,1},{1,0},{2,3},{3,2},{4,5},{5,4},{6,7},{7,6},{8,9},{9,8},{10,11... | collective-permute-start | bytes 319496 | tf_op jit(solution)/shard_map/ppermute | solution.py:277
  29.0 0.7 copy-start.11
  29.0 0.7 copy-start.14
  32.9 29.0 %all-to-all-start = ((bf16[16,8,400]{2,1,0:T(8,128)(2,1)}), bf16[16,8,400]{2,1,0:T(8,128)(2,1)S(1)}, u32[]{:S(2)}, u32[]{:S(2)}) async-start(bf16[16,8,400]{2,1,0:T(8,128)(2,1)} %get-tuple-element.381), calls=%async_computation | async-start | bytes 262144 | tf_op jit(solution)/shard_map/all_to_all | solution.py:321
  50.8 18.7 %collective-permute-start.27 = (bf16[400,256]{1,0:T(8,128)(2,1)S(1)}, bf16[400,256]{1,0:T(8,128)(2,1)S(1)}, u32[]{:S(2)}, u32[]{:S(2)}) collective-permute-start(bf16[400,256]{1,0:T(8,128)(2,1)S(1)} %shard_map.159.own_ref), channel_id=1, source_target_pairs={{0,3},{1,2},{2,1},{3,0},{4,7},{5,6},{6,5},{7,4},{8,11},{9,10},{10,... | collective-permute-start | bytes 614408 | tf_op jit(solution)/shard_map/ppermute | solution.py:277
  53.5 16.0 %collective-permute-start.26 = (bf16[400,256]{1,0:T(8,128)(2,1)S(1)}, bf16[400,256]{1,0:T(8,128)(2,1)S(1)}, u32[]{:S(2)}, u32[]{:S(2)}) collective-permute-start(bf16[400,256]{1,0:T(8,128)(2,1)S(1)} %shard_map.159.own_ref), channel_id=1, source_target_pairs={{0,2},{1,3},{2,0},{3,1},{4,6},{5,7},{6,4},{7,5},{8,10},{9,11},{10,... | collective-permute-start | bytes 614408 | tf_op jit(solution)/shard_map/ppermute | solution.py:277
  56.2 13.3 %collective-permute-start.25 = (bf16[400,256]{1,0:T(8,128)(2,1)S(1)}, bf16[400,256]{1,0:T(8,128)(2,1)S(1)}, u32[]{:S(2)}, u32[]{:S(2)}) collective-permute-start(bf16[400,256]{1,0:T(8,128)(2,1)S(1)} %shard_map.159.own_ref), channel_id=1, source_target_pairs={{0,1},{1,0},{2,3},{3,2},{4,5},{5,4},{6,7},{7,6},{8,9},{9,8},{10,11... | collective-permute-start | bytes 614408 | tf_op jit(solution)/shard_map/ppermute | solution.py:277
  62.6 14.7 %all-to-all-start.1 = ((bf16[8,8,400]{2,1,0:T(8,128)(2,1)}), bf16[8,8,400]{2,1,0:T(8,128)(2,1)S(1)}, u32[]{:S(2)}, u32[]{:S(2)}) async-start(bf16[8,8,400]{2,1,0:T(8,128)(2,1)} %broadcast_in_dim.2), calls=%async_computation.1 | async-start | bytes 131072 | tf_op jit(solution)/shard_map/all_to_all | solution.py:340
  69.5 0.7 copy-start.3
  77.3 0.7 copy-start.15

commit v4 on v3

--- a/solution.py
+++ b/solution.py
@@ -33,9 +33,12 @@
 
 BF = jnp.bfloat16
 F32 = jnp.float32
-DOM = ("x", "yh", "z")
+XY = ("x", "yh")
+ZZ = ("zh", "zl")
+DOM = (*XY, *ZZ)
 Z = 16
-XY = 8
+FIRST = 8
+SECOND = 16
 
 
 def vmem():
@@ -120,29 +123,35 @@
     )
 
 
-def tile_ids(tile_ref, band_ref):
-    return [tile_ref[0, t] for t in range(E_TILES)], [band_ref[0, t] for t in range(B_TILES)]
-
-
-def second_count(neg_ref):
+def number(info, k):
+    return info[:, k : k + 1].astype(jnp.int32)
+
+
+def tile_numbers(info):
+    return [number(info, k) for k in range(A_TILES)]
+
+
+def same_order(core, own, other):
+    first = core == 0
+    return jnp.concatenate([jnp.where(first, own, other), jnp.where(first, other, own)], axis=1)
+
+
+def start_kernel(
+    core_ref, tile_ref, band_ref, live_ref, neg_ref, emb_ref, relw_ref, src_ref, dst_ref, bsrc_ref,
+    bdst_ref, bound_ref,
+    part_ref, up_ref, down_ref, brows_ref, info_ref,
+):
+    high, low = two(emb_ref[...])
+    part_ref[:D, :] = jnp.where(core_ref[0] == 0, high[:, :HALF], high[:, HALF:])
+    numbers = [tile_ref[0, t] for t in range(E_TILES)] + [band_ref[0, t] for t in range(B_TILES)]
     second = neg_ref[0, 0]
     for t in range(1, NEG_TILES):
         second = second + neg_ref[0, t]
-    return second
-
-
-def start_kernel(
-    core_ref, tile_ref, band_ref, live_ref, neg_ref, emb_ref, relw_ref, src_ref, dst_ref, bsrc_ref,
-    bdst_ref, bound_ref,
-    part_ref, up_ref, down_ref, brows_ref,
-):
-    high, low = two(emb_ref[...])
-    part_ref[:D, :] = jnp.where(core_ref[0] == 0, high[:, :HALF], high[:, HALF:])
-    edge_ids, band_ids = tile_ids(tile_ref, band_ref)
     lane = lax.broadcasted_iota(jnp.int32, (1, TILE), 1)
     scalars = jnp.zeros((1, TILE), F32)
-    for k, number in enumerate([*edge_ids, *band_ids, live_ref[0, 0], second_count(neg_ref)]):
-        scalars = jnp.where(lane == k, number.astype(F32), scalars)
+    for k, value in enumerate([*numbers, live_ref[0, 0], second, core_ref[0]]):
+        scalars = jnp.where(lane == k, value.astype(F32), scalars)
+    info_ref[...] = jnp.broadcast_to(scalars, (RELS, TILE))
     lists = []
     for ref in (src_ref, bsrc_ref, dst_ref):
         lists += [ref[:, k : k + TILE] for k in range(0, ref.shape[1], TILE)]
@@ -153,7 +162,7 @@
     pick = ones(hits(ROWS, bsrc_ref[...]))
     rows = mm(high, pick, NN) + mm(low, pick, NN)
     brows_ref[...] = rows
-    q = scaled(rows, weights(relw_ref[...], band_ids)).astype(BF)
+    q = scaled(rows, weights(relw_ref[...], numbers[E_TILES:])).astype(BF)
     info = stacked(RIM_INFO, RIM_WIDTH, [bdst_ref[...]])
     for ref in (up_ref, down_ref):
         ref[:D, BND:] = q
@@ -166,27 +175,30 @@
 
 
 def source_kernel(
-    tile_ref, band_ref, emb_ref, relw_ref, src_ref, bdst_ref, bound_ref, own_up_ref, own_down_ref,
-    low_ref, high_ref,
+    info_ref, emb_ref, relw_ref, src_ref, bdst_ref, bound_ref, own_up_ref, own_down_ref, low_ref,
+    high_ref,
     q_ref, rows_ref, dqb_ref, back_ref,
 ):
     high, low = two(emb_ref[...])
     pick = ones(hits(ROWS, src_ref[...]))
     rows = mm(high, pick, NN) + mm(low, pick, NN)
     rows_ref[...] = rows
-    edge_ids, _ = tile_ids(tile_ref, band_ref)
-    q_ref[:, :E_ROWS] = scaled(rows, weights(relw_ref[...], edge_ids)).astype(BF)
+    columns = weights(relw_ref[...], tile_numbers(info_ref[:1, :]))
+    q_ref[:, :E_ROWS] = scaled(rows, columns).astype(BF)
     qb = own_up_ref[:D, BND:]
     q_ref[:, E_ROWS:] = qb
     near = jnp.concatenate([low_ref[:D, :BND], high_ref[:D, :BND]], axis=1)
-    dqb_ref[...] = mm(near, pull(mm(near, qb, TN), hits(2 * BND, bdst_ref[...])).astype(BF), NN)
+    first, second = two(pull(mm(near, qb, TN), hits(2 * BND, bdst_ref[...])))
+    dqb_ref[...] = mm(near, first, NN) + mm(near, second, NN)
     grads = []
     for got_ref, mine_ref, shift in ((low_ref, own_down_ref, BND), (high_ref, own_up_ref, 0)):
         qn = got_ref[:D, BND:]
         ids = got_ref[D:, :].astype(F32)[:1, :B_ROWS].astype(jnp.int32) - shift
-        grads.append(mm(qn, pull(mm(mine_ref[:D, :BND], qn, TN), hits(BND, ids)).astype(BF), NT))
-    grads = jnp.concatenate(grads, axis=1).astype(BF)
-    back_ref[...] = mm(grads, ones(hits(ROWS, bound_ref[...])), NT)
+        first, second = two(pull(mm(mine_ref[:D, :BND], qn, TN), hits(BND, ids)))
+        grads.append(mm(qn, first, NT) + mm(qn, second, NT))
+    first, second = two(jnp.concatenate(grads, axis=1))
+    pick = ones(hits(ROWS, bound_ref[...]))
+    back_ref[...] = mm(first, pick, NT) + mm(second, pick, NT)
 
 
 def coefficients(scores, dst, live, second):
@@ -197,59 +209,54 @@
     )
     dneg = (jax.nn.sigmoid(scores) * (valid / NEG)).astype(BF).astype(F32) * counts
     positive = pull(scores[:, :E_ROWS], hits(ROWS, dst)) * valid[:, :E_ROWS]
-    return jnp.concatenate([dneg[:, :E_ROWS] + positive, dneg[:, E_ROWS:]], axis=1).astype(BF)
-
-
-def far_block(core_ref, got_ref, other_ref):
-    got, other = got_ref[:D, :], other_ref[:D, :]
-    first = core_ref[0] == 0
-    return jnp.concatenate([jnp.where(first, got, other), jnp.where(first, other, got)], axis=1)
+    high, low = two(dneg[:, :E_ROWS] + positive)
+    return jnp.concatenate([high, dneg[:, E_ROWS:].astype(BF)], axis=1), low
 
 
 def relation_kernel(
-    core_ref, tile_ref, band_ref, live_ref, neg_ref, got_ref, other_ref, q_ref, rows_ref, brows_ref,
-    dqb_ref, relw_ref, dst_ref,
+    info_ref, got_ref, other_ref, q_ref, rows_ref, brows_ref, dqb_ref, relw_ref, dst_ref,
     gw_ref, step_ref,
 ):
-    far = far_block(core_ref, got_ref, other_ref)
+    info = info_ref[:1, :]
+    ids = tile_numbers(info)
+    far = same_order(number(info, A_TILES + 2), got_ref[:D, :], other_ref[:D, :])
     scores = mm(far, q_ref[...], TN)
-    coef = coefficients(
-        scores, dst_ref[...], live_ref[0, 0], second_count(neg_ref).astype(F32)
-    )
-    edge_ids, band_ids = tile_ids(tile_ref, band_ref)
-    chosen = relations(edge_ids + band_ids)
+    coef, rest = coefficients(
+        scores, dst_ref[...], number(info, A_TILES), info[:, A_TILES + 1 : A_TILES + 2]
+    )
+    chosen = relations(ids)
     dq = mm(far, coef, NN)
+    dq_edge = dq[:, :E_ROWS] + mm(far, rest, NN)
     dq_band = dq[:, E_ROWS:] + dqb_ref[...]
-    first = (dq[:, :E_ROWS] * rows_ref[...]).astype(BF)
+    first = (dq_edge * rows_ref[...]).astype(BF)
     second = (dq_band * brows_ref[...]).astype(BF)
     gw = mm(chosen[:, :E_ROWS], first, NT) + mm(chosen[:, E_ROWS:], second, NT)
     gw = gw.astype(BF)
-    for k in range(Z):
+    for k in range(FIRST):
         gw_ref[k, :, :] = gw
-    columns = weights(relw_ref[...], edge_ids + band_ids)
-    step_ref[:, :E_ROWS] = scaled(dq[:, :E_ROWS], columns).astype(BF)
+    columns = weights(relw_ref[...], ids)
+    step_ref[:, :E_ROWS] = scaled(dq_edge, columns).astype(BF)
     step_ref[:, E_ROWS:] = scaled(dq_band, columns[:, E_TILES:A_TILES]).astype(BF)
 
 
 def partner_kernel(
-    core_ref, got_ref, other_ref, emb_ref, relw_ref, step_ref, src_ref, bsrc_ref, back_ref,
+    info_ref, got_ref, other_ref, emb_ref, relw_ref, step_ref, src_ref, bsrc_ref, back_ref,
     total_ref,
 ):
-    far = far_block(core_ref, got_ref, other_ref)
+    core = number(info_ref[:1, :], A_TILES + 2)
+    far = same_order(core, got_ref[:D, :], other_ref[:D, :])
     info = got_ref[D:, :].astype(F32)
     ids = jnp.concatenate([info[k : k + 1, :] for k in range(10)], axis=1).astype(jnp.int32)
     scalars = info[10:11, :]
-    columns = weights(relw_ref[...], [scalars[:, t : t + 1].astype(jnp.int32) for t in range(A_TILES)])
+    columns = weights(relw_ref[...], tile_numbers(scalars))
     q = scaled(mm(far, ones(hits(ROWS, ids[:, :A_ROWS])), NN), columns).astype(BF)
     scores = mm(emb_ref[...].astype(BF), q, TN)
-    coef = coefficients(
-        scores,
-        ids[:, A_ROWS:],
-        scalars[:, A_TILES : A_TILES + 1].astype(jnp.int32),
-        scalars[:, A_TILES + 1 : A_TILES + 2],
+    coef, rest = coefficients(
+        scores, ids[:, A_ROWS:], number(scalars, A_TILES), scalars[:, A_TILES + 1 : A_TILES + 2]
     )
     pick = jnp.concatenate([ones(hits(ROWS, src_ref[...])), ones(hits(ROWS, bsrc_ref[...]))], axis=1)
     total = back_ref[...] + mm(step_ref[...], pick, NT) + mm(q, coef, NT)
+    total = total + mm(q[:, :E_ROWS], rest, NT)
     total_ref[...] = total.astype(BF)
 
 
@@ -286,44 +293,48 @@
     core = lax.bitwise_and(lax.axis_index("rel").astype(jnp.int32), 1).reshape(1)
     count = lax.axis_size(DOM)
     emb_t = emb.T
-    part, to_up, to_down, band_rows = call(
+    part, to_up, to_down, band_rows, info = call(
         start_kernel,
         "sssssvvvvvvv",
-        [((SENT, HALF), BF), ((RIM, RIM_WIDTH), BF), ((RIM, RIM_WIDTH), BF), ((D, B_ROWS), F32)],
+        [
+            ((SENT, HALF), BF),
+            ((RIM, RIM_WIDTH), BF),
+            ((RIM, RIM_WIDTH), BF),
+            ((D, B_ROWS), F32),
+            ((RELS, TILE), F32),
+        ],
         core, tile_rel, band_rel, live_tiles, neg_tiles, emb_t, rel_weight, src_rows, dst_rows,
         band_src, band_dst, bound,
     )
     from_low = lax.ppermute(to_up, DOM, [(i, i + 1) for i in range(count - 1)])
     from_high = lax.ppermute(to_down, DOM, [(i + 1, i) for i in range(count - 1)])
-    (got,) = swap("z", Z, lax.bitwise_and(mask, 15), lambda: ())(part)
+    (got,) = swap(ZZ, Z, lax.bitwise_and(mask, 15), lambda: ())(part)
 
     def sources(*args):
         return call(
             source_kernel,
-            "ssvvvvvvvvv",
+            "vvvvvvvvvv",
             [((D, A_ROWS), BF), ((D, E_ROWS), F32), ((D, B_ROWS), F32), ((D, ROWS), F32)],
             *args,
         )
 
-    along_xy = swap(("x", "yh"), XY, lax.shift_right_logical(mask, 4), sources)
+    along_xy = swap(XY, 8, lax.shift_right_logical(mask, 4), sources)
     got, q, rows, dq_band, back = along_xy(
-        got, tile_rel, band_rel, emb_t, rel_weight, src_rows, band_dst, bound, to_up, to_down,
-        from_low, from_high,
+        got, info, emb_t, rel_weight, src_rows, band_dst, bound, to_up, to_down, from_low, from_high
     )
     other_half = trade(got, 1)
     gw, step = call(
         relation_kernel,
-        "sssssvvvvvvvv",
-        [((Z, RELS, D), BF), ((D, A_ROWS), BF)],
-        core, tile_rel, band_rel, live_tiles, neg_tiles, got, other_half, q, rows, band_rows,
-        dq_band, rel_weight, dst_rows,
-    )
-    gw = lax.all_to_all(gw, "z", split_axis=0, concat_axis=0, tiled=True)
+        "vvvvvvvvv",
+        [((FIRST, RELS, D), BF), ((D, A_ROWS), BF)],
+        info, got, other_half, q, rows, band_rows, dq_band, rel_weight, dst_rows,
+    )
+    gw = lax.all_to_all(gw, "zh", split_axis=0, concat_axis=0, tiled=True)
     (total,) = call(
         partner_kernel,
-        "svvvvvvvv",
+        "vvvvvvvvv",
         [((D, ROWS), BF)],
-        core, got, other_half, emb_t, rel_weight, step, src_rows,
+        info, got, other_half, emb_t, rel_weight, step, src_rows,
         band_src, back,
     )
     from_cross = trade(total, 3)
@@ -336,15 +347,15 @@
         total, from_core, from_y, from_cross, emb_t, emb_state.reshape(1, ROWS),
     )
     gw = jnp.sum(gw.astype(F32), axis=0).astype(BF)
-    gw = jnp.broadcast_to(gw[None], (XY, RELS, D))
-    gw = lax.all_to_all(gw, ("x", "yh"), split_axis=0, concat_axis=0, tiled=True)
+    gw = jnp.broadcast_to(gw[None], (SECOND, RELS, D))
+    gw = lax.all_to_all(gw, (*XY, "zl"), split_axis=0, concat_axis=0, tiled=True)
     gw = jnp.sum(gw.astype(F32), axis=0)
     rel_new = rel_weight - step_rate * gw / jnp.sqrt(rel_state + jnp.mean(gw * gw, axis=1))[:, None]
     return (new_t.T, fresh.reshape(ROWS), rel_new)
 
 
 def solution(mesh):
-    fine = Mesh(mesh.devices.reshape(4, 2, Z, N_REL), ("x", "yh", "z", "rel"))
+    fine = Mesh(mesh.devices.reshape(4, 2, 8, 2, N_REL), (*DOM, "rel"))
     in_specs = (
         P(DOM, None),
         P(DOM),

time: 79.2 us -> 87.5 us (1.10)
  the two profiles are of different devices: /device:TPU:32 before, /device:TPU:1 now
where the time goes in v4:
time: 87.5 us; the launch traced here: 86.8 us
  starting transfers between devices  35.1 us (40%)
  blocking collectives  22.8 us (26%)
  waiting for transfers between devices  12.6 us (14%)
  Pallas kernels  10.6 us (12%)
  local copies, waits for them, and re-layouts  2.57 us (3%)
  between operations  2.16 us (2%)
    all_to_all x1, blocking collectives, body(): gw = lax.all_to_all(gw, 'zh', split_axis=0, concat_axis=0, tiled=True)  22.8 us
    ppermute x4, starting transfers between devices, trade(): return lax.ppermute(values, 'rel', [(i, i ^ bit) for i in range(N_REL)])  12.6 us
    pallas_call x5, Pallas kernels, call(): pl.pallas_call(kernel, in_specs=[smem() if kind == 's' else vmem() for ki...  10.6 us
    all_to_all x1, starting transfers between devices, body(): lax.all_to_all(gw, (*XY, 'zl'), split_axis=0, concat_axis=0, tiled=True)  8.58 us
    ppermute x1, starting transfers between devices, run(): moved = lax.ppermute(moved, axes, [(i, i ^ k) for i in range(size)])  8.21 us
    ppermute x1, waiting for transfers between devices, run(): moved = lax.ppermute(moved, axes, [(i, i ^ k) for i in range(size)])  6.32 us
    ppermute x4, waiting for transfers between devices, trade(): return lax.ppermute(values, 'rel', [(i, i ^ bit) for i in range(N_REL)])  6.24 us
    ppermute x1, starting transfers between devices, body(): from_low = lax.ppermute(to_up, DOM, [(i, i + 1) for i in range(count - 1)])  4.37 us
  transfers between devices with their start and end apart: 8, of which 4 were waited for; matrix products, arithmetic and copies ran while one was open for 1% of the time, Pallas kernels for 4%

profile of v4, /device:TPU:1, one launch (start us, length us, event | category | flops | bytes accessed | tf_op | source)
XLA Modules:
  0.0 86.8 jit_solution(17020389020353354744)
XLA Ops:
  1.4 0.6 copy-done.9
  2.0 0.0 copy-done.10
  2.0 0.0 copy-done
  2.1 0.0 copy-done.1
  2.1 1.8 %shard_map.157 = (bf16[416,128]{1,0:T(8,128)(2,1)}, bf16[408,384]{1,0:T(8,128)(2,1)S(1)}, bf16[408,384]{1,0:T(8,128)(2,1)S(1)}, f32[400,256]{1,0:T(8,128)S(1)}, f32[8,128]{1,0:T(8,128)S(1)}) custom-call(s32[1]{0:T(128)} %bitcast.core_ref, s32[1,4]{1,0:T(1,128)S(1)} %copy-done.3, s32[1,2]{1,0:T(1,128)S(1)} %copy-done.4, s32[1,1]{1,0:T(1,128)S(6)} %copy.74.live_ref, ...), custom_call_target="tpu_custom_call" | custom-call | tf_op jit(solution)/shard_map/pallas_call | solution.py:53
  3.8 4.4 %collective-permute-start.22 = (bf16[408,384]{1,0:T(8,128)(2,1)S(1)}, bf16[408,384]{1,0:T(8,128)(2,1)S(1)}, u32[]{:S(2)}, u32[]{:S(2)}) collective-permute-start(bf16[408,384]{1,0:T(8,128)(2,1)S(1)} %get-tuple-element.347), channel_id=1, source_target_pairs={{0,4},{4,8},{8,12},{12,16},{16,20},{20,24},{24,28},{28,32},{32,36}... | collective-permute-start | bytes 940040 | tf_op jit(solution)/shard_map/ppermute | solution.py:309
  8.2 1.3 %collective-permute-start.23 = (bf16[408,384]{1,0:T(8,128)(2,1)S(1)}, bf16[408,384]{1,0:T(8,128)(2,1)S(1)}, u32[]{:S(2)}, u32[]{:S(2)}) collective-permute-start(bf16[408,384]{1,0:T(8,128)(2,1)S(1)} %get-tuple-element.348), channel_id=1, source_target_pairs={{4,0},{8,4},{12,8},{16,12},{20,16},{24,20},{28,24},{32,28},{36,32}... | collective-permute-start | bytes 940040 | tf_op jit(solution)/shard_map/ppermute | solution.py:310
  10.2 0.0 copy-start.7
  10.2 15.2 %conditional.2 = (bf16[416,128]{1,0:T(8,128)(2,1)}) conditional(s32[]{:T(128)} %bitcast.4, bf16[416,128]{1,0:T(8,128)(2,1)} %get-tuple-element.349, bf16[416,128]{1,0:T(8,128)(2,1)} %get-tuple-element.349, bf16[416,128]{1,0:T(8,128)(2,1)} %get-tuple-element.349, bf16[416,128]{1,0:T(8,128)(2,1)} %get-tuple-element.349, ...), branch_computations={%region_0.0_spmd, %region_1.0_spmd, %region_2.0_spmd, %region_3.0_... | conditional | bytes 639024 | solution.py:280
  10.2 8.2 %collective-permute-start.2 = (bf16[416,128]{1,0:T(8,128)(2,1)}, bf16[416,128]{1,0:T(8,128)(2,1)S(1)}, u32[]{:S(2)}, u32[]{:S(2)}) collective-permute-start(bf16[416,128]{1,0:T(8,128)(2,1)} %param.3), channel_id=1, source_target_pairs={{0,12},{4,8},{8,4},{12,0},{16,28},{20,24},{24,20},{28,16},{32,44},... | collective-permute-start | bytes 319496 | tf_op jit(solution)/shard_map/cond/branch_3_fun/ppermute | solution.py:275
  18.4 6.3 %collective-permute-done.2 = bf16[416,128]{1,0:T(8,128)(2,1)S(1)} collective-permute-done((bf16[416,128]{1,0:T(8,128)(2,1)}, bf16[416,128]{1,0:T(8,128)(2,1)S(1)}, u32[]{:S(2)}, u32[]{:S(2)}) %collective-permute-start.2) | collective-permute-done | bytes 106528 | tf_op jit(solution)/shard_map/cond/branch_3_fun/ppermute | solution.py:275
  24.8 0.6 copy.20
  25.4 2.3 %conditional.3 = (bf16[416,128]{1,0:T(8,128)(2,1)}, bf16[400,768]{1,0:T(8,128)(2,1)S(1)}, f32[400,512]{1,0:T(8,128)S(1)}, f32[400,256]{1,0:T(8,128)S(1)}, f32[400,256]{1,0:T(8,128)}) conditional(s32[]{:T(128)} %bitcast.3, (f32[8,128]{1,0:T(8,128)S(1)}, f32[400,256]{1,0:T(8,128)S(1)}, f32[8,400]{1,0:T(8,128)S(1)}, ...), branch_computations={%region_16.0_spmd, %region_17.0_spmd, %region_18.0_spmd, %region_1... | conditional | bytes 639056 | solution.py:280
  25.5 2.3 %branch_0_fun.1 = (bf16[400,768]{1,0:T(8,128)(2,1)S(1)}, f32[400,512]{1,0:T(8,128)S(1)}, f32[400,256]{1,0:T(8,128)S(1)}, f32[400,256]{1,0:T(8,128)}) custom-call(f32[8,128]{1,0:T(8,128)S(1)} %get-tuple-element.210.info_ref, f32[400,256]{1,0:T(8,128)S(1)} %get-tuple-element.211.emb_ref, f32[8,400]{1,0:T(8,128)S(1)} %get-tuple-element.212.relw_ref, ...), custom_call_target="tpu_custom_call" | custom-call | tf_op jit(solution)/shard_map/cond/branch_0_fun/pallas_call | solution.py:53
  27.8 3.4 %collective-permute-start.24 = (bf16[416,128]{1,0:T(8,128)(2,1)}, bf16[416,128]{1,0:T(8,128)(2,1)S(1)}, u32[]{:S(2)}, u32[]{:S(2)}) collective-permute-start(bf16[416,128]{1,0:T(8,128)(2,1)} %get-tuple-element.350.got_ref), channel_id=1, source_target_pairs={{0,1},{1,0},{2,3},{3,2},{4,5},{5,4},{6,7},{7,6},{8,9},{9,8},{10,11... | collective-permute-start | bytes 319496 | tf_op jit(solution)/shard_map/ppermute | solution.py:284
  31.2 1.1 %collective-permute-done.24.other_ref = bf16[416,128]{1,0:T(8,128)(2,1)S(1)} collective-permute-done((bf16[416,128]{1,0:T(8,128)(2,1)}, bf16[416,128]{1,0:T(8,128)(2,1)S(1)}, u32[]{:S(2)}, u32[]{:S(2)}) %collective-permute-start.24) | collective-permute-done | bytes 106528 | tf_op jit(solution)/shard_map/ppermute | solution.py:284
  32.4 2.7 %shard_map.158 = (bf16[8,8,400]{2,1,0:T(8,128)(2,1)S(1)}, bf16[400,768]{1,0:T(8,128)(2,1)S(1)}) custom-call(f32[8,128]{1,0:T(8,128)S(1)} %get-tuple-element.346.info_ref, bf16[416,128]{1,0:T(8,128)(2,1)} %get-tuple-element.350.got_ref, bf16[416,128]{1,0:T(8,128)(2,1)S(1)} %collective-permute-done.24.other_ref, ...), custom_call_target="tpu_custom_call" | custom-call | tf_op jit(solution)/shard_map/pallas_call | solution.py:53
  35.1 0.0 copy-start.8
  35.1 22.8 %all_to_all.10 = bf16[8,8,400]{2,1,0:T(8,128)(2,1)S(1)} all-to-all(bf16[8,8,400]{2,1,0:T(8,128)(2,1)S(1)} %get-tuple-element.359), channel_id=1, replica_groups=mesh['x'=4,'yh'=2,'zh'=8,'zl'=2,'rel'=4] {'zh'}, dimensions={0} | all-to-all | bytes 102400 | tf_op jit(solution)/shard_map/all_to_all | solution.py:332
  58.0 0.7 broadcast_in_dim.2
  58.6 8.6 %all-to-all-start.1 = ((bf16[16,8,400]{2,1,0:T(8,128)(2,1)}), bf16[16,8,400]{2,1,0:T(8,128)(2,1)S(1)}, u32[]{:S(2)}, u32[]{:S(2)}) async-start(bf16[16,8,400]{2,1,0:T(8,128)(2,1)} %broadcast_in_dim.2), calls=%async_computation.1 | async-start | bytes 262144 | tf_op jit(solution)/shard_map/all_to_all | solution.py:351
  67.2 2.8 %shard_map.159.own_ref = bf16[400,256]{1,0:T(8,128)(2,1)S(1)} custom-call(f32[8,128]{1,0:T(8,128)S(1)} %get-tuple-element.346.info_ref, bf16[416,128]{1,0:T(8,128)(2,1)} %get-tuple-element.350.got_ref, bf16[416,128]{1,0:T(8,128)(2,1)S(1)} %collective-permute-done.24.other_ref, f32[400,256]{1,0:T(8,128)S(1)} %bitcast.18, f32[8,400]{1,0:T(8,128)S(1)} %copy-done.7, ...), custom_call_target="tpu_custom_call" | custom-call | tf_op jit(solution)/shard_map/pallas_call | solution.py:53
  70.0 0.0 copy-start.2
  70.0 4.3 %collective-permute-start.27 = (bf16[400,256]{1,0:T(8,128)(2,1)S(1)}, bf16[400,256]{1,0:T(8,128)(2,1)S(1)}, u32[]{:S(2)}, u32[]{:S(2)}) collective-permute-start(bf16[400,256]{1,0:T(8,128)(2,1)S(1)} %shard_map.159.own_ref), channel_id=1, source_target_pairs={{0,3},{1,2},{2,1},{3,0},{4,7},{5,6},{6,5},{7,4},{8,11},{9,10},{10,... | collective-permute-start | bytes 614408 | tf_op jit(solution)/shard_map/ppermute | solution.py:284
  74.4 3.0 %collective-permute-start.26 = (bf16[400,256]{1,0:T(8,128)(2,1)S(1)}, bf16[400,256]{1,0:T(8,128)(2,1)S(1)}, u32[]{:S(2)}, u32[]{:S(2)}) collective-permute-start(bf16[400,256]{1,0:T(8,128)(2,1)S(1)} %shard_map.159.own_ref), channel_id=1, source_target_pairs={{0,2},{1,3},{2,0},{3,1},{4,6},{5,7},{6,4},{7,5},{8,10},{9,11},{10,... | collective-permute-start | bytes 614408 | tf_op jit(solution)/shard_map/ppermute | solution.py:284
  77.4 1.9 %collective-permute-start.25 = (bf16[400,256]{1,0:T(8,128)(2,1)S(1)}, bf16[400,256]{1,0:T(8,128)(2,1)S(1)}, u32[]{:S(2)}, u32[]{:S(2)}) collective-permute-start(bf16[400,256]{1,0:T(8,128)(2,1)S(1)} %shard_map.159.own_ref), channel_id=1, source_target_pairs={{0,1},{1,0},{2,3},{3,2},{4,5},{5,4},{6,7},{7,6},{8,9},{9,8},{10,11... | collective-permute-start | bytes 614408 | tf_op jit(solution)/shard_map/ppermute | solution.py:284
  79.3 0.2 collective-permute-done.27.cross_ref
  79.5 4.9 %collective-permute-done.26.far_ref = bf16[400,256]{1,0:T(8,128)(2,1)S(1)} collective-permute-done((bf16[400,256]{1,0:T(8,128)(2,1)S(1)}, bf16[400,256]{1,0:T(8,128)(2,1)S(1)}, u32[]{:S(2)}, u32[]{:S(2)}) %collective-permute-start.26) | collective-permute-done | bytes 204832 | tf_op jit(solution)/shard_map/ppermute | solution.py:284
  84.4 1.0 %shard_map.160 = (f32[400,256]{1,0:T(8,128)}, f32[1,256]{1,0:T(1,128)}) custom-call(bf16[400,256]{1,0:T(8,128)(2,1)S(1)} %shard_map.159.own_ref, bf16[400,256]{1,0:T(8,128)(2,1)S(1)} %collective-permute-done.25.core_ref, bf16[400,256]{1,0:T(8,128)(2,1)S(1)} %collective-permute-done.26.far_ref, bf16[400,256]{1,0:T(8,128)(2,1)S(1)} %collective-permute-done.27.cross_ref, ...), custom_call_target="tpu_custom_call" | custom-call | tf_op jit(solution)/shard_map/pallas_call | solution.py:53
  85.4 0.1 multiply_reduce_fusion
  85.5 0.5 copy-done.12
  86.1 0.7 divide_subtract_fusion
  (25 shorter events, 0.1 us)
Async XLA Ops:
  0.6 0.7 copy-start.11
  1.3 0.7 copy-start.9
  1.3 0.7 copy-start.4
  1.3 0.7 copy-start.5
  1.3 0.7 copy-start.10
  1.3 0.7 copy-start
  1.4 0.7 copy-start.1
  1.4 0.7 copy-start.3
  3.8 21.6 %collective-permute-start.22 = (bf16[408,384]{1,0:T(8,128)(2,1)S(1)}, bf16[408,384]{1,0:T(8,128)(2,1)S(1)}, u32[]{:S(2)}, u32[]{:S(2)}) collective-permute-start(bf16[408,384]{1,0:T(8,128)(2,1)S(1)} %get-tuple-element.347), channel_id=1, source_target_pairs={{0,4},{4,8},{8,12},{12,16},{16,20},{20,24},{24,28},{28,32},{32,36}... | collective-permute-start | bytes 940040 | tf_op jit(solution)/shard_map/ppermute | solution.py:309
  8.2 17.2 %collective-permute-start.23 = (bf16[408,384]{1,0:T(8,128)(2,1)S(1)}, bf16[408,384]{1,0:T(8,128)(2,1)S(1)}, u32[]{:S(2)}, u32[]{:S(2)}) collective-permute-start(bf16[408,384]{1,0:T(8,128)(2,1)S(1)} %get-tuple-element.348), channel_id=1, source_target_pairs={{4,0},{8,4},{12,8},{16,12},{20,16},{24,20},{28,24},{32,28},{36,32}... | collective-permute-start | bytes 940040 | tf_op jit(solution)/shard_map/ppermute | solution.py:310
  10.2 15.3 %copy-start.6 = (f32[256,400]{0,1:T(8,128)S(1)}, f32[256,400]{0,1:T(8,128)}, u32[]{:S(2)}) copy-start(f32[256,400]{0,1:T(8,128)} %param.38) | copy-start | bytes 1228804
  10.2 15.2 %copy-start.7 = (f32[8,400]{1,0:T(8,128)S(1)}, f32[8,400]{1,0:T(8,128)}, u32[]{:S(2)}) copy-start(f32[8,400]{1,0:T(8,128)} %relw_ref.5) | copy-start | bytes 38404
  10.2 14.5 %collective-permute-start.2 = (bf16[416,128]{1,0:T(8,128)(2,1)}, bf16[416,128]{1,0:T(8,128)(2,1)S(1)}, u32[]{:S(2)}, u32[]{:S(2)}) collective-permute-start(bf16[416,128]{1,0:T(8,128)(2,1)} %param.3), channel_id=1, source_target_pairs={{0,12},{4,8},{8,4},{12,0},{16,28},{20,24},{24,20},{28,16},{32,44},... | collective-permute-start | bytes 319496 | tf_op jit(solution)/shard_map/cond/branch_3_fun/ppermute | solution.py:275
  27.8 4.6 %collective-permute-start.24 = (bf16[416,128]{1,0:T(8,128)(2,1)}, bf16[416,128]{1,0:T(8,128)(2,1)S(1)}, u32[]{:S(2)}, u32[]{:S(2)}) collective-permute-start(bf16[416,128]{1,0:T(8,128)(2,1)} %get-tuple-element.350.got_ref), channel_id=1, source_target_pairs={{0,1},{1,0},{2,3},{3,2},{4,5},{5,4},{6,7},{7,6},{8,9},{9,8},{10,11... | collective-permute-start | bytes 319496 | tf_op jit(solution)/shard_map/ppermute | solution.py:284
  35.1 32.1 %copy-start.8 = (f32[400,256]{1,0:T(8,128)S(1)}, f32[400,256]{1,0:T(8,128)}, u32[]{:S(2)}) copy-start(f32[400,256]{1,0:T(8,128)} %get-tuple-element.356.back_ref) | copy-start | bytes 1228804
  58.6 26.8 %all-to-all-start.1 = ((bf16[16,8,400]{2,1,0:T(8,128)(2,1)}), bf16[16,8,400]{2,1,0:T(8,128)(2,1)S(1)}, u32[]{:S(2)}, u32[]{:S(2)}) async-start(bf16[16,8,400]{2,1,0:T(8,128)(2,1)} %broadcast_in_dim.2), calls=%async_computation.1 | async-start | bytes 262144 | tf_op jit(solution)/shard_map/all_to_all | solution.py:351
  70.0 14.4 %copy-start.2 = (f32[256]{0:T(256)S(1)}, f32[256]{0:T(256)}, u32[]{:S(2)}) copy-start(f32[256]{0:T(256)} %param.39) | copy-start | bytes 3076
  70.0 9.5 %collective-permute-start.27 = (bf16[400,256]{1,0:T(8,128)(2,1)S(1)}, bf16[400,256]{1,0:T(8,128)(2,1)S(1)}, u32[]{:S(2)}, u32[]{:S(2)}) collective-permute-start(bf16[400,256]{1,0:T(8,128)(2,1)S(1)} %shard_map.159.own_ref), channel_id=1, source_target_pairs={{0,3},{1,2},{2,1},{3,0},{4,7},{5,6},{6,5},{7,4},{8,11},{9,10},{10,... | collective-permute-start | bytes 614408 | tf_op jit(solution)/shard_map/ppermute | solution.py:284
  74.4 10.0 %collective-permute-start.26 = (bf16[400,256]{1,0:T(8,128)(2,1)S(1)}, bf16[400,256]{1,0:T(8,128)(2,1)S(1)}, u32[]{:S(2)}, u32[]{:S(2)}) collective-permute-start(bf16[400,256]{1,0:T(8,128)(2,1)S(1)} %shard_map.159.own_ref), channel_id=1, source_target_pairs={{0,2},{1,3},{2,0},{3,1},{4,6},{5,7},{6,4},{7,5},{8,10},{9,11},{10,... | collective-permute-start | bytes 614408 | tf_op jit(solution)/shard_map/ppermute | solution.py:284
  77.4 7.0 %collective-permute-start.25 = (bf16[400,256]{1,0:T(8,128)(2,1)S(1)}, bf16[400,256]{1,0:T(8,128)(2,1)S(1)}, u32[]{:S(2)}, u32[]{:S(2)}) collective-permute-start(bf16[400,256]{1,0:T(8,128)(2,1)S(1)} %shard_map.159.own_ref), channel_id=1, source_target_pairs={{0,1},{1,0},{2,3},{3,2},{4,5},{5,4},{6,7},{7,6},{8,9},{9,8},{10,11... | collective-permute-start | bytes 614408 | tf_op jit(solution)/shard_map/ppermute | solution.py:284
  85.4 0.7 copy-start.12

commit v5 on v4

--- a/solution.py
+++ b/solution.py
@@ -30,6 +30,7 @@
 RIM_WIDTH = BND + B_ROWS
 
 LIMIT = 24 << 20
+WIDE = 56 << 20
 
 BF = jnp.bfloat16
 F32 = jnp.float32
@@ -37,8 +38,8 @@
 ZZ = ("zh", "zl")
 DOM = (*XY, *ZZ)
 Z = 16
-FIRST = 8
-SECOND = 16
+FIRST = 16
+SECOND = 8
 
 
 def vmem():
@@ -49,13 +50,13 @@
     return pl.BlockSpec(memory_space=pltpu.SMEM)
 
 
-def call(kernel, ins, outs, *args):
+def call(kernel, ins, outs, *args, limit=LIMIT):
     return pl.pallas_call(
         kernel,
         in_specs=[smem() if kind == "s" else vmem() for kind in ins],
         out_specs=[vmem() for _ in outs],
         out_shape=[jax.ShapeDtypeStruct(shape, dtype) for shape, dtype in outs],
-        compiler_params=pltpu.CompilerParams(vmem_limit_bytes=LIMIT),
+        compiler_params=pltpu.CompilerParams(vmem_limit_bytes=limit),
     )(*args)
 
 
@@ -241,7 +242,7 @@
 
 def partner_kernel(
     info_ref, got_ref, other_ref, emb_ref, relw_ref, step_ref, src_ref, bsrc_ref, back_ref,
-    total_ref,
+    keep_ref, give_ref,
 ):
     core = number(info_ref[:1, :], A_TILES + 2)
     far = same_order(core, got_ref[:D, :], other_ref[:D, :])
@@ -257,12 +258,12 @@
     pick = jnp.concatenate([ones(hits(ROWS, src_ref[...])), ones(hits(ROWS, bsrc_ref[...]))], axis=1)
     total = back_ref[...] + mm(step_ref[...], pick, NT) + mm(q, coef, NT)
     total = total + mm(q[:, :E_ROWS], rest, NT)
-    total_ref[...] = total.astype(BF)
-
-
-def final_kernel(own_ref, core_ref, far_ref, cross_ref, emb_ref, state_ref, new_ref, fresh_ref):
-    near = own_ref[...].astype(F32) + core_ref[...].astype(F32)
-    grad = near + (far_ref[...].astype(F32) + cross_ref[...].astype(F32))
+    keep_ref[...] = jnp.where(core == 0, total[:, :HALF], total[:, HALF:])
+    give_ref[...] = jnp.where(core == 0, total[:, HALF:], total[:, :HALF]).astype(BF)
+
+
+def final_kernel(info_ref, mine_ref, other_ref, emb_ref, state_ref, new_ref, fresh_ref):
+    grad = same_order(number(info_ref[:1, :], A_TILES + 2), mine_ref[...], other_ref[...])
     fresh = state_ref[...] + jnp.sum(grad * grad, axis=0, keepdims=True) / D
     fresh_ref[...] = fresh
     new_ref[...] = emb_ref[...] - step_rate * grad / jnp.sqrt(fresh)
@@ -304,22 +305,22 @@
             ((RELS, TILE), F32),
         ],
         core, tile_rel, band_rel, live_tiles, neg_tiles, emb_t, rel_weight, src_rows, dst_rows,
-        band_src, band_dst, bound,
+        band_src, band_dst, bound, limit=WIDE,
     )
     from_low = lax.ppermute(to_up, DOM, [(i, i + 1) for i in range(count - 1)])
     from_high = lax.ppermute(to_down, DOM, [(i + 1, i) for i in range(count - 1)])
-    (got,) = swap(ZZ, Z, lax.bitwise_and(mask, 15), lambda: ())(part)
+    (got,) = swap(XY, 8, lax.shift_right_logical(mask, 4), lambda: ())(part)
 
     def sources(*args):
         return call(
             source_kernel,
             "vvvvvvvvvv",
             [((D, A_ROWS), BF), ((D, E_ROWS), F32), ((D, B_ROWS), F32), ((D, ROWS), F32)],
-            *args,
+            *args, limit=WIDE,
         )
 
-    along_xy = swap(XY, 8, lax.shift_right_logical(mask, 4), sources)
-    got, q, rows, dq_band, back = along_xy(
+    along_z = swap(ZZ, Z, lax.bitwise_and(mask, 15), sources)
+    got, q, rows, dq_band, back = along_z(
         got, info, emb_t, rel_weight, src_rows, band_dst, bound, to_up, to_down, from_low, from_high
     )
     other_half = trade(got, 1)
@@ -329,26 +330,25 @@
         [((FIRST, RELS, D), BF), ((D, A_ROWS), BF)],
         info, got, other_half, q, rows, band_rows, dq_band, rel_weight, dst_rows,
     )
-    gw = lax.all_to_all(gw, "zh", split_axis=0, concat_axis=0, tiled=True)
-    (total,) = call(
+    gw = lax.all_to_all(gw, ZZ, split_axis=0, concat_axis=0, tiled=True)
+    keep, give = call(
         partner_kernel,
         "vvvvvvvvv",
-        [((D, ROWS), BF)],
-        info, got, other_half, emb_t, rel_weight, step, src_rows,
-        band_src, back,
-    )
-    from_cross = trade(total, 3)
-    from_y = trade(total, 2)
-    from_core = trade(total, 1)
+        [((D, HALF), F32), ((D, HALF), BF)],
+        info, got, other_half, emb_t, rel_weight, step, src_rows, band_src, back,
+    )
+    half = (keep + trade(give, 1).astype(F32)).astype(BF)
+    mine = half.astype(F32) + trade(half, 2).astype(F32)
+    other = trade(mine, 1)
     new_t, fresh = call(
         final_kernel,
-        "vvvvvv",
+        "vvvvv",
         [((D, ROWS), F32), ((1, ROWS), F32)],
-        total, from_core, from_y, from_cross, emb_t, emb_state.reshape(1, ROWS),
+        info, mine, other, emb_t, emb_state.reshape(1, ROWS),
     )
     gw = jnp.sum(gw.astype(F32), axis=0).astype(BF)
     gw = jnp.broadcast_to(gw[None], (SECOND, RELS, D))
-    gw = lax.all_to_all(gw, (*XY, "zl"), split_axis=0, concat_axis=0, tiled=True)
+    gw = lax.all_to_all(gw, XY, split_axis=0, concat_axis=0, tiled=True)
     gw = jnp.sum(gw.astype(F32), axis=0)
     rel_new = rel_weight - step_rate * gw / jnp.sqrt(rel_state + jnp.mean(gw * gw, axis=1))[:, None]
     return (new_t.T, fresh.reshape(ROWS), rel_new)

time: 87.5 us -> 91.2 us (1.042)
  the two profiles are of different devices: /device:TPU:1 before, /device:TPU:32 now
where the time goes in v5:
time: 91.2 us; the launch traced here: 90.6 us
  starting transfers between devices  44.5 us (49%)
  waiting for transfers between devices  28.7 us (31%)
  Pallas kernels  9.79 us (11%)
  local copies, waits for them, and re-layouts  4.55 us (5%)
  between operations  2.1 us (2%)
  other arithmetic  0.92 us (1%)
    all_to_all x1, starting transfers between devices, body(): gw = lax.all_to_all(gw, ZZ, split_axis=0, concat_axis=0, tiled=True)  14.4 us
    all_to_all x1, waiting for transfers between devices, body(): gw = lax.all_to_all(gw, ZZ, split_axis=0, concat_axis=0, tiled=True)  12.4 us
    pallas_call x5, Pallas kernels, call(): pl.pallas_call(kernel, in_specs=[smem() if kind == 's' else vmem() for ki...  9.79 us
    ppermute x4, starting transfers between devices, trade(): return lax.ppermute(values, 'rel', [(i, i ^ bit) for i in range(N_REL)])  9.58 us
    all_to_all x1, starting transfers between devices, body(): gw = lax.all_to_all(gw, XY, split_axis=0, concat_axis=0, tiled=True)  6.63 us
    all_to_all x1, waiting for transfers between devices, body(): gw = lax.all_to_all(gw, XY, split_axis=0, concat_axis=0, tiled=True)  6.07 us
    ppermute x1, starting transfers between devices, run(): moved = lax.ppermute(moved, axes, [(i, i ^ k) for i in range(size)])  5.17 us
    ppermute x1, starting transfers between devices, body(): lax.ppermute(to_down, DOM, [(i + 1, i) for i in range(count - 1)])  4.85 us
  transfers between devices with their start and end apart: 9, of which 7 were waited for; matrix products, arithmetic and copies ran while one was open for 1% of the time, Pallas kernels for 3%

profile of v5, /device:TPU:32, one launch (start us, length us, event | category | flops | bytes accessed | tf_op | source)
XLA Modules:
  0.0 90.6 jit_solution(17818814764001850992)
XLA Ops:
  1.3 0.7 copy-done.10
  2.0 0.0 copy-done.6
  2.0 2.3 %shard_map.157 = (bf16[416,128]{1,0:T(8,128)(2,1)S(1)}, bf16[408,384]{1,0:T(8,128)(2,1)S(1)}, bf16[408,384]{1,0:T(8,128)(2,1)S(1)}, f32[400,256]{1,0:T(8,128)}, f32[8,128]{1,0:T(8,128)S(1)}) custom-call(s32[1]{0:T(128)} %bitcast.core_ref, s32[1,4]{1,0:T(1,128)} %tile_ref.1, s32[1,2]{1,0:T(1,128)} %band_ref.1, s32[1,1]{1,0:T(1,128)S(6)} %copy.106.live_ref, ...), custom_call_target="tpu_custom_call" | custom-call | tf_op jit(solution)/shard_map/pallas_call | solution.py:54
  4.3 3.8 %collective-permute-start.22 = (bf16[408,384]{1,0:T(8,128)(2,1)S(1)}, bf16[408,384]{1,0:T(8,128)(2,1)S(1)}, u32[]{:S(2)}, u32[]{:S(2)}) collective-permute-start(bf16[408,384]{1,0:T(8,128)(2,1)S(1)} %get-tuple-element.629), channel_id=1, source_target_pairs={{0,4},{4,8},{8,12},{12,16},{16,20},{20,24},{24,28},{28,32},{32,36}... | collective-permute-start | bytes 940040 | tf_op jit(solution)/shard_map/ppermute | solution.py:310
  8.1 4.8 %collective-permute-start.23 = (bf16[408,384]{1,0:T(8,128)(2,1)S(1)}, bf16[408,384]{1,0:T(8,128)(2,1)S(1)}, u32[]{:S(2)}, u32[]{:S(2)}) collective-permute-start(bf16[408,384]{1,0:T(8,128)(2,1)S(1)} %get-tuple-element.630), channel_id=1, source_target_pairs={{4,0},{8,4},{12,8},{16,12},{20,16},{24,20},{28,24},{32,28},{36,32}... | collective-permute-start | bytes 940040 | tf_op jit(solution)/shard_map/ppermute | solution.py:311
  13.7 2.2 %collective-permute-done.22 = bf16[408,384]{1,0:T(8,128)(2,1)S(1)} collective-permute-done((bf16[408,384]{1,0:T(8,128)(2,1)S(1)}, bf16[408,384]{1,0:T(8,128)(2,1)S(1)}, u32[]{:S(2)}, u32[]{:S(2)}) %collective-permute-start.22) | collective-permute-done | bytes 313376 | tf_op jit(solution)/shard_map/ppermute | solution.py:310
  15.9 3.1 %collective-permute-done.23 = bf16[408,384]{1,0:T(8,128)(2,1)S(1)} collective-permute-done((bf16[408,384]{1,0:T(8,128)(2,1)S(1)}, bf16[408,384]{1,0:T(8,128)(2,1)S(1)}, u32[]{:S(2)}, u32[]{:S(2)}) %collective-permute-start.23) | collective-permute-done | bytes 313376 | tf_op jit(solution)/shard_map/ppermute | solution.py:311
  19.0 9.9 %conditional.3 = (bf16[416,128]{1,0:T(8,128)(2,1)}, bf16[400,768]{1,0:T(8,128)(2,1)S(1)}, f32[400,512]{1,0:T(8,128)S(1)}, f32[400,256]{1,0:T(8,128)S(1)}, f32[400,256]{1,0:T(8,128)S(1)}) conditional(s32[]{:T(128)} %bitcast.3, (f32[8,128]{1,0:T(8,128)S(1)}, f32[400,256]{1,0:T(8,128)S(1)}, f32[8,400]{1,0:T(8,128)S(1)}, ...), branch_computations={%region_8.0_spmd, %region_9.0_spmd, %region_10.0_spmd, %region_11.... | conditional | bytes 639056 | solution.py:281
  19.1 5.2 %collective-permute-start.9 = (bf16[416,128]{1,0:T(8,128)(2,1)}, bf16[416,128]{1,0:T(8,128)(2,1)S(1)}, u32[]{:S(2)}, u32[]{:S(2)}) collective-permute-start(bf16[416,128]{1,0:T(8,128)(2,1)} %get-tuple-element.414), channel_id=1, source_target_pairs={{0,12},{4,8},{8,4},{12,0},{16,28},{20,24},{24,20},{28,16},{32,44},... | collective-permute-start | bytes 319496 | tf_op jit(solution)/shard_map/cond/branch_3_fun/ppermute | solution.py:276
  24.3 1.6 %branch_3_fun.1 = (bf16[400,768]{1,0:T(8,128)(2,1)S(1)}, f32[400,512]{1,0:T(8,128)S(1)}, f32[400,256]{1,0:T(8,128)S(1)}, f32[400,256]{1,0:T(8,128)S(1)}) custom-call(f32[8,128]{1,0:T(8,128)S(1)} %get-tuple-element.415.info_ref, f32[400,256]{1,0:T(8,128)S(1)} %get-tuple-element.416.emb_ref, f32[8,400]{1,0:T(8,128)S(1)} %get-tuple-element.417.relw_ref, ...), custom_call_target="tpu_custom_call" | custom-call | tf_op jit(solution)/shard_map/cond/branch_3_fun/pallas_call | solution.py:54
  25.8 2.5 %collective-permute-done.9 = bf16[416,128]{1,0:T(8,128)(2,1)S(1)} collective-permute-done((bf16[416,128]{1,0:T(8,128)(2,1)}, bf16[416,128]{1,0:T(8,128)(2,1)S(1)}, u32[]{:S(2)}, u32[]{:S(2)}) %collective-permute-start.9) | collective-permute-done | bytes 106528 | tf_op jit(solution)/shard_map/cond/branch_3_fun/ppermute | solution.py:276
  28.3 0.7 copy.40
  28.9 2.1 %collective-permute-start.24 = (bf16[416,128]{1,0:T(8,128)(2,1)}, bf16[416,128]{1,0:T(8,128)(2,1)S(1)}, u32[]{:S(2)}, u32[]{:S(2)}) collective-permute-start(bf16[416,128]{1,0:T(8,128)(2,1)} %get-tuple-element.632.got_ref), channel_id=1, source_target_pairs={{0,1},{1,0},{2,3},{3,2},{4,5},{5,4},{6,7},{7,6},{8,9},{9,8},{10,11... | collective-permute-start | bytes 319496 | tf_op jit(solution)/shard_map/ppermute | solution.py:285
  31.1 1.3 %collective-permute-done.24.other_ref = bf16[416,128]{1,0:T(8,128)(2,1)S(1)} collective-permute-done((bf16[416,128]{1,0:T(8,128)(2,1)}, bf16[416,128]{1,0:T(8,128)(2,1)S(1)}, u32[]{:S(2)}, u32[]{:S(2)}) %collective-permute-start.24) | collective-permute-done | bytes 106528 | tf_op jit(solution)/shard_map/ppermute | solution.py:285
  32.4 0.7 copy-done.1
  33.0 3.0 %shard_map.158 = (bf16[16,8,400]{2,1,0:T(8,128)(2,1)}, bf16[400,768]{1,0:T(8,128)(2,1)S(1)}) custom-call(f32[8,128]{1,0:T(8,128)S(1)} %get-tuple-element.628.info_ref, bf16[416,128]{1,0:T(8,128)(2,1)} %get-tuple-element.632.got_ref, bf16[416,128]{1,0:T(8,128)(2,1)S(1)} %collective-permute-done.24.other_ref, bf16[400,768]{1,0:T(8,128)(2,1)S(1)} %get-tuple-element.633.q_ref, ...), custom_call_target="tpu_custom_call" | custom-call | tf_op jit(solution)/shard_map/pallas_call | solution.py:54
  36.1 0.7 copy-done.2
  36.7 1.9 %shard_map.159 = (f32[400,128]{1,0:T(8,128)S(1)}, bf16[400,128]{1,0:T(8,128)(2,1)S(1)}) custom-call(f32[8,128]{1,0:T(8,128)S(1)} %get-tuple-element.628.info_ref, bf16[416,128]{1,0:T(8,128)(2,1)S(1)} %copy-done.8, bf16[416,128]{1,0:T(8,128)(2,1)S(1)} %collective-permute-done.24.other_ref, f32[400,256]{1,0:T(8,128)S(1)} %bitcast.26, f32[8,400]{1,0:T(8,128)S(1)} %copy-done.5, ...), custom_call_target="tpu_custom_call" | custom-call | tf_op jit(solution)/shard_map/pallas_call | solution.py:54
  38.7 2.1 %collective-permute-start.25 = (bf16[400,128]{1,0:T(8,128)(2,1)S(1)}, bf16[400,128]{1,0:T(8,128)(2,1)S(1)}, u32[]{:S(2)}, u32[]{:S(2)}) collective-permute-start(bf16[400,128]{1,0:T(8,128)(2,1)S(1)} %get-tuple-element.640), channel_id=1, source_target_pairs={{0,1},{1,0},{2,3},{3,2},{4,5},{5,4},{6,7},{7,6},{8,9},{9,8},{10,11... | collective-permute-start | bytes 307208 | tf_op jit(solution)/shard_map/ppermute | solution.py:285
  40.7 1.1 %collective-permute-done.25 = bf16[400,128]{1,0:T(8,128)(2,1)S(1)} collective-permute-done((bf16[400,128]{1,0:T(8,128)(2,1)S(1)}, bf16[400,128]{1,0:T(8,128)(2,1)S(1)}, u32[]{:S(2)}, u32[]{:S(2)}) %collective-permute-start.25) | collective-permute-done | bytes 102432 | tf_op jit(solution)/shard_map/ppermute | solution.py:285
  41.9 3.5 %collective-permute-start.26 = (bf16[400,128]{1,0:T(8,128)(2,1)S(1)}, bf16[400,128]{1,0:T(8,128)(2,1)S(1)}, u32[]{:S(2)}, u32[]{:S(2)}) collective-permute-start(bf16[400,128]{1,0:T(8,128)(2,1)S(1)} %add_convert_fusion), channel_id=1, source_target_pairs={{0,2},{1,3},{2,0},{3,1},{4,6},{5,7},{6,4},{7,5},{8,10},{9,11},{10,... | collective-permute-start | bytes 307208 | tf_op jit(solution)/shard_map/ppermute | solution.py:285
  45.4 14.4 %all-to-all-start = ((bf16[16,8,400]{2,1,0:T(8,128)(2,1)}), bf16[16,8,400]{2,1,0:T(8,128)(2,1)S(1)}, u32[]{:S(2)}, u32[]{:S(2)}) async-start(bf16[16,8,400]{2,1,0:T(8,128)(2,1)} %get-tuple-element.643), calls=%async_computation | async-start | bytes 262144 | tf_op jit(solution)/shard_map/all_to_all | solution.py:333
  59.9 1.9 %collective-permute-start.27 = (f32[400,128]{1,0:T(8,128)S(1)}, f32[400,128]{1,0:T(8,128)S(1)}, u32[]{:S(2)}, u32[]{:S(2)}) collective-permute-start(f32[400,128]{1,0:T(8,128)S(1)} %convert_add_fusion.mine_ref), channel_id=1, source_target_pairs={{0,1},{1,0},{2,3},{3,2},{4,5},{5,4},{6,7},{7,6},{8,9},{9,8},{10,11... | collective-permute-start | bytes 614408 | tf_op jit(solution)/shard_map/ppermute | solution.py:285
  61.8 12.4 %all-to-all-done = bf16[16,8,400]{2,1,0:T(8,128)(2,1)S(1)} async-done(((bf16[16,8,400]{2,1,0:T(8,128)(2,1)}), bf16[16,8,400]{2,1,0:T(8,128)(2,1)S(1)}, u32[]{:S(2)}, u32[]{:S(2)}) %all-to-all-start) | async-done | bytes 102432 | tf_op jit(solution)/shard_map/all_to_all | solution.py:333
  74.2 0.6 broadcast_in_dim.2
  74.9 6.6 %all-to-all-start.1 = ((bf16[8,8,400]{2,1,0:T(8,128)(2,1)}), bf16[8,8,400]{2,1,0:T(8,128)(2,1)S(1)}, u32[]{:S(2)}, u32[]{:S(2)}) async-start(bf16[8,8,400]{2,1,0:T(8,128)(2,1)} %broadcast_in_dim.2), calls=%async_computation.1 | async-start | bytes 131072 | tf_op jit(solution)/shard_map/all_to_all | solution.py:351
  81.5 0.7 copy-done.3
  82.2 1.0 %shard_map.160 = (f32[400,256]{1,0:T(8,128)}, f32[1,256]{1,0:T(1,128)}) custom-call(f32[8,128]{1,0:T(8,128)S(1)} %get-tuple-element.628.info_ref, f32[400,128]{1,0:T(8,128)S(1)} %convert_add_fusion.mine_ref, f32[400,128]{1,0:T(8,128)S(1)} %collective-permute-done.27.other_ref, f32[400,256]{1,0:T(8,128)S(1)} %bitcast.27, f32[1,256]{1,0:T(1,128)S(1)} %bitcast.8), custom_call_target="tpu_custom_call" | custom-call | tf_op jit(solution)/shard_map/pallas_call | solution.py:54
  83.2 6.1 %all-to-all-done.1 = bf16[8,8,400]{2,1,0:T(8,128)(2,1)S(1)} async-done(((bf16[8,8,400]{2,1,0:T(8,128)(2,1)}), bf16[8,8,400]{2,1,0:T(8,128)(2,1)S(1)}, u32[]{:S(2)}, u32[]{:S(2)}) %all-to-all-start.1) | async-done | bytes 51232 | tf_op jit(solution)/shard_map/all_to_all | solution.py:351
  89.3 0.1 multiply_reduce_fusion
  89.4 0.5 copy-done.11
  89.9 0.7 divide_subtract_fusion
  (26 shorter events, 0.2 us)
Async XLA Ops:
  1.3 0.7 copy-start.10
  1.3 0.7 copy-start.6
  1.3 0.7 copy-start.9
  4.3 11.6 %collective-permute-start.22 = (bf16[408,384]{1,0:T(8,128)(2,1)S(1)}, bf16[408,384]{1,0:T(8,128)(2,1)S(1)}, u32[]{:S(2)}, u32[]{:S(2)}) collective-permute-start(bf16[408,384]{1,0:T(8,128)(2,1)S(1)} %get-tuple-element.629), channel_id=1, source_target_pairs={{0,4},{4,8},{8,12},{12,16},{16,20},{20,24},{24,28},{28,32},{32,36}... | collective-permute-start | bytes 940040 | tf_op jit(solution)/shard_map/ppermute | solution.py:310
  8.1 10.9 %collective-permute-start.23 = (bf16[408,384]{1,0:T(8,128)(2,1)S(1)}, bf16[408,384]{1,0:T(8,128)(2,1)S(1)}, u32[]{:S(2)}, u32[]{:S(2)}) collective-permute-start(bf16[408,384]{1,0:T(8,128)(2,1)S(1)} %get-tuple-element.630), channel_id=1, source_target_pairs={{4,0},{8,4},{12,8},{16,12},{20,16},{24,20},{28,24},{32,28},{36,32}... | collective-permute-start | bytes 940040 | tf_op jit(solution)/shard_map/ppermute | solution.py:311
  13.6 5.4 %copy-start.4 = (f32[256,400]{0,1:T(8,128)S(1)}, f32[256,400]{0,1:T(8,128)}, u32[]{:S(2)}) copy-start(f32[256,400]{0,1:T(8,128)} %param.38) | copy-start | bytes 1228804
  13.6 5.4 %copy-start.5 = (f32[8,400]{1,0:T(8,128)S(1)}, f32[8,400]{1,0:T(8,128)}, u32[]{:S(2)}) copy-start(f32[8,400]{1,0:T(8,128)} %relw_ref.5) | copy-start | bytes 38404
  13.7 5.4 %copy-start.7 = (bf16[416,128]{1,0:T(8,128)(2,1)}, bf16[416,128]{1,0:T(8,128)(2,1)S(1)}, u32[]{:S(2)}) copy-start(bf16[416,128]{1,0:T(8,128)(2,1)S(1)} %get-tuple-element.724) | copy-start | bytes 319492
  19.0 13.3 %copy-start = (f32[400,256]{1,0:T(8,128)S(1)}, f32[400,256]{1,0:T(8,128)}, u32[]{:S(2)}) copy-start(f32[400,256]{1,0:T(8,128)} %get-tuple-element.635.brows_ref) | copy-start | bytes 1228804
  19.1 9.2 %collective-permute-start.9 = (bf16[416,128]{1,0:T(8,128)(2,1)}, bf16[416,128]{1,0:T(8,128)(2,1)S(1)}, u32[]{:S(2)}, u32[]{:S(2)}) collective-permute-start(bf16[416,128]{1,0:T(8,128)(2,1)} %get-tuple-element.414), channel_id=1, source_target_pairs={{0,12},{4,8},{8,4},{12,0},{16,28},{20,24},{24,20},{28,16},{32,44},... | collective-permute-start | bytes 319496 | tf_op jit(solution)/shard_map/cond/branch_3_fun/ppermute | solution.py:276
  28.9 3.4 %collective-permute-start.24 = (bf16[416,128]{1,0:T(8,128)(2,1)}, bf16[416,128]{1,0:T(8,128)(2,1)S(1)}, u32[]{:S(2)}, u32[]{:S(2)}) collective-permute-start(bf16[416,128]{1,0:T(8,128)(2,1)} %get-tuple-element.632.got_ref), channel_id=1, source_target_pairs={{0,1},{1,0},{2,3},{3,2},{4,5},{5,4},{6,7},{7,6},{8,9},{9,8},{10,11... | collective-permute-start | bytes 319496 | tf_op jit(solution)/shard_map/ppermute | solution.py:285
  32.3 0.7 copy-start.1
  33.0 3.0 %copy-start.8 = (bf16[416,128]{1,0:T(8,128)(2,1)S(1)}, bf16[416,128]{1,0:T(8,128)(2,1)}, u32[]{:S(2)}) copy-start(bf16[416,128]{1,0:T(8,128)(2,1)} %get-tuple-element.632.got_ref) | copy-start | bytes 319492
  36.1 0.7 copy-start.2
  38.7 3.2 %collective-permute-start.25 = (bf16[400,128]{1,0:T(8,128)(2,1)S(1)}, bf16[400,128]{1,0:T(8,128)(2,1)S(1)}, u32[]{:S(2)}, u32[]{:S(2)}) collective-permute-start(bf16[400,128]{1,0:T(8,128)(2,1)S(1)} %get-tuple-element.640), channel_id=1, source_target_pairs={{0,1},{1,0},{2,3},{3,2},{4,5},{5,4},{6,7},{7,6},{8,9},{9,8},{10,11... | collective-permute-start | bytes 307208 | tf_op jit(solution)/shard_map/ppermute | solution.py:285
  41.9 17.9 %collective-permute-start.26 = (bf16[400,128]{1,0:T(8,128)(2,1)S(1)}, bf16[400,128]{1,0:T(8,128)(2,1)S(1)}, u32[]{:S(2)}, u32[]{:S(2)}) collective-permute-start(bf16[400,128]{1,0:T(8,128)(2,1)S(1)} %add_convert_fusion), channel_id=1, source_target_pairs={{0,2},{1,3},{2,0},{3,1},{4,6},{5,7},{6,4},{7,5},{8,10},{9,11},{10,... | collective-permute-start | bytes 307208 | tf_op jit(solution)/shard_map/ppermute | solution.py:285
  45.4 28.8 %all-to-all-start = ((bf16[16,8,400]{2,1,0:T(8,128)(2,1)}), bf16[16,8,400]{2,1,0:T(8,128)(2,1)S(1)}, u32[]{:S(2)}, u32[]{:S(2)}) async-start(bf16[16,8,400]{2,1,0:T(8,128)(2,1)} %get-tuple-element.643), calls=%async_computation | async-start | bytes 262144 | tf_op jit(solution)/shard_map/all_to_all | solution.py:333
  59.9 21.6 %collective-permute-start.27 = (f32[400,128]{1,0:T(8,128)S(1)}, f32[400,128]{1,0:T(8,128)S(1)}, u32[]{:S(2)}, u32[]{:S(2)}) collective-permute-start(f32[400,128]{1,0:T(8,128)S(1)} %convert_add_fusion.mine_ref), channel_id=1, source_target_pairs={{0,1},{1,0},{2,3},{3,2},{4,5},{5,4},{6,7},{7,6},{8,9},{9,8},{10,11... | collective-permute-start | bytes 614408 | tf_op jit(solution)/shard_map/ppermute | solution.py:285
  74.9 14.4 %all-to-all-start.1 = ((bf16[8,8,400]{2,1,0:T(8,128)(2,1)}), bf16[8,8,400]{2,1,0:T(8,128)(2,1)S(1)}, u32[]{:S(2)}, u32[]{:S(2)}) async-start(bf16[8,8,400]{2,1,0:T(8,128)(2,1)} %broadcast_in_dim.2), calls=%async_computation.1 | async-start | bytes 131072 | tf_op jit(solution)/shard_map/all_to_all | solution.py:351
  81.5 0.7 copy-start.3
  89.3 0.7 copy-start.11

commit v6 on v5

--- a/solution.py
+++ b/solution.py
@@ -92,7 +92,7 @@
                 [values, jnp.zeros((1, width - values.shape[1]), F32)], axis=1
             )
         block = jnp.where(row == k, values, block)
-    return block.astype(BF)
+    return block
 
 
 def relations(ids):
@@ -132,6 +132,11 @@
     return [number(info, k) for k in range(A_TILES)]
 
 
+def parts_of(info):
+    ids = jnp.concatenate([info[k : k + 1, :] for k in range(10)], axis=1).astype(jnp.int32)
+    return ids[:, :A_ROWS], ids[:, A_ROWS:], info[10:11, :]
+
+
 def same_order(core, own, other):
     first = core == 0
     return jnp.concatenate([jnp.where(first, own, other), jnp.where(first, other, own)], axis=1)
@@ -152,11 +157,12 @@
     scalars = jnp.zeros((1, TILE), F32)
     for k, value in enumerate([*numbers, live_ref[0, 0], second, core_ref[0]]):
         scalars = jnp.where(lane == k, value.astype(F32), scalars)
-    info_ref[...] = jnp.broadcast_to(scalars, (RELS, TILE))
     lists = []
     for ref in (src_ref, bsrc_ref, dst_ref):
         lists += [ref[:, k : k + TILE] for k in range(0, ref.shape[1], TILE)]
-    part_ref[D:, :] = stacked(INFO, TILE, [*lists, scalars])
+    info = stacked(INFO, TILE, [*lists, scalars])
+    info_ref[...] = info
+    part_ref[D:, :] = info.astype(BF)
     rim = mm(high, ones(hits(ROWS, bound_ref[...])), NN).astype(BF)
     up_ref[:D, :BND] = rim[:, BND:]
     down_ref[:D, :BND] = rim[:, :BND]
@@ -164,7 +170,7 @@
     rows = mm(high, pick, NN) + mm(low, pick, NN)
     brows_ref[...] = rows
     q = scaled(rows, weights(relw_ref[...], numbers[E_TILES:])).astype(BF)
-    info = stacked(RIM_INFO, RIM_WIDTH, [bdst_ref[...]])
+    info = stacked(RIM_INFO, RIM_WIDTH, [bdst_ref[...]]).astype(BF)
     for ref in (up_ref, down_ref):
         ref[:D, BND:] = q
         ref[D:, :] = info
@@ -176,15 +182,16 @@
 
 
 def source_kernel(
-    info_ref, emb_ref, relw_ref, src_ref, bdst_ref, bound_ref, own_up_ref, own_down_ref, low_ref,
+    info_ref, emb_ref, relw_ref, bdst_ref, bound_ref, own_up_ref, own_down_ref, low_ref,
     high_ref,
     q_ref, rows_ref, dqb_ref, back_ref,
 ):
     high, low = two(emb_ref[...])
-    pick = ones(hits(ROWS, src_ref[...]))
+    src, _, scalars = parts_of(info_ref[...])
+    pick = ones(hits(ROWS, src[:, :E_ROWS]))
     rows = mm(high, pick, NN) + mm(low, pick, NN)
     rows_ref[...] = rows
-    columns = weights(relw_ref[...], tile_numbers(info_ref[:1, :]))
+    columns = weights(relw_ref[...], tile_numbers(scalars))
     q_ref[:, :E_ROWS] = scaled(rows, columns).astype(BF)
     qb = own_up_ref[:D, BND:]
     q_ref[:, E_ROWS:] = qb
@@ -215,15 +222,15 @@
 
 
 def relation_kernel(
-    info_ref, got_ref, other_ref, q_ref, rows_ref, brows_ref, dqb_ref, relw_ref, dst_ref,
+    info_ref, got_ref, other_ref, q_ref, rows_ref, brows_ref, dqb_ref, relw_ref,
     gw_ref, step_ref,
 ):
-    info = info_ref[:1, :]
+    _, dst, info = parts_of(info_ref[...])
     ids = tile_numbers(info)
     far = same_order(number(info, A_TILES + 2), got_ref[:D, :], other_ref[:D, :])
     scores = mm(far, q_ref[...], TN)
     coef, rest = coefficients(
-        scores, dst_ref[...], number(info, A_TILES), info[:, A_TILES + 1 : A_TILES + 2]
+        scores, dst, number(info, A_TILES), info[:, A_TILES + 1 : A_TILES + 2]
     )
     chosen = relations(ids)
     dq = mm(far, coef, NN)
@@ -241,21 +248,20 @@
 
 
 def partner_kernel(
-    info_ref, got_ref, other_ref, emb_ref, relw_ref, step_ref, src_ref, bsrc_ref, back_ref,
+    info_ref, got_ref, other_ref, emb_ref, relw_ref, step_ref, back_ref,
     keep_ref, give_ref,
 ):
-    core = number(info_ref[:1, :], A_TILES + 2)
+    own_src, _, own_scalars = parts_of(info_ref[...])
+    core = number(own_scalars, A_TILES + 2)
     far = same_order(core, got_ref[:D, :], other_ref[:D, :])
-    info = got_ref[D:, :].astype(F32)
-    ids = jnp.concatenate([info[k : k + 1, :] for k in range(10)], axis=1).astype(jnp.int32)
-    scalars = info[10:11, :]
+    src, dst, scalars = parts_of(got_ref[D:, :].astype(F32))
     columns = weights(relw_ref[...], tile_numbers(scalars))
-    q = scaled(mm(far, ones(hits(ROWS, ids[:, :A_ROWS])), NN), columns).astype(BF)
+    q = scaled(mm(far, ones(hits(ROWS, src)), NN), columns).astype(BF)
     scores = mm(emb_ref[...].astype(BF), q, TN)
     coef, rest = coefficients(
-        scores, ids[:, A_ROWS:], number(scalars, A_TILES), scalars[:, A_TILES + 1 : A_TILES + 2]
-    )
-    pick = jnp.concatenate([ones(hits(ROWS, src_ref[...])), ones(hits(ROWS, bsrc_ref[...]))], axis=1)
+        scores, dst, number(scalars, A_TILES), scalars[:, A_TILES + 1 : A_TILES + 2]
+    )
+    pick = ones(hits(ROWS, own_src))
     total = back_ref[...] + mm(step_ref[...], pick, NT) + mm(q, coef, NT)
     total = total + mm(q[:, :E_ROWS], rest, NT)
     keep_ref[...] = jnp.where(core == 0, total[:, :HALF], total[:, HALF:])
@@ -263,7 +269,7 @@
 
 
 def final_kernel(info_ref, mine_ref, other_ref, emb_ref, state_ref, new_ref, fresh_ref):
-    grad = same_order(number(info_ref[:1, :], A_TILES + 2), mine_ref[...], other_ref[...])
+    grad = same_order(number(info_ref[10:11, :], A_TILES + 2), mine_ref[...], other_ref[...])
     fresh = state_ref[...] + jnp.sum(grad * grad, axis=0, keepdims=True) / D
     fresh_ref[...] = fresh
     new_ref[...] = emb_ref[...] - step_rate * grad / jnp.sqrt(fresh)
@@ -302,7 +308,7 @@
             ((RIM, RIM_WIDTH), BF),
             ((RIM, RIM_WIDTH), BF),
             ((D, B_ROWS), F32),
-            ((RELS, TILE), F32),
+            ((INFO, TILE), F32),
         ],
         core, tile_rel, band_rel, live_tiles, neg_tiles, emb_t, rel_weight, src_rows, dst_rows,
         band_src, band_dst, bound, limit=WIDE,
@@ -314,28 +320,28 @@
     def sources(*args):
         return call(
             source_kernel,
-            "vvvvvvvvvv",
+            "vvvvvvvvv",
             [((D, A_ROWS), BF), ((D, E_ROWS), F32), ((D, B_ROWS), F32), ((D, ROWS), F32)],
             *args, limit=WIDE,
         )
 
     along_z = swap(ZZ, Z, lax.bitwise_and(mask, 15), sources)
     got, q, rows, dq_band, back = along_z(
-        got, info, emb_t, rel_weight, src_rows, band_dst, bound, to_up, to_down, from_low, from_high
+        got, info, emb_t, rel_weight, band_dst, bound, to_up, to_down, from_low, from_high
     )
     other_half = trade(got, 1)
     gw, step = call(
         relation_kernel,
-        "vvvvvvvvv",
+        "vvvvvvvv",
         [((FIRST, RELS, D), BF), ((D, A_ROWS), BF)],
-        info, got, other_half, q, rows, band_rows, dq_band, rel_weight, dst_rows,
+        info, got, other_half, q, rows, band_rows, dq_band, rel_weight,
     )
     gw = lax.all_to_all(gw, ZZ, split_axis=0, concat_axis=0, tiled=True)
     keep, give = call(
         partner_kernel,
-        "vvvvvvvvv",
+        "vvvvvvv",
         [((D, HALF), F32), ((D, HALF), BF)],
-        info, got, other_half, emb_t, rel_weight, step, src_rows, band_src, back,
+        info, got, other_half, emb_t, rel_weight, step, back,
     )
     half = (keep + trade(give, 1).astype(F32)).astype(BF)
     mine = half.astype(F32) + trade(half, 2).astype(F32)

time: 91.2 us -> 89.8 us (0.985)
  local copies, waits for them, and re-layouts: 4.55 us -> 3.17 us
    unnamed x24 -> x18, local copies, waits for them, and re-layouts: 3.27 us -> 1.9 us
where the time goes in v6:
time: 89.8 us; the launch traced here: 89.3 us
  starting transfers between devices  44.5 us (50%)
  waiting for transfers between devices  28.7 us (32%)
  Pallas kernels  9.81 us (11%)
  local copies, waits for them, and re-layouts  3.17 us (4%)
  between operations  2.1 us (2%)
  other arithmetic  0.91 us (1%)
    all_to_all x1, starting transfers between devices, body(): gw = lax.all_to_all(gw, ZZ, split_axis=0, concat_axis=0, tiled=True)  14.4 us
    all_to_all x1, waiting for transfers between devices, body(): gw = lax.all_to_all(gw, ZZ, split_axis=0, concat_axis=0, tiled=True)  12.4 us
    pallas_call x5, Pallas kernels, call(): pl.pallas_call(kernel, in_specs=[smem() if kind == 's' else vmem() for ki...  9.81 us
    ppermute x4, starting transfers between devices, trade(): return lax.ppermute(values, 'rel', [(i, i ^ bit) for i in range(N_REL)])  9.59 us
    all_to_all x1, starting transfers between devices, body(): gw = lax.all_to_all(gw, XY, split_axis=0, concat_axis=0, tiled=True)  6.65 us
    all_to_all x1, waiting for transfers between devices, body(): gw = lax.all_to_all(gw, XY, split_axis=0, concat_axis=0, tiled=True)  6.07 us
    ppermute x1, starting transfers between devices, run(): moved = lax.ppermute(moved, axes, [(i, i ^ k) for i in range(size)])  5.17 us
    ppermute x1, starting transfers between devices, body(): lax.ppermute(to_down, DOM, [(i + 1, i) for i in range(count - 1)])  4.85 us
  transfers between devices with their start and end apart: 9, of which 7 were waited for; matrix products, arithmetic and copies ran while one was open for 1% of the time, Pallas kernels for 3%

profile of v6, /device:TPU:32, one launch (start us, length us, event | category | flops | bytes accessed | tf_op | source)
XLA Modules:
  0.0 89.3 jit_solution(7707721311200352781)
XLA Ops:
  1.3 0.7 copy-done.7
  2.0 0.0 copy-done.6
  2.0 2.3 %shard_map.157 = (bf16[416,128]{1,0:T(8,128)(2,1)S(1)}, bf16[408,384]{1,0:T(8,128)(2,1)S(1)}, bf16[408,384]{1,0:T(8,128)(2,1)S(1)}, f32[400,256]{1,0:T(8,128)}, f32[16,128]{1,0:T(8,128)S(1)}) custom-call(s32[1]{0:T(128)} %bitcast.core_ref, s32[1,4]{1,0:T(1,128)} %tile_ref.1, s32[1,2]{1,0:T(1,128)} %band_ref.1, s32[1,1]{1,0:T(1,128)S(6)} %copy.106.live_ref, ...), custom_call_target="tpu_custom_call" | custom-call | tf_op jit(solution)/shard_map/pallas_call | solution.py:54
  4.3 3.8 %collective-permute-start.22 = (bf16[408,384]{1,0:T(8,128)(2,1)S(1)}, bf16[408,384]{1,0:T(8,128)(2,1)S(1)}, u32[]{:S(2)}, u32[]{:S(2)}) collective-permute-start(bf16[408,384]{1,0:T(8,128)(2,1)S(1)} %get-tuple-element.581), channel_id=1, source_target_pairs={{0,4},{4,8},{8,12},{12,16},{16,20},{20,24},{24,28},{28,32},{32,36}... | collective-permute-start | bytes 940040 | tf_op jit(solution)/shard_map/ppermute | solution.py:316
  8.1 4.8 %collective-permute-start.23 = (bf16[408,384]{1,0:T(8,128)(2,1)S(1)}, bf16[408,384]{1,0:T(8,128)(2,1)S(1)}, u32[]{:S(2)}, u32[]{:S(2)}) collective-permute-start(bf16[408,384]{1,0:T(8,128)(2,1)S(1)} %get-tuple-element.582), channel_id=1, source_target_pairs={{4,0},{8,4},{12,8},{16,12},{20,16},{24,20},{28,24},{32,28},{36,32}... | collective-permute-start | bytes 940040 | tf_op jit(solution)/shard_map/ppermute | solution.py:317
  13.6 0.0 copy-start.2
  13.6 0.0 copy-start.3
  13.7 2.2 %collective-permute-done.22 = bf16[408,384]{1,0:T(8,128)(2,1)S(1)} collective-permute-done((bf16[408,384]{1,0:T(8,128)(2,1)S(1)}, bf16[408,384]{1,0:T(8,128)(2,1)S(1)}, u32[]{:S(2)}, u32[]{:S(2)}) %collective-permute-start.22) | collective-permute-done | bytes 313376 | tf_op jit(solution)/shard_map/ppermute | solution.py:316
  15.9 3.1 %collective-permute-done.23 = bf16[408,384]{1,0:T(8,128)(2,1)S(1)} collective-permute-done((bf16[408,384]{1,0:T(8,128)(2,1)S(1)}, bf16[408,384]{1,0:T(8,128)(2,1)S(1)}, u32[]{:S(2)}, u32[]{:S(2)}) %collective-permute-start.23) | collective-permute-done | bytes 313376 | tf_op jit(solution)/shard_map/ppermute | solution.py:317
  19.1 9.9 %conditional.3 = (bf16[416,128]{1,0:T(8,128)(2,1)}, bf16[400,768]{1,0:T(8,128)(2,1)S(1)}, f32[400,512]{1,0:T(8,128)S(1)}, f32[400,256]{1,0:T(8,128)S(1)}, f32[400,256]{1,0:T(8,128)S(1)}) conditional(s32[]{:T(128)} %bitcast.3, (f32[16,128]{1,0:T(8,128)S(1)}, f32[400,256]{1,0:T(8,128)S(1)}, f32[8,400]{1,0:T(8,128)S(1)}, ...), branch_computations={%region_8.0_spmd, %region_9.0_spmd, %region_10.0_spmd, %region_11.... | conditional | bytes 639056 | solution.py:287
  19.1 5.2 %collective-permute-start.9 = (bf16[416,128]{1,0:T(8,128)(2,1)}, bf16[416,128]{1,0:T(8,128)(2,1)S(1)}, u32[]{:S(2)}, u32[]{:S(2)}) collective-permute-start(bf16[416,128]{1,0:T(8,128)(2,1)} %get-tuple-element.379), channel_id=1, source_target_pairs={{0,12},{4,8},{8,4},{12,0},{16,28},{20,24},{24,20},{28,16},{32,44},... | collective-permute-start | bytes 319496 | tf_op jit(solution)/shard_map/cond/branch_3_fun/ppermute | solution.py:282
  24.3 1.6 %branch_3_fun.1 = (bf16[400,768]{1,0:T(8,128)(2,1)S(1)}, f32[400,512]{1,0:T(8,128)S(1)}, f32[400,256]{1,0:T(8,128)S(1)}, f32[400,256]{1,0:T(8,128)S(1)}) custom-call(f32[16,128]{1,0:T(8,128)S(1)} %get-tuple-element.380.info_ref, f32[400,256]{1,0:T(8,128)S(1)} %get-tuple-element.381.emb_ref, f32[8,400]{1,0:T(8,128)S(1)} %get-tuple-element.382.relw_ref, ...), custom_call_target="tpu_custom_call" | custom-call | tf_op jit(solution)/shard_map/cond/branch_3_fun/pallas_call | solution.py:54
  25.8 2.4 %collective-permute-done.9 = bf16[416,128]{1,0:T(8,128)(2,1)S(1)} collective-permute-done((bf16[416,128]{1,0:T(8,128)(2,1)}, bf16[416,128]{1,0:T(8,128)(2,1)S(1)}, u32[]{:S(2)}, u32[]{:S(2)}) %collective-permute-start.9) | collective-permute-done | bytes 106528 | tf_op jit(solution)/shard_map/cond/branch_3_fun/ppermute | solution.py:282
  28.3 0.6 copy.40
  28.9 2.1 %collective-permute-start.24 = (bf16[416,128]{1,0:T(8,128)(2,1)}, bf16[416,128]{1,0:T(8,128)(2,1)S(1)}, u32[]{:S(2)}, u32[]{:S(2)}) collective-permute-start(bf16[416,128]{1,0:T(8,128)(2,1)} %get-tuple-element.584.got_ref), channel_id=1, source_target_pairs={{0,1},{1,0},{2,3},{3,2},{4,5},{5,4},{6,7},{7,6},{8,9},{9,8},{10,11... | collective-permute-start | bytes 319496 | tf_op jit(solution)/shard_map/ppermute | solution.py:291
  31.1 1.3 %collective-permute-done.24.other_ref = bf16[416,128]{1,0:T(8,128)(2,1)S(1)} collective-permute-done((bf16[416,128]{1,0:T(8,128)(2,1)}, bf16[416,128]{1,0:T(8,128)(2,1)S(1)}, u32[]{:S(2)}, u32[]{:S(2)}) %collective-permute-start.24) | collective-permute-done | bytes 106528 | tf_op jit(solution)/shard_map/ppermute | solution.py:291
  32.3 3.0 %shard_map.158 = (bf16[16,8,400]{2,1,0:T(8,128)(2,1)}, bf16[400,768]{1,0:T(8,128)(2,1)S(1)}) custom-call(f32[16,128]{1,0:T(8,128)S(1)} %get-tuple-element.580.info_ref, bf16[416,128]{1,0:T(8,128)(2,1)} %get-tuple-element.584.got_ref, bf16[416,128]{1,0:T(8,128)(2,1)S(1)} %collective-permute-done.24.other_ref, bf16[400,768]{1,0:T(8,128)(2,1)S(1)} %get-tuple-element.585.q_ref, ...), custom_call_target="tpu_custom_call" | custom-call | tf_op jit(solution)/shard_map/pallas_call | solution.py:54
  35.4 1.9 %shard_map.159 = (f32[400,128]{1,0:T(8,128)S(1)}, bf16[400,128]{1,0:T(8,128)(2,1)S(1)}) custom-call(f32[16,128]{1,0:T(8,128)S(1)} %get-tuple-element.580.info_ref, bf16[416,128]{1,0:T(8,128)(2,1)S(1)} %copy-done.5, bf16[416,128]{1,0:T(8,128)(2,1)S(1)} %collective-permute-done.24.other_ref, f32[400,256]{1,0:T(8,128)S(1)} %bitcast.26, f32[8,400]{1,0:T(8,128)S(1)} %copy-done.3, ...), custom_call_target="tpu_custom_call" | custom-call | tf_op jit(solution)/shard_map/pallas_call | solution.py:54
  37.3 2.1 %collective-permute-start.25 = (bf16[400,128]{1,0:T(8,128)(2,1)S(1)}, bf16[400,128]{1,0:T(8,128)(2,1)S(1)}, u32[]{:S(2)}, u32[]{:S(2)}) collective-permute-start(bf16[400,128]{1,0:T(8,128)(2,1)S(1)} %get-tuple-element.592), channel_id=1, source_target_pairs={{0,1},{1,0},{2,3},{3,2},{4,5},{5,4},{6,7},{7,6},{8,9},{9,8},{10,11... | collective-permute-start | bytes 307208 | tf_op jit(solution)/shard_map/ppermute | solution.py:291
  39.4 1.1 %collective-permute-done.25 = bf16[400,128]{1,0:T(8,128)(2,1)S(1)} collective-permute-done((bf16[400,128]{1,0:T(8,128)(2,1)S(1)}, bf16[400,128]{1,0:T(8,128)(2,1)S(1)}, u32[]{:S(2)}, u32[]{:S(2)}) %collective-permute-start.25) | collective-permute-done | bytes 102432 | tf_op jit(solution)/shard_map/ppermute | solution.py:291
  40.5 3.5 %collective-permute-start.26 = (bf16[400,128]{1,0:T(8,128)(2,1)S(1)}, bf16[400,128]{1,0:T(8,128)(2,1)S(1)}, u32[]{:S(2)}, u32[]{:S(2)}) collective-permute-start(bf16[400,128]{1,0:T(8,128)(2,1)S(1)} %add_convert_fusion), channel_id=1, source_target_pairs={{0,2},{1,3},{2,0},{3,1},{4,6},{5,7},{6,4},{7,5},{8,10},{9,11},{10,... | collective-permute-start | bytes 307208 | tf_op jit(solution)/shard_map/ppermute | solution.py:291
  44.0 14.4 %all-to-all-start = ((bf16[16,8,400]{2,1,0:T(8,128)(2,1)}), bf16[16,8,400]{2,1,0:T(8,128)(2,1)S(1)}, u32[]{:S(2)}, u32[]{:S(2)}) async-start(bf16[16,8,400]{2,1,0:T(8,128)(2,1)} %get-tuple-element.595), calls=%async_computation | async-start | bytes 262144 | tf_op jit(solution)/shard_map/all_to_all | solution.py:339
  58.5 1.9 %collective-permute-start.27 = (f32[400,128]{1,0:T(8,128)S(1)}, f32[400,128]{1,0:T(8,128)S(1)}, u32[]{:S(2)}, u32[]{:S(2)}) collective-permute-start(f32[400,128]{1,0:T(8,128)S(1)} %convert_add_fusion.mine_ref), channel_id=1, source_target_pairs={{0,1},{1,0},{2,3},{3,2},{4,5},{5,4},{6,7},{7,6},{8,9},{9,8},{10,11... | collective-permute-start | bytes 614408 | tf_op jit(solution)/shard_map/ppermute | solution.py:291
  60.4 12.4 %all-to-all-done = bf16[16,8,400]{2,1,0:T(8,128)(2,1)S(1)} async-done(((bf16[16,8,400]{2,1,0:T(8,128)(2,1)}), bf16[16,8,400]{2,1,0:T(8,128)(2,1)S(1)}, u32[]{:S(2)}, u32[]{:S(2)}) %all-to-all-start) | async-done | bytes 102432 | tf_op jit(solution)/shard_map/all_to_all | solution.py:339
  72.8 0.6 broadcast_in_dim.2
  73.5 6.6 %all-to-all-start.1 = ((bf16[8,8,400]{2,1,0:T(8,128)(2,1)}), bf16[8,8,400]{2,1,0:T(8,128)(2,1)S(1)}, u32[]{:S(2)}, u32[]{:S(2)}) async-start(bf16[8,8,400]{2,1,0:T(8,128)(2,1)} %broadcast_in_dim.2), calls=%async_computation.1 | async-start | bytes 131072 | tf_op jit(solution)/shard_map/all_to_all | solution.py:357
  80.1 0.7 copy-done.1
  80.8 1.0 %shard_map.160 = (f32[400,256]{1,0:T(8,128)}, f32[1,256]{1,0:T(1,128)}) custom-call(f32[16,128]{1,0:T(8,128)S(1)} %get-tuple-element.580.info_ref, f32[400,128]{1,0:T(8,128)S(1)} %convert_add_fusion.mine_ref, f32[400,128]{1,0:T(8,128)S(1)} %collective-permute-done.27.other_ref, f32[400,256]{1,0:T(8,128)S(1)} %bitcast.27, f32[1,256]{1,0:T(1,128)S(1)} %bitcast.8), custom_call_target="tpu_custom_call" | custom-call | tf_op jit(solution)/shard_map/pallas_call | solution.py:54
  81.8 6.1 %all-to-all-done.1 = bf16[8,8,400]{2,1,0:T(8,128)(2,1)S(1)} async-done(((bf16[8,8,400]{2,1,0:T(8,128)(2,1)}), bf16[8,8,400]{2,1,0:T(8,128)(2,1)S(1)}, u32[]{:S(2)}, u32[]{:S(2)}) %all-to-all-start.1) | async-done | bytes 51232 | tf_op jit(solution)/shard_map/all_to_all | solution.py:357
  87.9 0.1 multiply_reduce_fusion
  88.0 0.5 copy-done.8
  88.6 0.7 divide_subtract_fusion
  (20 shorter events, 0.2 us)
Async XLA Ops:
  1.3 0.7 copy-start.7
  1.3 0.7 copy-start.6
  4.3 11.6 %collective-permute-start.22 = (bf16[408,384]{1,0:T(8,128)(2,1)S(1)}, bf16[408,384]{1,0:T(8,128)(2,1)S(1)}, u32[]{:S(2)}, u32[]{:S(2)}) collective-permute-start(bf16[408,384]{1,0:T(8,128)(2,1)S(1)} %get-tuple-element.581), channel_id=1, source_target_pairs={{0,4},{4,8},{8,12},{12,16},{16,20},{20,24},{24,28},{28,32},{32,36}... | collective-permute-start | bytes 940040 | tf_op jit(solution)/shard_map/ppermute | solution.py:316
  8.1 10.9 %collective-permute-start.23 = (bf16[408,384]{1,0:T(8,128)(2,1)S(1)}, bf16[408,384]{1,0:T(8,128)(2,1)S(1)}, u32[]{:S(2)}, u32[]{:S(2)}) collective-permute-start(bf16[408,384]{1,0:T(8,128)(2,1)S(1)} %get-tuple-element.582), channel_id=1, source_target_pairs={{4,0},{8,4},{12,8},{16,12},{20,16},{24,20},{28,24},{32,28},{36,32}... | collective-permute-start | bytes 940040 | tf_op jit(solution)/shard_map/ppermute | solution.py:317
  13.6 5.4 %copy-start.2 = (f32[256,400]{0,1:T(8,128)S(1)}, f32[256,400]{0,1:T(8,128)}, u32[]{:S(2)}) copy-start(f32[256,400]{0,1:T(8,128)} %param.38) | copy-start | bytes 1228804
  13.6 5.4 %copy-start.3 = (f32[8,400]{1,0:T(8,128)S(1)}, f32[8,400]{1,0:T(8,128)}, u32[]{:S(2)}) copy-start(f32[8,400]{1,0:T(8,128)} %relw_ref.5) | copy-start | bytes 38404
  13.7 5.4 %copy-start.4 = (bf16[416,128]{1,0:T(8,128)(2,1)}, bf16[416,128]{1,0:T(8,128)(2,1)S(1)}, u32[]{:S(2)}) copy-start(bf16[416,128]{1,0:T(8,128)(2,1)S(1)} %get-tuple-element.676) | copy-start | bytes 319492
  19.0 13.3 %copy-start = (f32[400,256]{1,0:T(8,128)S(1)}, f32[400,256]{1,0:T(8,128)}, u32[]{:S(2)}) copy-start(f32[400,256]{1,0:T(8,128)} %get-tuple-element.587.brows_ref) | copy-start | bytes 1228804
  19.1 9.2 %collective-permute-start.9 = (bf16[416,128]{1,0:T(8,128)(2,1)}, bf16[416,128]{1,0:T(8,128)(2,1)S(1)}, u32[]{:S(2)}, u32[]{:S(2)}) collective-permute-start(bf16[416,128]{1,0:T(8,128)(2,1)} %get-tuple-element.379), channel_id=1, source_target_pairs={{0,12},{4,8},{8,4},{12,0},{16,28},{20,24},{24,20},{28,16},{32,44},... | collective-permute-start | bytes 319496 | tf_op jit(solution)/shard_map/cond/branch_3_fun/ppermute | solution.py:282
  28.9 3.4 %collective-permute-start.24 = (bf16[416,128]{1,0:T(8,128)(2,1)}, bf16[416,128]{1,0:T(8,128)(2,1)S(1)}, u32[]{:S(2)}, u32[]{:S(2)}) collective-permute-start(bf16[416,128]{1,0:T(8,128)(2,1)} %get-tuple-element.584.got_ref), channel_id=1, source_target_pairs={{0,1},{1,0},{2,3},{3,2},{4,5},{5,4},{6,7},{7,6},{8,9},{9,8},{10,11... | collective-permute-start | bytes 319496 | tf_op jit(solution)/shard_map/ppermute | solution.py:291
  32.3 3.0 %copy-start.5 = (bf16[416,128]{1,0:T(8,128)(2,1)S(1)}, bf16[416,128]{1,0:T(8,128)(2,1)}, u32[]{:S(2)}) copy-start(bf16[416,128]{1,0:T(8,128)(2,1)} %get-tuple-element.584.got_ref) | copy-start | bytes 319492
  37.3 3.2 %collective-permute-start.25 = (bf16[400,128]{1,0:T(8,128)(2,1)S(1)}, bf16[400,128]{1,0:T(8,128)(2,1)S(1)}, u32[]{:S(2)}, u32[]{:S(2)}) collective-permute-start(bf16[400,128]{1,0:T(8,128)(2,1)S(1)} %get-tuple-element.592), channel_id=1, source_target_pairs={{0,1},{1,0},{2,3},{3,2},{4,5},{5,4},{6,7},{7,6},{8,9},{9,8},{10,11... | collective-permute-start | bytes 307208 | tf_op jit(solution)/shard_map/ppermute | solution.py:291
  40.5 17.9 %collective-permute-start.26 = (bf16[400,128]{1,0:T(8,128)(2,1)S(1)}, bf16[400,128]{1,0:T(8,128)(2,1)S(1)}, u32[]{:S(2)}, u32[]{:S(2)}) collective-permute-start(bf16[400,128]{1,0:T(8,128)(2,1)S(1)} %add_convert_fusion), channel_id=1, source_target_pairs={{0,2},{1,3},{2,0},{3,1},{4,6},{5,7},{6,4},{7,5},{8,10},{9,11},{10,... | collective-permute-start | bytes 307208 | tf_op jit(solution)/shard_map/ppermute | solution.py:291
  44.0 28.8 %all-to-all-start = ((bf16[16,8,400]{2,1,0:T(8,128)(2,1)}), bf16[16,8,400]{2,1,0:T(8,128)(2,1)S(1)}, u32[]{:S(2)}, u32[]{:S(2)}) async-start(bf16[16,8,400]{2,1,0:T(8,128)(2,1)} %get-tuple-element.595), calls=%async_computation | async-start | bytes 262144 | tf_op jit(solution)/shard_map/all_to_all | solution.py:339
  58.5 21.6 %collective-permute-start.27 = (f32[400,128]{1,0:T(8,128)S(1)}, f32[400,128]{1,0:T(8,128)S(1)}, u32[]{:S(2)}, u32[]{:S(2)}) collective-permute-start(f32[400,128]{1,0:T(8,128)S(1)} %convert_add_fusion.mine_ref), channel_id=1, source_target_pairs={{0,1},{1,0},{2,3},{3,2},{4,5},{5,4},{6,7},{7,6},{8,9},{9,8},{10,11... | collective-permute-start | bytes 614408 | tf_op jit(solution)/shard_map/ppermute | solution.py:291
  73.5 14.4 %all-to-all-start.1 = ((bf16[8,8,400]{2,1,0:T(8,128)(2,1)}), bf16[8,8,400]{2,1,0:T(8,128)(2,1)S(1)}, u32[]{:S(2)}, u32[]{:S(2)}) async-start(bf16[8,8,400]{2,1,0:T(8,128)(2,1)} %broadcast_in_dim.2), calls=%async_computation.1 | async-start | bytes 131072 | tf_op jit(solution)/shard_map/all_to_all | solution.py:357
  80.1 0.7 copy-start.1
  87.9 0.7 copy-start.8

commit v7 on v6

--- a/solution.py
+++ b/solution.py
@@ -275,6 +275,18 @@
     new_ref[...] = emb_ref[...] - step_rate * grad / jnp.sqrt(fresh)
 
 
+def update_kernel(state_ref, gw_ref, relw_ref, new_ref):
+    gw = gw_ref[0, :, :].astype(F32)
+    for k in range(1, SECOND):
+        gw = gw + gw_ref[k, :, :].astype(F32)
+    row = lax.broadcasted_iota(jnp.int32, (RELS, 1), 0)
+    state = jnp.zeros((RELS, 1), F32)
+    for k in range(RELS):
+        state = jnp.where(row == k, state_ref[k], state)
+    fresh = state + jnp.sum(gw * gw, axis=1, keepdims=True) / D
+    new_ref[...] = relw_ref[...] - step_rate * gw / jnp.sqrt(fresh)
+
+
 def swap(axes, size, number, work):
     def branch(k):
         def run(moved, *args):
@@ -355,8 +367,7 @@
     gw = jnp.sum(gw.astype(F32), axis=0).astype(BF)
     gw = jnp.broadcast_to(gw[None], (SECOND, RELS, D))
     gw = lax.all_to_all(gw, XY, split_axis=0, concat_axis=0, tiled=True)
-    gw = jnp.sum(gw.astype(F32), axis=0)
-    rel_new = rel_weight - step_rate * gw / jnp.sqrt(rel_state + jnp.mean(gw * gw, axis=1))[:, None]
+    (rel_new,) = call(update_kernel, "svv", [((RELS, D), F32)], rel_state, gw, rel_weight)
     return (new_t.T, fresh.reshape(ROWS), rel_new)
 
 

time: 89.8 us -> 87.8 us (0.978)
  local copies, waits for them, and re-layouts: 3.17 us -> 2.01 us
    unnamed x18 -> x14, local copies, waits for them, and re-layouts: 1.9 us -> 1.36 us
    pallas_call x5 -> x6, Pallas kernels: 9.81 us -> 10.1 us  [call(): pl.pallas_call(kernel, in_specs=[smem() if kind == 's' else vmem() for ki...]
where the time goes in v7:
time: 87.8 us; the launch traced here: 87.3 us
  starting transfers between devices  44.5 us (51%)
  waiting for transfers between devices  28.3 us (32%)
  Pallas kernels  10.1 us (12%)
  between operations  2.07 us (2%)
  local copies, waits for them, and re-layouts  2.01 us (2%)
    all_to_all x1, starting transfers between devices, body(): gw = lax.all_to_all(gw, ZZ, split_axis=0, concat_axis=0, tiled=True)  14.4 us
    all_to_all x1, waiting for transfers between devices, body(): gw = lax.all_to_all(gw, ZZ, split_axis=0, concat_axis=0, tiled=True)  12.4 us
    pallas_call x6, Pallas kernels, call(): pl.pallas_call(kernel, in_specs=[smem() if kind == 's' else vmem() for ki...  10.1 us
    ppermute x4, starting transfers between devices, trade(): return lax.ppermute(values, 'rel', [(i, i ^ bit) for i in range(N_REL)])  9.61 us
    all_to_all x1, starting transfers between devices, body(): gw = lax.all_to_all(gw, XY, split_axis=0, concat_axis=0, tiled=True)  6.63 us
    all_to_all x1, waiting for transfers between devices, body(): gw = lax.all_to_all(gw, XY, split_axis=0, concat_axis=0, tiled=True)  6.06 us
    ppermute x1, starting transfers between devices, run(): moved = lax.ppermute(moved, axes, [(i, i ^ k) for i in range(size)])  5.17 us
    ppermute x1, starting transfers between devices, body(): lax.ppermute(to_down, DOM, [(i + 1, i) for i in range(count - 1)])  4.85 us
  transfers between devices with their start and end apart: 9, of which 7 were waited for; matrix products, arithmetic and copies ran while one was open for 1% of the time, Pallas kernels for 3%

profile of v7, /device:TPU:32, one launch (start us, length us, event | category | flops | bytes accessed | tf_op | source)
XLA Modules:
  0.0 87.3 jit_solution(5055403301763731117)
XLA Ops:
  1.3 0.0 copy-start.6
  1.3 0.7 copy-done.6
  2.0 0.0 copy-done.5
  2.0 2.3 %shard_map.157 = (bf16[416,128]{1,0:T(8,128)(2,1)S(1)}, bf16[408,384]{1,0:T(8,128)(2,1)S(1)}, bf16[408,384]{1,0:T(8,128)(2,1)S(1)}, f32[400,256]{1,0:T(8,128)}, f32[16,128]{1,0:T(8,128)S(1)}) custom-call(s32[1]{0:T(128)} %bitcast.core_ref, s32[1,4]{1,0:T(1,128)} %tile_ref.1, s32[1,2]{1,0:T(1,128)} %band_ref.1, s32[1,1]{1,0:T(1,128)S(6)} %copy.106.live_ref, ...), custom_call_target="tpu_custom_call" | custom-call | tf_op jit(solution)/shard_map/pallas_call | solution.py:54
  4.3 3.8 %collective-permute-start.22 = (bf16[408,384]{1,0:T(8,128)(2,1)S(1)}, bf16[408,384]{1,0:T(8,128)(2,1)S(1)}, u32[]{:S(2)}, u32[]{:S(2)}) collective-permute-start(bf16[408,384]{1,0:T(8,128)(2,1)S(1)} %get-tuple-element.581), channel_id=1, source_target_pairs={{0,4},{4,8},{8,12},{12,16},{16,20},{20,24},{24,28},{28,32},{32,36}... | collective-permute-start | bytes 940040 | tf_op jit(solution)/shard_map/ppermute | solution.py:328
  8.1 4.8 %collective-permute-start.23 = (bf16[408,384]{1,0:T(8,128)(2,1)S(1)}, bf16[408,384]{1,0:T(8,128)(2,1)S(1)}, u32[]{:S(2)}, u32[]{:S(2)}) collective-permute-start(bf16[408,384]{1,0:T(8,128)(2,1)S(1)} %get-tuple-element.582), channel_id=1, source_target_pairs={{4,0},{8,4},{12,8},{16,12},{20,16},{24,20},{28,24},{32,28},{36,32}... | collective-permute-start | bytes 940040 | tf_op jit(solution)/shard_map/ppermute | solution.py:329
  13.6 0.0 copy-start.3
  13.6 0.0 copy-start.4
  13.7 2.2 %collective-permute-done.22 = bf16[408,384]{1,0:T(8,128)(2,1)S(1)} collective-permute-done((bf16[408,384]{1,0:T(8,128)(2,1)S(1)}, bf16[408,384]{1,0:T(8,128)(2,1)S(1)}, u32[]{:S(2)}, u32[]{:S(2)}) %collective-permute-start.22) | collective-permute-done | bytes 313376 | tf_op jit(solution)/shard_map/ppermute | solution.py:328
  15.9 3.1 %collective-permute-done.23 = bf16[408,384]{1,0:T(8,128)(2,1)S(1)} collective-permute-done((bf16[408,384]{1,0:T(8,128)(2,1)S(1)}, bf16[408,384]{1,0:T(8,128)(2,1)S(1)}, u32[]{:S(2)}, u32[]{:S(2)}) %collective-permute-start.23) | collective-permute-done | bytes 313376 | tf_op jit(solution)/shard_map/ppermute | solution.py:329
  19.0 9.2 %conditional.3 = (bf16[416,128]{1,0:T(8,128)(2,1)S(1)}, bf16[400,768]{1,0:T(8,128)(2,1)S(1)}, f32[400,512]{1,0:T(8,128)S(1)}, f32[400,256]{1,0:T(8,128)S(1)}, f32[400,256]{1,0:T(8,128)S(1)}) conditional(s32[]{:T(128)} %bitcast.3, (f32[16,128]{1,0:T(8,128)S(1)}, f32[400,256]{1,0:T(8,128)S(1)}, f32[8,400]{1,0:T(8,128)S(1)}, ...), branch_computations={%region_8.0_spmd, %region_9.0_spmd, %region_10.0_spmd, %region_11.... | conditional | bytes 639056 | solution.py:299
  19.1 5.2 %collective-permute-start.9 = (bf16[416,128]{1,0:T(8,128)(2,1)S(1)}, bf16[416,128]{1,0:T(8,128)(2,1)S(1)}, u32[]{:S(2)}, u32[]{:S(2)}) collective-permute-start(bf16[416,128]{1,0:T(8,128)(2,1)S(1)} %get-tuple-element.379), channel_id=1, source_target_pairs={{0,12},{4,8},{8,4},{12,0},{16,28},{20,24},{24,20},{28,16},{32,44},... | collective-permute-start | bytes 319496 | tf_op jit(solution)/shard_map/cond/branch_3_fun/ppermute | solution.py:294
  24.2 1.6 %branch_3_fun.1 = (bf16[400,768]{1,0:T(8,128)(2,1)S(1)}, f32[400,512]{1,0:T(8,128)S(1)}, f32[400,256]{1,0:T(8,128)S(1)}, f32[400,256]{1,0:T(8,128)S(1)}) custom-call(f32[16,128]{1,0:T(8,128)S(1)} %get-tuple-element.380.info_ref, f32[400,256]{1,0:T(8,128)S(1)} %get-tuple-element.381.emb_ref, f32[8,400]{1,0:T(8,128)S(1)} %get-tuple-element.382.relw_ref, ...), custom_call_target="tpu_custom_call" | custom-call | tf_op jit(solution)/shard_map/cond/branch_3_fun/pallas_call | solution.py:54
  25.8 2.2 %collective-permute-done.9 = bf16[416,128]{1,0:T(8,128)(2,1)S(1)} collective-permute-done((bf16[416,128]{1,0:T(8,128)(2,1)S(1)}, bf16[416,128]{1,0:T(8,128)(2,1)S(1)}, u32[]{:S(2)}, u32[]{:S(2)}) %collective-permute-start.9) | collective-permute-done | bytes 106528 | tf_op jit(solution)/shard_map/cond/branch_3_fun/ppermute | solution.py:294
  28.3 2.1 %collective-permute-start.24 = (bf16[416,128]{1,0:T(8,128)(2,1)S(1)}, bf16[416,128]{1,0:T(8,128)(2,1)S(1)}, u32[]{:S(2)}, u32[]{:S(2)}) collective-permute-start(bf16[416,128]{1,0:T(8,128)(2,1)S(1)} %get-tuple-element.584.got_ref), channel_id=1, source_target_pairs={{0,1},{1,0},{2,3},{3,2},{4,5},{5,4},{6,7},{7,6},{8,9},{9,8},{10,11... | collective-permute-start | bytes 319496 | tf_op jit(solution)/shard_map/ppermute | solution.py:303
  30.4 1.1 %collective-permute-done.24.other_ref = bf16[416,128]{1,0:T(8,128)(2,1)S(1)} collective-permute-done((bf16[416,128]{1,0:T(8,128)(2,1)S(1)}, bf16[416,128]{1,0:T(8,128)(2,1)S(1)}, u32[]{:S(2)}, u32[]{:S(2)}) %collective-permute-start.24) | collective-permute-done | bytes 106528 | tf_op jit(solution)/shard_map/ppermute | solution.py:303
  31.5 2.0 %shard_map.158 = (bf16[16,8,400]{2,1,0:T(8,128)(2,1)}, bf16[400,768]{1,0:T(8,128)(2,1)S(1)}) custom-call(f32[16,128]{1,0:T(8,128)S(1)} %get-tuple-element.580.info_ref, bf16[416,128]{1,0:T(8,128)(2,1)S(1)} %get-tuple-element.584.got_ref, bf16[416,128]{1,0:T(8,128)(2,1)S(1)} %collective-permute-done.24.other_ref, ...), custom_call_target="tpu_custom_call" | custom-call | tf_op jit(solution)/shard_map/pallas_call | solution.py:54
  33.5 1.9 %shard_map.159 = (f32[400,128]{1,0:T(8,128)S(1)}, bf16[400,128]{1,0:T(8,128)(2,1)S(1)}) custom-call(f32[16,128]{1,0:T(8,128)S(1)} %get-tuple-element.580.info_ref, bf16[416,128]{1,0:T(8,128)(2,1)S(1)} %get-tuple-element.584.got_ref, bf16[416,128]{1,0:T(8,128)(2,1)S(1)} %collective-permute-done.24.other_ref, f32[400,256]{1,0:T(8,128)S(1)} %bitcast.26, ...), custom_call_target="tpu_custom_call" | custom-call | tf_op jit(solution)/shard_map/pallas_call | solution.py:54
  35.5 2.1 %collective-permute-start.25 = (bf16[400,128]{1,0:T(8,128)(2,1)S(1)}, bf16[400,128]{1,0:T(8,128)(2,1)S(1)}, u32[]{:S(2)}, u32[]{:S(2)}) collective-permute-start(bf16[400,128]{1,0:T(8,128)(2,1)S(1)} %get-tuple-element.592), channel_id=1, source_target_pairs={{0,1},{1,0},{2,3},{3,2},{4,5},{5,4},{6,7},{7,6},{8,9},{9,8},{10,11... | collective-permute-start | bytes 307208 | tf_op jit(solution)/shard_map/ppermute | solution.py:303
  37.5 1.1 %collective-permute-done.25 = bf16[400,128]{1,0:T(8,128)(2,1)S(1)} collective-permute-done((bf16[400,128]{1,0:T(8,128)(2,1)S(1)}, bf16[400,128]{1,0:T(8,128)(2,1)S(1)}, u32[]{:S(2)}, u32[]{:S(2)}) %collective-permute-start.25) | collective-permute-done | bytes 102432 | tf_op jit(solution)/shard_map/ppermute | solution.py:303
  38.7 3.5 %collective-permute-start.26 = (bf16[400,128]{1,0:T(8,128)(2,1)S(1)}, bf16[400,128]{1,0:T(8,128)(2,1)S(1)}, u32[]{:S(2)}, u32[]{:S(2)}) collective-permute-start(bf16[400,128]{1,0:T(8,128)(2,1)S(1)} %add_convert_fusion), channel_id=1, source_target_pairs={{0,2},{1,3},{2,0},{3,1},{4,6},{5,7},{6,4},{7,5},{8,10},{9,11},{10,... | collective-permute-start | bytes 307208 | tf_op jit(solution)/shard_map/ppermute | solution.py:303
  42.2 14.4 %all-to-all-start = ((bf16[16,8,400]{2,1,0:T(8,128)(2,1)}), bf16[16,8,400]{2,1,0:T(8,128)(2,1)S(1)}, u32[]{:S(2)}, u32[]{:S(2)}) async-start(bf16[16,8,400]{2,1,0:T(8,128)(2,1)} %get-tuple-element.595), calls=%async_computation | async-start | bytes 262144 | tf_op jit(solution)/shard_map/all_to_all | solution.py:351
  56.6 0.0 collective-permute-done.26
  56.7 1.9 %collective-permute-start.27 = (f32[400,128]{1,0:T(8,128)S(1)}, f32[400,128]{1,0:T(8,128)S(1)}, u32[]{:S(2)}, u32[]{:S(2)}) collective-permute-start(f32[400,128]{1,0:T(8,128)S(1)} %convert_add_fusion.mine_ref), channel_id=1, source_target_pairs={{0,1},{1,0},{2,3},{3,2},{4,5},{5,4},{6,7},{7,6},{8,9},{9,8},{10,11... | collective-permute-start | bytes 614408 | tf_op jit(solution)/shard_map/ppermute | solution.py:303
  58.6 12.4 %all-to-all-done = bf16[16,8,400]{2,1,0:T(8,128)(2,1)S(1)} async-done(((bf16[16,8,400]{2,1,0:T(8,128)(2,1)}), bf16[16,8,400]{2,1,0:T(8,128)(2,1)S(1)}, u32[]{:S(2)}, u32[]{:S(2)}) %all-to-all-start) | async-done | bytes 102432 | tf_op jit(solution)/shard_map/all_to_all | solution.py:351
  71.0 0.6 broadcast_in_dim.2
  71.7 6.6 %all-to-all-start.1 = ((bf16[8,8,400]{2,1,0:T(8,128)(2,1)}), bf16[8,8,400]{2,1,0:T(8,128)(2,1)S(1)}, u32[]{:S(2)}, u32[]{:S(2)}) async-start(bf16[8,8,400]{2,1,0:T(8,128)(2,1)} %broadcast_in_dim.2), calls=%async_computation.1 | async-start | bytes 131072 | tf_op jit(solution)/shard_map/all_to_all | solution.py:369
  78.3 0.0 collective-permute-done.27.other_ref
  78.3 0.7 copy-done.1
  79.0 1.0 %shard_map.160 = (f32[400,256]{1,0:T(8,128)}, f32[1,256]{1,0:T(1,128)}) custom-call(f32[16,128]{1,0:T(8,128)S(1)} %get-tuple-element.580.info_ref, f32[400,128]{1,0:T(8,128)S(1)} %convert_add_fusion.mine_ref, f32[400,128]{1,0:T(8,128)S(1)} %collective-permute-done.27.other_ref, f32[400,256]{1,0:T(8,128)S(1)} %bitcast.27, f32[1,256]{1,0:T(1,128)S(1)} %bitcast.8), custom_call_target="tpu_custom_call" | custom-call | tf_op jit(solution)/shard_map/pallas_call | solution.py:54
  80.0 6.1 %all-to-all-done.1.gw_ref = bf16[8,8,400]{2,1,0:T(8,128)(2,1)S(1)} async-done(((bf16[8,8,400]{2,1,0:T(8,128)(2,1)}), bf16[8,8,400]{2,1,0:T(8,128)(2,1)S(1)}, u32[]{:S(2)}, u32[]{:S(2)}) %all-to-all-start.1) | async-done | bytes 51232 | tf_op jit(solution)/shard_map/all_to_all | solution.py:369
  86.1 1.3 %shard_map.161 = f32[8,400]{1,0:T(8,128)} custom-call(f32[8]{0:T(128)S(1)} %copy-done.2, bf16[8,8,400]{2,1,0:T(8,128)(2,1)S(1)} %all-to-all-done.1.gw_ref, f32[8,400]{1,0:T(8,128)S(1)} %copy-done.4), custom_call_target="tpu_custom_call" | custom-call | tf_op jit(solution)/shard_map/pallas_call | solution.py:54
  (13 shorter events, 0.1 us)
Async XLA Ops:
  1.3 0.7 copy-start.6
  1.3 0.7 copy-start.5
  4.3 11.6 %collective-permute-start.22 = (bf16[408,384]{1,0:T(8,128)(2,1)S(1)}, bf16[408,384]{1,0:T(8,128)(2,1)S(1)}, u32[]{:S(2)}, u32[]{:S(2)}) collective-permute-start(bf16[408,384]{1,0:T(8,128)(2,1)S(1)} %get-tuple-element.581), channel_id=1, source_target_pairs={{0,4},{4,8},{8,12},{12,16},{16,20},{20,24},{24,28},{28,32},{32,36}... | collective-permute-start | bytes 940040 | tf_op jit(solution)/shard_map/ppermute | solution.py:328
  8.1 10.9 %collective-permute-start.23 = (bf16[408,384]{1,0:T(8,128)(2,1)S(1)}, bf16[408,384]{1,0:T(8,128)(2,1)S(1)}, u32[]{:S(2)}, u32[]{:S(2)}) collective-permute-start(bf16[408,384]{1,0:T(8,128)(2,1)S(1)} %get-tuple-element.582), channel_id=1, source_target_pairs={{4,0},{8,4},{12,8},{16,12},{20,16},{24,20},{28,24},{32,28},{36,32}... | collective-permute-start | bytes 940040 | tf_op jit(solution)/shard_map/ppermute | solution.py:329
  13.6 5.4 %copy-start.3 = (f32[256,400]{0,1:T(8,128)S(1)}, f32[256,400]{0,1:T(8,128)}, u32[]{:S(2)}) copy-start(f32[256,400]{0,1:T(8,128)} %param.38) | copy-start | bytes 1228804
  13.6 5.4 %copy-start.4 = (f32[8,400]{1,0:T(8,128)S(1)}, f32[8,400]{1,0:T(8,128)}, u32[]{:S(2)}) copy-start(f32[8,400]{1,0:T(8,128)} %relw_ref.7) | copy-start | bytes 38404
  19.0 12.4 %copy-start = (f32[400,256]{1,0:T(8,128)S(1)}, f32[400,256]{1,0:T(8,128)}, u32[]{:S(2)}) copy-start(f32[400,256]{1,0:T(8,128)} %get-tuple-element.587.brows_ref) | copy-start | bytes 1228804
  19.1 9.0 %collective-permute-start.9 = (bf16[416,128]{1,0:T(8,128)(2,1)S(1)}, bf16[416,128]{1,0:T(8,128)(2,1)S(1)}, u32[]{:S(2)}, u32[]{:S(2)}) collective-permute-start(bf16[416,128]{1,0:T(8,128)(2,1)S(1)} %get-tuple-element.379), channel_id=1, source_target_pairs={{0,12},{4,8},{8,4},{12,0},{16,28},{20,24},{24,20},{28,16},{32,44},... | collective-permute-start | bytes 319496 | tf_op jit(solution)/shard_map/cond/branch_3_fun/ppermute | solution.py:294
  28.3 3.2 %collective-permute-start.24 = (bf16[416,128]{1,0:T(8,128)(2,1)S(1)}, bf16[416,128]{1,0:T(8,128)(2,1)S(1)}, u32[]{:S(2)}, u32[]{:S(2)}) collective-permute-start(bf16[416,128]{1,0:T(8,128)(2,1)S(1)} %get-tuple-element.584.got_ref), channel_id=1, source_target_pairs={{0,1},{1,0},{2,3},{3,2},{4,5},{5,4},{6,7},{7,6},{8,9},{9,8},{10,11... | collective-permute-start | bytes 319496 | tf_op jit(solution)/shard_map/ppermute | solution.py:303
  35.5 3.2 %collective-permute-start.25 = (bf16[400,128]{1,0:T(8,128)(2,1)S(1)}, bf16[400,128]{1,0:T(8,128)(2,1)S(1)}, u32[]{:S(2)}, u32[]{:S(2)}) collective-permute-start(bf16[400,128]{1,0:T(8,128)(2,1)S(1)} %get-tuple-element.592), channel_id=1, source_target_pairs={{0,1},{1,0},{2,3},{3,2},{4,5},{5,4},{6,7},{7,6},{8,9},{9,8},{10,11... | collective-permute-start | bytes 307208 | tf_op jit(solution)/shard_map/ppermute | solution.py:303
  38.7 17.9 %collective-permute-start.26 = (bf16[400,128]{1,0:T(8,128)(2,1)S(1)}, bf16[400,128]{1,0:T(8,128)(2,1)S(1)}, u32[]{:S(2)}, u32[]{:S(2)}) collective-permute-start(bf16[400,128]{1,0:T(8,128)(2,1)S(1)} %add_convert_fusion), channel_id=1, source_target_pairs={{0,2},{1,3},{2,0},{3,1},{4,6},{5,7},{6,4},{7,5},{8,10},{9,11},{10,... | collective-permute-start | bytes 307208 | tf_op jit(solution)/shard_map/ppermute | solution.py:303
  42.2 28.8 %all-to-all-start = ((bf16[16,8,400]{2,1,0:T(8,128)(2,1)}), bf16[16,8,400]{2,1,0:T(8,128)(2,1)S(1)}, u32[]{:S(2)}, u32[]{:S(2)}) async-start(bf16[16,8,400]{2,1,0:T(8,128)(2,1)} %get-tuple-element.595), calls=%async_computation | async-start | bytes 262144 | tf_op jit(solution)/shard_map/all_to_all | solution.py:351
  56.7 21.6 %collective-permute-start.27 = (f32[400,128]{1,0:T(8,128)S(1)}, f32[400,128]{1,0:T(8,128)S(1)}, u32[]{:S(2)}, u32[]{:S(2)}) collective-permute-start(f32[400,128]{1,0:T(8,128)S(1)} %convert_add_fusion.mine_ref), channel_id=1, source_target_pairs={{0,1},{1,0},{2,3},{3,2},{4,5},{5,4},{6,7},{7,6},{8,9},{9,8},{10,11... | collective-permute-start | bytes 614408 | tf_op jit(solution)/shard_map/ppermute | solution.py:303
  71.7 14.4 %all-to-all-start.1 = ((bf16[8,8,400]{2,1,0:T(8,128)(2,1)}), bf16[8,8,400]{2,1,0:T(8,128)(2,1)S(1)}, u32[]{:S(2)}, u32[]{:S(2)}) async-start(bf16[8,8,400]{2,1,0:T(8,128)(2,1)} %broadcast_in_dim.2), calls=%async_computation.1 | async-start | bytes 131072 | tf_op jit(solution)/shard_map/all_to_all | solution.py:369
  78.3 0.7 copy-start.1
  79.0 7.1 %copy-start.2 = (f32[8]{0:T(128)S(1)}, f32[8]{0:T(128)}, u32[]{:S(2)}) copy-start(f32[8]{0:T(128)} %state_ref.1) | copy-start | bytes 100
